TPU v7x, 32 devices: a whole 2x2x4 slice. The times are simulated.
32 devices in a mesh: seg: 2 (over y), tile: 4 (over z), depth: 4 (over x, core).
Axes of the slice: x: 2, y: 2, z: 4, core: 2. Of those that a mesh axis runs over, the one named last changes fastest.
Arguments:
- initial_states: float32 [2, 2, 76, 16, 512], P('seg', None, 'depth', 'tile'), may hold values from 0 to 2
- velocity: float32 [2, 2, 76, 16, 512], P('seg', None, 'depth', 'tile'), may hold values from -0.35 to 0.35
- growth: float32 [2, 16, 512], P('seg', 'tile'), may hold values from 0.1 to 1
- land_sea: int32 [16, 512], P('tile'), may hold values 0 or 1
- depth_index: int32 [16, 512], P('tile'), may hold values from 1 to 76
- column_ops: bfloat16 [2, 76, 76], replicated, may hold values from 0 to 1
Outputs:
- mismatch: float32 [2, 2, 76, 16, 512], P('seg', None, 'depth', 'tile')
All inputs are finite; a program needn't handle non-finite values. No bound on the sum of `land_sea` on one device may be relied on, other than what follows from the above.
Results may differ from a plain program's by a relative error of at most 0.00033.
Values may be sent and summed in bfloat16 or wider, within the bound.
No kernel may reach another device: no remote copies, remote signals or barrier semaphores. Data moves between devices by JAX's collectives and lax.ppermute only.
A program may use at most 64 MiB of HBM per device.

v0:
```python
import jax
import jax.numpy as jnp
from jax import lax
from jax.sharding import PartitionSpec as P

STEPS = 4


half_sat_sq = 0.25
remin_rate = 0.2


def with_halo(cells, sides, width):
    for axis, dim in sides:
        count = lax.axis_size(axis)
        ends = count - 1
        head = lax.slice_in_dim(cells, 0, width, axis=dim)
        tail = lax.slice_in_dim(cells, cells.shape[dim] - width, cells.shape[dim], axis=dim)
        cells = jnp.concatenate(
            [
                lax.ppermute(tail, axis, [(i, (i + 1) % count) for i in range(ends)]),
                cells,
                lax.ppermute(head, axis, [((i + 1) % count, i) for i in range(ends)]),
            ],
            axis=dim,
        )
    return cells


def passed_along(block, axis, distance):
    devices = range(lax.axis_size(axis))
    route = [((i - distance) % len(devices), i) for i in devices]
    return lax.ppermute(block, axis, route)


def face_flux(behind, near_side, far_side, beyond, courant):
    return (
        courant * (7.0 * (near_side + far_side) - (behind + beyond)) / 12.0
        - jnp.abs(courant) * (3.0 * (far_side - near_side) - (beyond - behind)) / 12.0
    )


def tendency(padded, north_faces, east_faces):
    merid = face_flux(
        padded[..., :-3, :],
        padded[..., 1:-2, :],
        padded[..., 2:-1, :],
        padded[..., 3:, :],
        north_faces,
    )
    centre = padded[..., 2:-2, :]
    zonal_flux = face_flux(
        jnp.roll(centre, 1, axis=-1),
        centre,
        jnp.roll(centre, -1, axis=-1),
        jnp.roll(centre, -2, axis=-1),
        east_faces,
    )
    return merid[..., :-1, :] - merid[..., 1:, :] + (jnp.roll(zonal_flux, 1, axis=-1) - zonal_flux)


def biology(mixed, rate, light_level, wet_cells):
    phosphate = mixed[..., 0, :, :, :]
    particles = mixed[..., 1, :, :, :]
    uptake = (
        rate
        * light_level
        * phosphate
        * phosphate
        * phosphate
        / (phosphate * phosphate + half_sat_sq)
    )
    return jnp.stack(
        [
            wet_cells * (phosphate - uptake + remin_rate * particles),
            wet_cells * (particles + uptake - remin_rate * particles),
        ],
        axis=-4,
    )


def shards(initial_states, velocity, growth, land_sea, depth_index, column_ops):
    seg_dev = initial_states.shape[0]
    lev_dev = initial_states.shape[2]
    first_level = lax.axis_index("depth") * lev_dev
    levels = first_level + lax.iota(jnp.int32, lev_dev)
    wet_cells = jnp.where(
        (land_sea[None] == 1) & (levels[:, None, None] < depth_index[None]), 1.0, 0.0
    ).astype(jnp.float32)
    light_level = jnp.exp(-4.0 * levels.astype(jnp.float32) / column_ops.shape[1])[:, None, None]
    own_rows = lax.dynamic_slice_in_dim(column_ops, first_level, lev_dev, 1)
    uptake_rate = growth[:, None]
    tracer_state = wet_cells * initial_states
    flow_stack = jnp.concatenate([velocity[:, 0], velocity[:, 1], wet_cells[None]], axis=0)
    flow_edges = with_halo(flow_stack, (("tile", 2),), 3)
    wet_edges = flow_edges[2 * seg_dev]
    north_wide = (flow_edges[seg_dev : 2 * seg_dev, :, :-1] * wet_edges[:, :-1] * wet_edges[:, 1:])[
        :, None
    ]
    wet_wide = wet_edges[:, 1:-1]
    east_wide = (flow_edges[:seg_dev, :, 1:-1] * wet_wide * jnp.roll(wet_wide, -1, axis=-1))[
        :, None
    ]
    north_faces = north_wide[:, :, :, 2:-2]
    east_faces = east_wide[:, :, :, 2:-2]
    for step_index in range(STEPS):
        padded = with_halo(tracer_state, (("tile", 3),), 4)
        first_section = wet_wide * (padded[:, :, :, 2:-2] + tendency(padded, north_wide, east_wide))
        advected = wet_cells * (
            0.5 * tracer_state
            + 0.5
            * (first_section[:, :, :, 2:-2] + tendency(first_section, north_faces, east_faces))
        )
        rounded = advected.astype(jnp.bfloat16)
        mixed = jnp.einsum(
            "tkm,stmrl->stkrl",
            own_rows,
            lax.all_gather(rounded, "depth", axis=2, tiled=True),
            preferred_element_type=jnp.float32,
        )
        tracer_state = biology(wet_cells * mixed, uptake_rate, light_level, wet_cells)
    previous = passed_along(tracer_state, "seg", 1)
    before = jnp.concatenate([previous, tracer_state[: seg_dev - 1]], axis=0)
    return wet_cells * (before - initial_states)


def solution(mesh):
    return jax.shard_map(
        shards,
        mesh=mesh,
        in_specs=(
            P("seg", None, "depth", "tile", None),
            P("seg", None, "depth", "tile", None),
            P("seg", "tile", None),
            P("tile", None),
            P("tile", None),
            P(),
        ),
        out_specs=P("seg", None, "depth", "tile", None),
        check_vma=False,
    )
```

profile of v0, /device:TPU:0, one launch (start us, length us, event | category | flops | bytes accessed | tf_op | source)
XLA Modules:
  0.0 140.4 jit_solution(444824181553135492)
XLA Ops:
  0.0 0.8 broadcast_compare_fusion
  0.8 0.8 broadcast_multiply_fusion
  1.6 1.1 copy_multiply_fusion
  2.7 5.0 %collective-permute-start.2 = (f32[1,2,19,4,512]{4,2,3,1,0:T(8,128)S(1)}, f32[1,2,19,4,512]{4,2,3,1,0:T(8,128)S(1)}, u32[]{:S(2)}, u32[]{:S(2)}) collective-permute-start(f32[1,2,19,4,512]{4,2,3,1,0:T(8,128)S(1)} %copy_multiply_fusion), channel_id=1, source_target_pairs={{0,4},{4,8},{8,12},{1,5},{5,9},{9,13},{2,6},{6,10},{10,14},{3,7},{... | collective-permute-start | bytes 933896 | tf_op jit(solution)/shard_map/ppermute | solution.py:21
  7.7 1.3 collective-permute-start.3
  9.5 4.6 %collective-permute-start = (f32[3,19,3,512]{3,2,1,0:T(4,128)S(1)}, f32[3,19,3,512]{3,2,1,0:T(4,128)S(1)}, u32[]{:S(2)}, u32[]{:S(2)}) collective-permute-start(f32[3,19,3,512]{3,2,1,0:T(4,128)S(1)} %get-tuple-element.44), channel_id=1, source_target_pairs={{0,4},{4,8},{8,12},{1,5},{5,9},{9,13},{2,6},{6,10},{10,14},{3,7},{... | collective-permute-start | bytes 1050632 | tf_op jit(solution)/shard_map/ppermute | solution.py:21
  14.1 1.3 collective-permute-start.1
  15.4 1.7 %collective-permute-done.2 = f32[1,2,19,4,512]{4,2,3,1,0:T(8,128)S(1)} collective-permute-done((f32[1,2,19,4,512]{4,2,3,1,0:T(8,128)S(1)}, f32[1,2,19,4,512]{4,2,3,1,0:T(8,128)S(1)}, u32[]{:S(2)}, u32[]{:S(2)}) %collective-permute-start.2) | collective-permute-done | bytes 311328 | tf_op jit(solution)/shard_map/ppermute | solution.py:21
  17.1 4.6 %collective-permute-done.3 = f32[1,2,19,4,512]{4,2,3,1,0:T(8,128)} collective-permute-done((f32[1,2,19,4,512]{4,2,3,1,0:T(8,128)S(1)}, f32[1,2,19,4,512]{4,2,3,1,0:T(8,128)}, u32[]{:S(2)}, u32[]{:S(2)}) %collective-permute-start.3) | collective-permute-done | bytes 311328 | tf_op jit(solution)/shard_map/ppermute | solution.py:23
  21.7 1.1 pad_maximum_fusion.1
  23.2 0.3 fusion.68
  23.5 2.5 %collective-permute-done = f32[3,19,3,512]{3,2,1,0:T(4,128)S(1)} collective-permute-done((f32[3,19,3,512]{3,2,1,0:T(4,128)S(1)}, f32[3,19,3,512]{3,2,1,0:T(4,128)S(1)}, u32[]{:S(2)}, u32[]{:S(2)}) %collective-permute-start) | collective-permute-done | bytes 350240 | tf_op jit(solution)/shard_map/ppermute | solution.py:21
  26.0 4.1 %collective-permute-done.1 = f32[3,19,3,512]{3,2,1,0:T(4,128)S(1)} collective-permute-done((f32[3,19,3,512]{3,2,1,0:T(4,128)S(1)}, f32[3,19,3,512]{3,2,1,0:T(4,128)S(1)}, u32[]{:S(2)}, u32[]{:S(2)}) %collective-permute-start.1) | collective-permute-done | bytes 350240 | tf_op jit(solution)/shard_map/ppermute | solution.py:23
  30.1 0.5 pad_maximum_fusion
  31.7 0.6 multiply_subtract_fusion.7
  33.0 0.4 multiply_subtract_fusion.3
  33.4 0.4 fusion.15
  34.5 0.3 multiply_subtract_fusion.15
  35.5 0.7 copy-done.1
  36.2 0.3 fusion.46
  36.7 7.7 %all_gather.12 = bf16[1,2,76,4,512]{4,3,1,0,2:T(4,128)(2,1)S(1)} all-gather(bf16[1,2,19,4,512]{4,3,1,0,2:T(4,128)(2,1)S(1)} %copy.30), channel_id=1, replica_groups=mesh['seg'=2,'tile'=4,'depth'=4] {'depth'}, dimensions={2}, use_global_device_ids=true | all-gather | bytes 778240 | tf_op jit(solution)/shard_map/all_gather | solution.py:118
  44.4 0.3 fusion
  44.9 3.5 %collective-permute-start.4 = (f32[1,2,19,4,512]{4,2,3,1,0:T(8,128)S(1)}, f32[1,2,19,4,512]{4,2,3,1,0:T(8,128)S(1)}, u32[]{:S(2)}, u32[]{:S(2)}) collective-permute-start(f32[1,2,19,4,512]{4,2,3,1,0:T(8,128)S(1)} %pad_maximum_fusion.21), channel_id=1, source_target_pairs={{0,4},{4,8},{8,12},{1,5},{5,9},{9,13},{2,6},{6,10},{10,14},{3,7},{... | collective-permute-start | bytes 933896 | tf_op jit(solution)/shard_map/ppermute | solution.py:21
  48.4 1.3 collective-permute-start.5
  49.7 7.5 %collective-permute-done.4 = f32[1,2,19,4,512]{4,2,3,1,0:T(8,128)S(1)} collective-permute-done((f32[1,2,19,4,512]{4,2,3,1,0:T(8,128)S(1)}, f32[1,2,19,4,512]{4,2,3,1,0:T(8,128)S(1)}, u32[]{:S(2)}, u32[]{:S(2)}) %collective-permute-start.4) | collective-permute-done | bytes 311328 | tf_op jit(solution)/shard_map/ppermute | solution.py:21
  57.3 4.1 %collective-permute-done.5 = f32[1,2,19,4,512]{4,2,3,1,0:T(8,128)S(1)} collective-permute-done((f32[1,2,19,4,512]{4,2,3,1,0:T(8,128)S(1)}, f32[1,2,19,4,512]{4,2,3,1,0:T(8,128)S(1)}, u32[]{:S(2)}, u32[]{:S(2)}) %collective-permute-start.5) | collective-permute-done | bytes 311328 | tf_op jit(solution)/shard_map/ppermute | solution.py:23
  61.5 0.3 fusion.66
  61.8 0.3 slice.694
  62.3 0.4 multiply_subtract_fusion.2
  62.6 0.6 multiply_subtract_fusion.6
  63.4 0.4 fusion.12
  64.5 0.3 multiply_subtract_fusion.14
  64.9 0.3 fusion.41
  65.3 7.0 %all_gather.13 = bf16[1,2,76,4,512]{4,3,1,0,2:T(4,128)(2,1)S(1)} all-gather(bf16[1,2,19,4,512]{4,3,1,0,2:T(4,128)(2,1)S(1)} %copy.33), channel_id=1, replica_groups=mesh['seg'=2,'tile'=4,'depth'=4] {'depth'}, dimensions={2}, use_global_device_ids=true | all-gather | bytes 778240 | tf_op jit(solution)/shard_map/all_gather | solution.py:118
  72.2 0.3 fusion.1
  72.8 3.5 %collective-permute-start.6 = (f32[1,2,19,4,512]{4,2,3,1,0:T(8,128)S(1)}, f32[1,2,19,4,512]{4,2,3,1,0:T(8,128)S(1)}, u32[]{:S(2)}, u32[]{:S(2)}) collective-permute-start(f32[1,2,19,4,512]{4,2,3,1,0:T(8,128)S(1)} %pad_maximum_fusion.25), channel_id=1, source_target_pairs={{0,4},{4,8},{8,12},{1,5},{5,9},{9,13},{2,6},{6,10},{10,14},{3,7},{... | collective-permute-start | bytes 933896 | tf_op jit(solution)/shard_map/ppermute | solution.py:21
  76.2 1.3 collective-permute-start.7
  77.5 7.5 %collective-permute-done.6 = f32[1,2,19,4,512]{4,2,3,1,0:T(8,128)S(1)} collective-permute-done((f32[1,2,19,4,512]{4,2,3,1,0:T(8,128)S(1)}, f32[1,2,19,4,512]{4,2,3,1,0:T(8,128)S(1)}, u32[]{:S(2)}, u32[]{:S(2)}) %collective-permute-start.6) | collective-permute-done | bytes 311328 | tf_op jit(solution)/shard_map/ppermute | solution.py:21
  85.1 4.1 %collective-permute-done.7 = f32[1,2,19,4,512]{4,2,3,1,0:T(8,128)S(1)} collective-permute-done((f32[1,2,19,4,512]{4,2,3,1,0:T(8,128)S(1)}, f32[1,2,19,4,512]{4,2,3,1,0:T(8,128)S(1)}, u32[]{:S(2)}, u32[]{:S(2)}) %collective-permute-start.7) | collective-permute-done | bytes 311328 | tf_op jit(solution)/shard_map/ppermute | solution.py:23
  89.3 0.3 fusion.64
  89.6 0.3 slice.726
  90.1 0.4 multiply_subtract_fusion.1
  90.5 0.6 multiply_subtract_fusion.5
  91.2 0.4 fusion.9
  92.3 0.3 multiply_subtract_fusion.13
  92.7 0.3 fusion.36
  93.1 7.7 %all_gather.14 = bf16[1,2,76,4,512]{4,3,1,0,2:T(4,128)(2,1)S(1)} all-gather(bf16[1,2,19,4,512]{4,3,1,0,2:T(4,128)(2,1)S(1)} %copy.35), channel_id=1, replica_groups=mesh['seg'=2,'tile'=4,'depth'=4] {'depth'}, dimensions={2}, use_global_device_ids=true | all-gather | bytes 778240 | tf_op jit(solution)/shard_map/all_gather | solution.py:118
  100.8 0.3 fusion.2
  101.3 2.2 %collective-permute-start.8 = (f32[1,2,19,4,512]{4,2,3,1,0:T(8,128)S(1)}, f32[1,2,19,4,512]{4,2,3,1,0:T(8,128)S(1)}, u32[]{:S(2)}, u32[]{:S(2)}) collective-permute-start(f32[1,2,19,4,512]{4,2,3,1,0:T(8,128)S(1)} %pad_maximum_fusion.29), channel_id=1, source_target_pairs={{0,4},{4,8},{8,12},{1,5},{5,9},{9,13},{2,6},{6,10},{10,14},{3,7},{... | collective-permute-start | bytes 933896 | tf_op jit(solution)/shard_map/ppermute | solution.py:21
  103.5 1.3 collective-permute-start.9
  104.8 7.5 %collective-permute-done.8 = f32[1,2,19,4,512]{4,2,3,1,0:T(8,128)S(1)} collective-permute-done((f32[1,2,19,4,512]{4,2,3,1,0:T(8,128)S(1)}, f32[1,2,19,4,512]{4,2,3,1,0:T(8,128)S(1)}, u32[]{:S(2)}, u32[]{:S(2)}) %collective-permute-start.8) | collective-permute-done | bytes 311328 | tf_op jit(solution)/shard_map/ppermute | solution.py:21
  112.3 4.1 %collective-permute-done.9 = f32[1,2,19,4,512]{4,2,3,1,0:T(8,128)S(1)} collective-permute-done((f32[1,2,19,4,512]{4,2,3,1,0:T(8,128)S(1)}, f32[1,2,19,4,512]{4,2,3,1,0:T(8,128)S(1)}, u32[]{:S(2)}, u32[]{:S(2)}) %collective-permute-start.9) | collective-permute-done | bytes 311328 | tf_op jit(solution)/shard_map/ppermute | solution.py:23
  116.6 0.3 fusion.62
  116.9 0.3 slice.758
  117.3 0.4 multiply_subtract_fusion
  117.7 0.6 multiply_subtract_fusion.4
  118.4 0.4 fusion.6
  119.6 0.3 multiply_subtract_fusion.12
  120.0 0.3 fusion.31
  120.3 7.0 %all_gather.15 = bf16[1,2,76,4,512]{4,3,1,0,2:T(4,128)(2,1)S(1)} all-gather(bf16[1,2,19,4,512]{4,3,1,0,2:T(4,128)(2,1)S(1)} %copy.37), channel_id=1, replica_groups=mesh['seg'=2,'tile'=4,'depth'=4] {'depth'}, dimensions={2}, use_global_device_ids=true | all-gather | bytes 778240 | tf_op jit(solution)/shard_map/all_gather | solution.py:118
  127.4 0.3 fusion.3
  127.9 1.6 %collective-permute-start.10 = (f32[1,2,19,4,512]{4,2,3,1,0:T(8,128)S(1)}, f32[1,2,19,4,512]{4,2,3,1,0:T(8,128)S(1)}, u32[]{:S(2)}, u32[]{:S(2)}) collective-permute-start(f32[1,2,19,4,512]{4,2,3,1,0:T(8,128)S(1)} %pad_maximum_fusion.33), channel_id=1, source_target_pairs={{16,0},{0,16},{17,1},{1,17},{18,2},{2,18},{19,3},{3,19},{20,4},{4,... | collective-permute-start | bytes 933896 | tf_op jit(solution)/shard_map/ppermute | solution.py:33
  129.5 9.8 %collective-permute-done.10 = f32[1,2,19,4,512]{4,2,3,1,0:T(8,128)S(1)} collective-permute-done((f32[1,2,19,4,512]{4,2,3,1,0:T(8,128)S(1)}, f32[1,2,19,4,512]{4,2,3,1,0:T(8,128)S(1)}, u32[]{:S(2)}, u32[]{:S(2)}) %collective-permute-start.10) | collective-permute-done | bytes 311328 | tf_op jit(solution)/shard_map/ppermute | solution.py:33
  139.5 0.9 copy.40
  (95 shorter events, 8.6 us)
Async XLA Ops:
  0.0 15.4 %copy-start = (bf16[2,76,76]{2,0,1:T(2,128)(2,1)S(1)}, bf16[2,76,76]{2,0,1:T(2,128)(2,1)}, u32[]{:S(2)}) copy-start(bf16[2,76,76]{2,0,1:T(2,128)(2,1)} %param.11) | copy-start | bytes 69316
  0.0 9.0 %copy-start.3 = (s32[4,512]{1,0:T(4,128)S(1)}, s32[4,512]{1,0:T(4,128)}, u32[]{:S(2)}) copy-start(s32[4,512]{1,0:T(4,128)} %param.10) | copy-start | bytes 24580
  0.0 9.1 %copy-start.2 = (f32[1,2,19,4,512]{4,3,2,1,0:T(4,128)S(1)}, f32[1,2,19,4,512]{4,3,2,1,0:T(4,128)}, u32[]{:S(2)}) copy-start(f32[1,2,19,4,512]{4,3,2,1,0:T(4,128)} %param.7) | copy-start | bytes 933892
  0.0 9.0 %copy-start.8 = (s32[19]{0:T(128)}, s32[19]{0:T(128)S(1)}, u32[]{:S(2)}) copy-start(s32[19]{0:T(128)S(1)} %iota_add_fusion) | copy-start | bytes 232
  0.8 8.2 %copy-start.6 = (pred[4,512]{1,0:T(4,128)(4,1)}, pred[4,512]{1,0:T(4,128)(4,1)S(1)}, u32[]{:S(2)}) copy-start(pred[4,512]{1,0:T(4,128)(4,1)S(1)} %broadcast_compare_fusion) | copy-start | bytes 6148
  2.7 14.4 %collective-permute-start.2 = (f32[1,2,19,4,512]{4,2,3,1,0:T(8,128)S(1)}, f32[1,2,19,4,512]{4,2,3,1,0:T(8,128)S(1)}, u32[]{:S(2)}, u32[]{:S(2)}) collective-permute-start(f32[1,2,19,4,512]{4,2,3,1,0:T(8,128)S(1)} %copy_multiply_fusion), channel_id=1, source_target_pairs={{0,4},{4,8},{8,12},{1,5},{5,9},{9,13},{2,6},{6,10},{10,14},{3,7},{... | collective-permute-start | bytes 933896 | tf_op jit(solution)/shard_map/ppermute | solution.py:21
  7.7 14.0 %collective-permute-start.3 = (f32[1,2,19,4,512]{4,2,3,1,0:T(8,128)S(1)}, f32[1,2,19,4,512]{4,2,3,1,0:T(8,128)}, u32[]{:S(2)}, u32[]{:S(2)}) collective-permute-start(f32[1,2,19,4,512]{4,2,3,1,0:T(8,128)S(1)} %copy_multiply_fusion), channel_id=1, source_target_pairs={{4,0},{8,4},{12,8},{5,1},{9,5},{13,9},{6,2},{10,6},{14,10},{7,3},{... | collective-permute-start | bytes 933896 | tf_op jit(solution)/shard_map/ppermute | solution.py:23
  9.5 16.5 %collective-permute-start = (f32[3,19,3,512]{3,2,1,0:T(4,128)S(1)}, f32[3,19,3,512]{3,2,1,0:T(4,128)S(1)}, u32[]{:S(2)}, u32[]{:S(2)}) collective-permute-start(f32[3,19,3,512]{3,2,1,0:T(4,128)S(1)} %get-tuple-element.44), channel_id=1, source_target_pairs={{0,4},{4,8},{8,12},{1,5},{5,9},{9,13},{2,6},{6,10},{10,14},{3,7},{... | collective-permute-start | bytes 1050632 | tf_op jit(solution)/shard_map/ppermute | solution.py:21
  14.1 16.1 %collective-permute-start.1 = (f32[3,19,3,512]{3,2,1,0:T(4,128)S(1)}, f32[3,19,3,512]{3,2,1,0:T(4,128)S(1)}, u32[]{:S(2)}, u32[]{:S(2)}) collective-permute-start(f32[3,19,3,512]{3,2,1,0:T(4,128)S(1)} %get-tuple-element.45), channel_id=1, source_target_pairs={{4,0},{8,4},{12,8},{5,1},{9,5},{13,9},{6,2},{10,6},{14,10},{7,3},{... | collective-permute-start | bytes 1050632 | tf_op jit(solution)/shard_map/ppermute | solution.py:23
  35.2 1.0 copy-start.1
  36.5 8.1 %copy-start.4 = (s32[4,512]{1,0:T(4,128)S(1)}, s32[4,512]{1,0:T(4,128)}, u32[]{:S(2)}) copy-start(s32[4,512]{1,0:T(4,128)} %param.10) | copy-start | bytes 24580
  36.5 8.1 %copy-start.5 = (f32[1,4,512]{2,1,0:T(4,128)S(1)}, f32[1,4,512]{2,1,0:T(4,128)}, u32[]{:S(2)}) copy-start(f32[1,4,512]{2,1,0:T(4,128)} %param.8) | copy-start | bytes 24580
  36.5 8.1 %copy-start.7 = (pred[4,512]{1,0:T(4,128)(4,1)S(1)}, pred[4,512]{1,0:T(4,128)(4,1)}, u32[]{:S(2)}) copy-start(pred[4,512]{1,0:T(4,128)(4,1)} %copy-done.6) | copy-start | bytes 6148
  36.6 8.1 %copy-start.9 = (s32[19]{0:T(128)S(1)}, s32[19]{0:T(128)}, u32[]{:S(2)}) copy-start(s32[19]{0:T(128)} %copy-done.8) | copy-start | bytes 232
  44.9 12.3 %collective-permute-start.4 = (f32[1,2,19,4,512]{4,2,3,1,0:T(8,128)S(1)}, f32[1,2,19,4,512]{4,2,3,1,0:T(8,128)S(1)}, u32[]{:S(2)}, u32[]{:S(2)}) collective-permute-start(f32[1,2,19,4,512]{4,2,3,1,0:T(8,128)S(1)} %pad_maximum_fusion.21), channel_id=1, source_target_pairs={{0,4},{4,8},{8,12},{1,5},{5,9},{9,13},{2,6},{6,10},{10,14},{3,7},{... | collective-permute-start | bytes 933896 | tf_op jit(solution)/shard_map/ppermute | solution.py:21
  48.4 13.0 %collective-permute-start.5 = (f32[1,2,19,4,512]{4,2,3,1,0:T(8,128)S(1)}, f32[1,2,19,4,512]{4,2,3,1,0:T(8,128)S(1)}, u32[]{:S(2)}, u32[]{:S(2)}) collective-permute-start(f32[1,2,19,4,512]{4,2,3,1,0:T(8,128)S(1)} %pad_maximum_fusion.21), channel_id=1, source_target_pairs={{4,0},{8,4},{12,8},{5,1},{9,5},{13,9},{6,2},{10,6},{14,10},{7,3},{... | collective-permute-start | bytes 933896 | tf_op jit(solution)/shard_map/ppermute | solution.py:23
  72.8 12.3 %collective-permute-start.6 = (f32[1,2,19,4,512]{4,2,3,1,0:T(8,128)S(1)}, f32[1,2,19,4,512]{4,2,3,1,0:T(8,128)S(1)}, u32[]{:S(2)}, u32[]{:S(2)}) collective-permute-start(f32[1,2,19,4,512]{4,2,3,1,0:T(8,128)S(1)} %pad_maximum_fusion.25), channel_id=1, source_target_pairs={{0,4},{4,8},{8,12},{1,5},{5,9},{9,13},{2,6},{6,10},{10,14},{3,7},{... | collective-permute-start | bytes 933896 | tf_op jit(solution)/shard_map/ppermute | solution.py:21
  76.2 13.0 %collective-permute-start.7 = (f32[1,2,19,4,512]{4,2,3,1,0:T(8,128)S(1)}, f32[1,2,19,4,512]{4,2,3,1,0:T(8,128)S(1)}, u32[]{:S(2)}, u32[]{:S(2)}) collective-permute-start(f32[1,2,19,4,512]{4,2,3,1,0:T(8,128)S(1)} %pad_maximum_fusion.25), channel_id=1, source_target_pairs={{4,0},{8,4},{12,8},{5,1},{9,5},{13,9},{6,2},{10,6},{14,10},{7,3},{... | collective-permute-start | bytes 933896 | tf_op jit(solution)/shard_map/ppermute | solution.py:23
  101.3 11.1 %collective-permute-start.8 = (f32[1,2,19,4,512]{4,2,3,1,0:T(8,128)S(1)}, f32[1,2,19,4,512]{4,2,3,1,0:T(8,128)S(1)}, u32[]{:S(2)}, u32[]{:S(2)}) collective-permute-start(f32[1,2,19,4,512]{4,2,3,1,0:T(8,128)S(1)} %pad_maximum_fusion.29), channel_id=1, source_target_pairs={{0,4},{4,8},{8,12},{1,5},{5,9},{9,13},{2,6},{6,10},{10,14},{3,7},{... | collective-permute-start | bytes 933896 | tf_op jit(solution)/shard_map/ppermute | solution.py:21
  103.5 13.0 %collective-permute-start.9 = (f32[1,2,19,4,512]{4,2,3,1,0:T(8,128)S(1)}, f32[1,2,19,4,512]{4,2,3,1,0:T(8,128)S(1)}, u32[]{:S(2)}, u32[]{:S(2)}) collective-permute-start(f32[1,2,19,4,512]{4,2,3,1,0:T(8,128)S(1)} %pad_maximum_fusion.29), channel_id=1, source_target_pairs={{4,0},{8,4},{12,8},{5,1},{9,5},{13,9},{6,2},{10,6},{14,10},{7,3},{... | collective-permute-start | bytes 933896 | tf_op jit(solution)/shard_map/ppermute | solution.py:23
  127.9 11.4 %collective-permute-start.10 = (f32[1,2,19,4,512]{4,2,3,1,0:T(8,128)S(1)}, f32[1,2,19,4,512]{4,2,3,1,0:T(8,128)S(1)}, u32[]{:S(2)}, u32[]{:S(2)}) collective-permute-start(f32[1,2,19,4,512]{4,2,3,1,0:T(8,128)S(1)} %pad_maximum_fusion.33), channel_id=1, source_target_pairs={{16,0},{0,16},{17,1},{1,17},{18,2},{2,18},{19,3},{3,19},{20,4},{4,... | collective-permute-start | bytes 933896 | tf_op jit(solution)/shard_map/ppermute | solution.py:33
where the time goes:
time: 141 us; the launch traced here: 140 us
  waiting for transfers between devices  57.8 us (41%)
  blocking collectives  29.4 us (21%)
  starting transfers between devices  26.8 us (19%)
  other arithmetic  15.3 us (11%)
  local copies, waits for them, and re-layouts  9.22 us (7%)
    all_gather x4, blocking collectives, shards(): lax.all_gather(rounded, 'depth', axis=2, tiled=True)  29.4 us
    ppermute x5, waiting for transfers between devices, with_halo(): lax.ppermute(tail, axis, [(i, (i + 1) % count) for i in range(ends)])  26.8 us
    ppermute x5, waiting for transfers between devices, with_halo(): lax.ppermute(head, axis, [((i + 1) % count, i) for i in range(ends)])  21.1 us
    ppermute x5, starting transfers between devices, with_halo(): lax.ppermute(tail, axis, [(i, (i + 1) % count) for i in range(ends)])  18.7 us
    ppermute x1, waiting for transfers between devices, passed_along(): return lax.ppermute(block, axis, route)  9.85 us
    ppermute x5, starting transfers between devices, with_halo(): lax.ppermute(head, axis, [((i + 1) % count, i) for i in range(ends)])  6.46 us
    sub x16, other arithmetic, face_flux(): courant * (7.0 * (near_side + far_side) - (behind + beyond)) / 12.0  6.01 us
  transfers between devices with their start and end apart: 11, of which 11 were waited for; matrix products, arithmetic and copies ran while one was open for 2% of the time, Pallas kernels for 0%

commit v1 on v0

--- a/solution.py
+++ b/solution.py
@@ -1,6 +1,8 @@
 import jax
 import jax.numpy as jnp
 from jax import lax
+from jax.experimental import pallas as pl
+from jax.experimental.pallas import tpu as pltpu
 from jax.sharding import PartitionSpec as P
 
 STEPS = 4
@@ -79,7 +81,7 @@
     )
 
 
-def shards(initial_states, velocity, growth, land_sea, depth_index, column_ops):
+def stepwise_shards(initial_states, velocity, growth, land_sea, depth_index, column_ops):
     seg_dev = initial_states.shape[0]
     lev_dev = initial_states.shape[2]
     first_level = lax.axis_index("depth") * lev_dev
@@ -124,6 +126,384 @@
     return wet_cells * (before - initial_states)
 
 
+TILES = 4
+BLOCKS = 4
+LEVELS = 76
+OWN_LEVELS = LEVELS // BLOCKS
+PITCH = 80
+OWN = 32
+REACH = 4 * STEPS
+WINDOW = OWN + 2 * REACH
+CODE = 32000.0
+FASTEST = 0.35
+FIELDS = 4 * OWN_LEVELS + 4
+ENDS = 2 * OWN_LEVELS + 2
+
+F32 = jnp.float32
+I16 = jnp.int16
+VMEM = pl.BlockSpec(memory_space=pltpu.VMEM)
+
+
+def coded(values):
+    return jnp.floor(values + 0.5).astype(jnp.int32).astype(I16)
+
+
+def exponent(largest):
+    return jnp.clip(jnp.ceil(jnp.log2(jnp.maximum(largest, 1e-36))), -119.0, 125.0)
+
+
+def index(shape, dim):
+    return lax.broadcasted_iota(jnp.int32, shape, dim)
+
+
+def pack_kernel(state, velocity, growth, land_sea, depth_index, out):
+    scales = []
+    for t in range(2):
+        largest = jnp.abs(state[0, t, 0])
+        for k in range(1, OWN_LEVELS):
+            largest = jnp.maximum(largest, jnp.abs(state[0, t, k]))
+        scales.append(exponent(largest))
+    per_unit = [CODE * jnp.exp2(-e) for e in scales]
+    wet_levels = jnp.where(land_sea[...] == 1, depth_index[...], 0).astype(F32)
+
+    def field(n):
+        which, k = divmod(n, OWN_LEVELS)
+        if which < 2:
+            return state[0, which, k] * per_unit[which]
+        if which < 4:
+            return velocity[0, which - 2, k] * (CODE / FASTEST)
+        return [growth[0] * CODE, wet_levels, scales[0], scales[1]][k]
+
+    left = index((8, 128), 1) < 64
+    for pair in range(FIELDS // 8):
+        rows = []
+        for group in (2 * pair, 2 * pair + 1):
+            lo, hi = (
+                jnp.concatenate([field(4 * group + 2 * g), field(4 * group + 2 * g + 1)], axis=0)
+                for g in range(2)
+            )
+            quarter = []
+            for m in range(4):
+                a = pltpu.roll(lo, (REACH - OWN * m) % 512, 1)
+                b = pltpu.roll(hi, (REACH - OWN * m + 64) % 512, 1)
+                quarter.append(
+                    [
+                        jnp.where(left, a[:, 128 * q : 128 * q + 128], b[:, 128 * q : 128 * q + 128])
+                        for q in range(4)
+                    ]
+                )
+            rows.append(quarter)
+        for q in range(4):
+            for m in range(4):
+                block = jnp.concatenate([rows[0][m][q], rows[1][m][q]], axis=0)
+                out[4 * q + m, 16 * pair : 16 * pair + 16, :] = coded(block)
+
+
+def steps_kernel(recv, ops, out0, out1, out2, out3, cells, moved, flow, coef, plane, light, ends):
+    sub = index((8, 128), 0)
+    lane = index((8, 128), 1)
+    left = lane < 64
+    row = sub + 8 * (lane // 64)
+
+    def spread(d, pair):
+        sent = [
+            recv[4 * t + d, 16 * pair : 16 * pair + 16, :].astype(jnp.int32).astype(F32)
+            for t in range(4)
+        ]
+        fields = []
+        for part in range(2):
+            m = [x[8 * part : 8 * part + 8] for x in sent]
+            up, across = {}, {}
+            for h in range(2):
+                a, b = m[2 * h], m[2 * h + 1]
+                up[0, h] = jnp.where(sub < 4, a, pltpu.roll(b, 4, 0))
+                up[1, h] = jnp.where(sub < 4, pltpu.roll(a, 4, 0), b)
+            for p in range(2):
+                a, b = up[p, 0], up[p, 1]
+                across[p, 0] = jnp.where(left, a, pltpu.roll(b, 64, 1))
+                across[p, 1] = jnp.where(left, pltpu.roll(a, 64, 1), b)
+            fields += [across[0, 0], across[1, 0], across[0, 1], across[1, 1]]
+        return fields
+
+    def take(d, carry):
+        last = spread(d, FIELDS // 8 - 1)
+        plane[0] = last[4] * (1.0 / CODE)
+        plane[1] = last[5]
+        unit = [jnp.exp2(last[6 + t]) * (1.0 / CODE) for t in range(2)]
+        for pair in range(FIELDS // 8):
+            fields = last if pair == FIELDS // 8 - 1 else spread(d, pair)
+            for i, value in enumerate(fields):
+                which, k = divmod(8 * pair + i, OWN_LEVELS)
+                if which < 2:
+                    cells[pl.ds(which * 8 * PITCH + OWN_LEVELS * d + k, 8, stride=PITCH), :] = (
+                        value * unit[which]
+                    )
+                elif which < 4:
+                    flow[which - 2, OWN_LEVELS * d + k] = value * (FASTEST / CODE)
+        return carry
+
+    lax.fori_loop(0, BLOCKS, take, 0)
+
+    wet_levels = plane[1]
+
+    def north(x, by):
+        y = pltpu.roll(x, 64, 1)
+        return pltpu.roll(jnp.where(sub < by, y, x), 8 - by, 0)
+
+    def south(x, by):
+        y = pltpu.roll(x, 64, 1)
+        return pltpu.roll(jnp.where(sub >= 8 - by, y, x), by, 0)
+
+    def faces(w):
+        size = jnp.abs(w)
+        return (
+            (-w - size) * (1.0 / 12.0),
+            (7.0 * w + 3.0 * size) * (1.0 / 12.0),
+            (7.0 * w - 3.0 * size) * (1.0 / 12.0),
+            (size - w) * (1.0 / 12.0),
+        )
+
+    def prepare(k, carry):
+        wet = jnp.where(wet_levels > k.astype(F32), 1.0, 0.0)
+        for t in range(2):
+            at = pl.ds(t * 8 * PITCH + k, 8, stride=PITCH)
+            cells[at, :] = wet * cells[at, :]
+        east_w = flow[0, k] * wet * pltpu.roll(wet, 127, 1)
+        north_w = jnp.where(row == 15, 0.0, flow[1, k] * wet * north(wet, 1))
+        west_w = pltpu.roll(east_w, 1, 1)
+        south_w = jnp.where(row == 0, 0.0, south(north_w, 1))
+        a, b, d, e = faces(east_w)
+        a1, b1, d1, e1 = faces(west_w)
+        p, q, r, s = faces(north_w)
+        p1, q1, r1, s1 = faces(south_w)
+        coef[k, 0] = wet * (1.0 + (d1 - b) + (r1 - q))
+        coef[k, 1] = wet * a1
+        coef[k, 2] = wet * (b1 - a)
+        coef[k, 3] = wet * (e1 - d)
+        coef[k, 4] = -wet * e
+        coef[k, 5] = jnp.where(row <= 1, 0.0, wet * p1)
+        coef[k, 6] = jnp.where(row == 0, 0.0, wet * (q1 - p))
+        coef[k, 7] = jnp.where(row == 15, 0.0, wet * (s1 - r))
+        coef[k, 8] = jnp.where(row >= 14, 0.0, -wet * s)
+        return carry
+
+    lax.fori_loop(0, LEVELS, prepare, 0, unroll=2)
+
+    deep = index((LEVELS, 128), 0)
+    light[...] = jnp.exp(deep.astype(F32) * (-4.0 / LEVELS))
+
+    def stage(x, c):
+        y = pltpu.roll(x, 64, 1)
+        total = c[0] * x
+        total += c[1] * pltpu.roll(x, 2, 1) + c[2] * pltpu.roll(x, 1, 1)
+        total += c[3] * pltpu.roll(x, 127, 1) + c[4] * pltpu.roll(x, 126, 1)
+        total += c[5] * pltpu.roll(jnp.where(sub >= 6, y, x), 2, 0)
+        total += c[6] * pltpu.roll(jnp.where(sub >= 7, y, x), 1, 0)
+        total += c[7] * pltpu.roll(jnp.where(sub < 1, y, x), 7, 0)
+        total += c[8] * pltpu.roll(jnp.where(sub < 2, y, x), 6, 0)
+        return total
+
+    def transport(k, carry):
+        c = [coef[k, i] for i in range(9)]
+        for t in range(2):
+            at = pl.ds(t * 8 * PITCH + k, 8, stride=PITCH)
+            x = cells[at, :]
+            moved[at, :] = 0.5 * (x + stage(stage(x, c), c))
+        return carry
+
+    def step(n, carry):
+        lax.fori_loop(0, LEVELS, transport, 0, unroll=4)
+        for pair in range(4):
+            mixed = []
+            for t in range(2):
+                base = (t * 8 + 2 * pair) * PITCH
+                both = jnp.concatenate(
+                    [moved[base : base + LEVELS, :], moved[base + PITCH : base + PITCH + LEVELS, :]],
+                    axis=1,
+                ).astype(jnp.bfloat16)
+                mixed.append(jnp.dot(ops[t], both, preferred_element_type=F32))
+            for i in range(2):
+                s = 2 * pair + i
+                wet = deep.astype(F32) < plane[1, s : s + 1, :]
+                p = jnp.where(wet, mixed[0][:, 128 * i : 128 * i + 128], 0.0)
+                q = jnp.where(wet, mixed[1][:, 128 * i : 128 * i + 128], 0.0)
+                square = p * p
+                uptake = (plane[0, s : s + 1, :] * light[...]) * (
+                    square * p / (square + half_sat_sq)
+                )
+                gain = uptake - remin_rate * q
+                cells[s * PITCH : s * PITCH + LEVELS, :] = p - gain
+                cells[(8 + s) * PITCH : (8 + s) * PITCH + LEVELS, :] = q + gain
+        return carry
+
+    lax.fori_loop(0, STEPS, step, 0)
+
+    own = lax.axis_index("depth")
+    chunk = lane // 32
+
+    def send(n, carry):
+        to = own ^ n
+        blocks = []
+        for t in range(2):
+            def level(k):
+                return cells[pl.ds(t * 8 * PITCH + OWN_LEVELS * to + k, 8, stride=PITCH), :]
+
+            largest = jnp.abs(level(0))
+            for k in range(1, OWN_LEVELS):
+                largest = jnp.maximum(largest, jnp.abs(level(k)))
+            scale = exponent(largest)
+            per_unit = CODE * jnp.exp2(-scale)
+            blocks += [level(k) * per_unit for k in range(OWN_LEVELS)] + [scale]
+        for pair in range(ENDS // 4):
+            halves = []
+            for i in (2 * pair, 2 * pair + 1):
+                a, b = blocks[2 * i], blocks[2 * i + 1]
+                halves.append(
+                    jnp.where(
+                        chunk == 0,
+                        pltpu.roll(a, 112, 1),
+                        jnp.where(
+                            chunk == 1,
+                            pltpu.roll(a, 80, 1),
+                            jnp.where(chunk == 2, pltpu.roll(b, 48, 1), pltpu.roll(b, 16, 1)),
+                        ),
+                    )
+                )
+            ends[n, 16 * pair : 16 * pair + 16, :] = coded(jnp.concatenate(halves, axis=0))
+        return carry
+
+    lax.fori_loop(0, BLOCKS, send, 0)
+    for n, out in enumerate((out0, out1, out2, out3)):
+        out[...] = ends[n]
+
+
+def turn_kernel(in0, in1, in2, in3, out0, out1, out2, out3, got, sent):
+    block = lax.axis_index("depth")
+    tile = lax.axis_index("tile")
+    for n, ref in enumerate((in0, in1, in2, in3)):
+        got[block ^ n] = ref[...]
+    sub = index((8, 128), 0)
+    chunk = index((8, 128), 1) // 32
+    for pair in range(ENDS // 4):
+        whole = [
+            got[d, 16 * pair : 16 * pair + 16, :].astype(jnp.int32).astype(F32) for d in range(4)
+        ]
+        halves = {t: [] for t in range(4)}
+        for part in range(2):
+            m = [x[8 * part : 8 * part + 8] for x in whole]
+            lined = {}
+            for par in range(2):
+                for h in range(2):
+                    z = [pltpu.roll(m[d], (32 * (d - 2 * par - h)) % 128, 1) for d in range(4)]
+                    lined[par, h] = jnp.where(
+                        chunk == 0,
+                        z[0],
+                        jnp.where(chunk == 1, z[1], jnp.where(chunk == 2, z[2], z[3])),
+                    )
+            for h in range(2):
+                a, b = lined[0, h], lined[1, h]
+                halves[2 * h].append(jnp.where(sub < 4, a, pltpu.roll(b, 4, 0)))
+                halves[2 * h + 1].append(jnp.where(sub < 4, pltpu.roll(a, 4, 0), b))
+        for t in range(4):
+            sent[t, 16 * pair : 16 * pair + 16, :] = (
+                jnp.concatenate(halves[t], axis=0).astype(jnp.int32).astype(I16)
+            )
+    for n, out in enumerate((out0, out1, out2, out3)):
+        out[...] = sent[(tile + n) % TILES]
+
+
+def finish_kernel(in0, in1, in2, in3, state, land_sea, depth_index, out, got):
+    block = lax.axis_index("depth")
+    tile = lax.axis_index("tile")
+    for n, ref in enumerate((in0, in1, in2, in3)):
+        got[(tile + TILES - n) % TILES] = ref[...]
+    wet_levels = jnp.where(land_sea[...] == 1, depth_index[...], 0)
+    first = block * OWN_LEVELS
+    for q in range(4):
+        lanes = slice(128 * q, 128 * q + 128)
+        values = []
+        for pair in range(ENDS // 4):
+            x = got[q, 16 * pair : 16 * pair + 16, :].astype(jnp.int32).astype(F32)
+            values += [x[0:4], x[4:8], x[8:12], x[12:16]]
+        for t in range(2):
+            base = t * (OWN_LEVELS + 1)
+            unit = jnp.exp2(values[base + OWN_LEVELS]) * (1.0 / CODE)
+            for k in range(OWN_LEVELS):
+                wet = wet_levels[:, lanes] > first + k
+                out[0, t, k, :, lanes] = jnp.where(
+                    wet, values[base + k] * unit - state[0, t, k, :, lanes], 0.0
+                )
+
+
+def window_shards(initial_states, velocity, growth, land_sea, depth_index, column_ops):
+    group = ("tile", "depth")
+    devices = TILES * BLOCKS
+    chunk = (2 * FIELDS, 128)
+    packed = pl.pallas_call(
+        pack_kernel,
+        out_shape=jax.ShapeDtypeStruct((devices,) + chunk, I16),
+        in_specs=[VMEM] * 5,
+        out_specs=VMEM,
+    )(initial_states, velocity, growth, land_sea, depth_index)
+    received = lax.all_to_all(packed, group, 0, 0, tiled=True)
+    message = jax.ShapeDtypeStruct((4 * ENDS, 128), I16)
+    out = pl.pallas_call(
+        steps_kernel,
+        out_shape=[message] * 4,
+        in_specs=[VMEM] * 2,
+        out_specs=[VMEM] * 4,
+        scratch_shapes=[
+            pltpu.VMEM((2 * 8 * PITCH, 128), F32),
+            pltpu.VMEM((2 * 8 * PITCH, 128), F32),
+            pltpu.VMEM((2, LEVELS, 8, 128), F32),
+            pltpu.VMEM((LEVELS, 9, 8, 128), F32),
+            pltpu.VMEM((2, 8, 128), F32),
+            pltpu.VMEM((LEVELS, 128), F32),
+            pltpu.VMEM((4, 4 * ENDS, 128), I16),
+        ],
+    )(received, column_ops)
+    got = [out[0]] + [
+        lax.ppermute(out[n], "depth", [(i, i ^ n) for i in range(BLOCKS)]) for n in range(1, 4)
+    ]
+    turned = pl.pallas_call(
+        turn_kernel,
+        out_shape=[message] * 4,
+        in_specs=[VMEM] * 4,
+        out_specs=[VMEM] * 4,
+        scratch_shapes=[pltpu.VMEM((4, 4 * ENDS, 128), I16)] * 2,
+    )(*got)
+    segs = lax.axis_size("seg")
+    last = [
+        lax.ppermute(
+            turned[n],
+            ("seg", "tile"),
+            [
+                (s * TILES + t, ((s + 1) % segs) * TILES + (t + n) % TILES)
+                for s in range(segs)
+                for t in range(TILES)
+            ],
+        )
+        for n in range(4)
+    ]
+    return pl.pallas_call(
+        finish_kernel,
+        out_shape=jax.ShapeDtypeStruct(initial_states.shape, F32),
+        in_specs=[VMEM] * 7,
+        out_specs=VMEM,
+        scratch_shapes=[pltpu.VMEM((4, 4 * ENDS, 128), I16)],
+    )(*last, initial_states, land_sea, depth_index)
+
+
+def shards(initial_states, velocity, growth, land_sea, depth_index, column_ops):
+    fits = (
+        lax.axis_size("tile") == TILES
+        and lax.axis_size("depth") == BLOCKS
+        and initial_states.shape == (1, 2, OWN_LEVELS, 4, TILES * BLOCKS * OWN)
+    )
+    plan = window_shards if fits else stepwise_shards
+    return plan(initial_states, velocity, growth, land_sea, depth_index, column_ops)
+
+
 def solution(mesh):
     return jax.shard_map(
         shards,

time: 141 us -> 78.3 us (0.56)
  Pallas kernels: 0 us -> 35.5 us
  waiting for transfers between devices: 57.8 us -> 23 us
  blocking collectives: 29.4 us -> 0 us
  other arithmetic: 15.3 us -> 0 us
  starting transfers between devices: 26.8 us -> 16.8 us
  local copies, waits for them, and re-layouts: 9.22 us -> 2.71 us
    ppermute x11 -> x7, waiting for transfers between devices: 57.8 us -> 7.03 us  [the longest x3 3.62 us: window_shards(): lax.ppermute(out[n], 'depth', [(i, i ^ n) for i in range(BLOCKS)])]
    pallas_call x0 -> x4, Pallas kernels: none -> 35.5 us  [the longest x1 28.9 us: window_shards(): pl.pallas_call(steps_kernel, out_shape=[message] * 4, in_specs=[VMEM] * 2...]
    all_gather x4 -> x0, blocking collectives: 29.4 us -> none  [shards(): lax.all_gather(rounded, 'depth', axis=2, tiled=True)]
    ppermute x11 -> x7, starting transfers between devices: 26.8 us -> 9.27 us  [the longest x4 7.4 us: window_shards(): lax.ppermute(turned[n], ('seg', 'tile'), [(s * TILES + t, (s + 1) % segs...]
    all_to_all x0 -> x1, waiting for transfers between devices: none -> 16 us  [window_shards(): received = lax.all_to_all(packed, group, 0, 0, tiled=True)]
    all_to_all x0 -> x1, starting transfers between devices: none -> 7.49 us  [window_shards(): received = lax.all_to_all(packed, group, 0, 0, tiled=True)]
    sub x16 -> x0, other arithmetic: 6.01 us -> none  [face_flux(): courant * (7.0 * (near_side + far_side) - (behind + beyond)) / 12.0]
    slice x44 -> x0, local copies, waits for them, and re-layouts: 5.97 us -> none  [the longest x16 2.69 us: tendency(): jnp.roll(centre, -1, axis=-1)]
  transfers between devices with their start and end apart: 11 -> 8, of which waited for: 11 -> 6; matrix products, arithmetic and copies ran while one was open for 2% -> 1% of each run, Pallas kernels for 0% -> 0%
where the time goes in v1:
time: 78.3 us; the launch traced here: 78 us
  Pallas kernels  35.5 us (45%)
  waiting for transfers between devices  23 us (29%)
  starting transfers between devices  16.8 us (21%)
  local copies, waits for them, and re-layouts  2.71 us (3%)
    pallas_call x1, Pallas kernels, window_shards(): pl.pallas_call(steps_kernel, out_shape=[message] * 4, in_specs=[VMEM] * 2...  28.9 us
    all_to_all x1, waiting for transfers between devices, window_shards(): received = lax.all_to_all(packed, group, 0, 0, tiled=True)  16 us
    all_to_all x1, starting transfers between devices, window_shards(): received = lax.all_to_all(packed, group, 0, 0, tiled=True)  7.49 us
    ppermute x4, starting transfers between devices, window_shards(): lax.ppermute(turned[n], ('seg', 'tile'), [(s * TILES + t, (s + 1) % segs...  7.4 us
    ppermute x3, waiting for transfers between devices, window_shards(): lax.ppermute(out[n], 'depth', [(i, i ^ n) for i in range(BLOCKS)])  3.62 us
    ppermute x4, waiting for transfers between devices, window_shards(): lax.ppermute(turned[n], ('seg', 'tile'), [(s * TILES + t, (s + 1) % segs...  3.41 us
    unnamed x19, local copies, waits for them, and re-layouts  2.71 us
    pallas_call x1, Pallas kernels, window_shards(): pl.pallas_call(pack_kernel, out_shape=jax.ShapeDtypeStruct((devices,) + c...  2.71 us
  transfers between devices with their start and end apart: 8, of which 6 were waited for; matrix products, arithmetic and copies ran while one was open for 1% of the time, Pallas kernels for 0%

profile of v1, /device:TPU:0, one launch (start us, length us, event | category | flops | bytes accessed | tf_op | source)
XLA Modules:
  0.0 78.0 jit_solution(15157167745101446160)
XLA Ops:
  0.0 2.7 %shard_map.64 = s16[16,160,128]{2,1,0:T(8,128)(2,1)} custom-call(f32[1,2,19,4,512]{4,3,2,1,0:T(4,128)} %state.3, f32[1,2,19,4,512]{4,3,2,1,0:T(4,128)} %velocity.1, f32[1,4,512]{2,1,0:T(4,128)} %growth.1, s32[4,512]{1,0:T(4,128)} %land_sea.3, s32[4,512]{1,0:T(4,128)} %depth_index.3), custom_call_target="tpu_custom_call" | custom-call | tf_op jit(solution)/shard_map/pallas_call | solution.py:442
  2.7 0.0 copy-start.8
  2.7 7.5 %all-to-all-start = ((s16[16,160,128]{2,1,0:T(8,128)(2,1)}), s16[16,160,128]{2,1,0:T(8,128)(2,1)S(1)}, u32[]{:S(2)}, u32[]{:S(2)}) async-start(s16[16,160,128]{2,1,0:T(8,128)(2,1)} %shard_map.64), calls=%async_computation | async-start | bytes 1310720 | tf_op jit(solution)/shard_map/all_to_all | solution.py:448
  10.2 0.0 copy-done.8
  10.2 0.6 copy.7.ops
  10.8 16.0 %all-to-all-done.recv = s16[16,160,128]{2,1,0:T(8,128)(2,1)S(1)} async-done(((s16[16,160,128]{2,1,0:T(8,128)(2,1)}), s16[16,160,128]{2,1,0:T(8,128)(2,1)S(1)}, u32[]{:S(2)}, u32[]{:S(2)}) %all-to-all-start) | async-done | bytes 655392 | tf_op jit(solution)/shard_map/all_to_all | solution.py:448
  26.8 0.0 copy-start
  26.8 0.8 %copy-done = s16[16,160,128]{2,1,0:T(8,128)(2,1)} copy-done((s16[16,160,128]{2,1,0:T(8,128)(2,1)}, s16[16,160,128]{2,1,0:T(8,128)(2,1)S(1)}, u32[]{:S(2)}) %copy-start) | copy-done | bytes 655384
  27.7 28.9 %shard_map.65 = (s16[160,128]{1,0:T(8,128)(2,1)}, s16[160,128]{1,0:T(8,128)(2,1)}, s16[160,128]{1,0:T(8,128)(2,1)}, s16[160,128]{1,0:T(8,128)(2,1)}) custom-call(s16[16,160,128]{2,1,0:T(8,128)(2,1)} %copy-done, bf16[2,76,76]{2,1,0:T(8,128)(2,1)} %copy.7.ops), custom_call_target="tpu_custom_call" | custom-call | tf_op jit(solution)/shard_map/pallas_call | solution.py:450
  56.6 0.1 collective-permute-start
  56.7 1.4 %collective-permute-start.1 = (s16[160,128]{1,0:T(8,128)(2,1)}, s16[160,128]{1,0:T(8,128)(2,1)S(1)}, u32[]{:S(2)}, u32[]{:S(2)}) collective-permute-start(s16[160,128]{1,0:T(8,128)(2,1)} %get-tuple-element.15), channel_id=1, source_target_pairs={{0,2},{1,3},{2,0},{3,1},{4,6},{5,7},{6,4},{7,5},{8,10},{9,11},{10,... | collective-permute-start | bytes 122888 | tf_op jit(solution)/shard_map/ppermute | solution.py:466
  58.1 0.4 collective-permute-start.2
  58.5 0.0 collective-permute-done.in1
  58.5 0.0 copy-start.5
  58.5 2.4 %collective-permute-done.1.in2 = s16[160,128]{1,0:T(8,128)(2,1)S(1)} collective-permute-done((s16[160,128]{1,0:T(8,128)(2,1)}, s16[160,128]{1,0:T(8,128)(2,1)S(1)}, u32[]{:S(2)}, u32[]{:S(2)}) %collective-permute-start.1) | collective-permute-done | bytes 40992 | tf_op jit(solution)/shard_map/ppermute | solution.py:466
  60.9 0.0 copy-start.6
  60.9 1.2 %collective-permute-done.2.in3 = s16[160,128]{1,0:T(8,128)(2,1)S(1)} collective-permute-done((s16[160,128]{1,0:T(8,128)(2,1)}, s16[160,128]{1,0:T(8,128)(2,1)S(1)}, u32[]{:S(2)}, u32[]{:S(2)}) %collective-permute-start.2) | collective-permute-done | bytes 40992 | tf_op jit(solution)/shard_map/ppermute | solution.py:466
  62.1 0.0 copy-start.7
  62.1 0.0 copy-done.5
  62.1 0.0 copy-done.6
  62.1 0.6 copy-done.7
  62.7 1.9 %shard_map.66 = (s16[160,128]{1,0:T(8,128)(2,1)}, s16[160,128]{1,0:T(8,128)(2,1)}, s16[160,128]{1,0:T(8,128)(2,1)}, s16[160,128]{1,0:T(8,128)(2,1)}) custom-call(s16[160,128]{1,0:T(8,128)(2,1)} %get-tuple-element.13.in0, s16[160,128]{1,0:T(8,128)(2,1)} %copy-done.5, s16[160,128]{1,0:T(8,128)(2,1)} %copy-done.6, s16[160,128]{1,0:T(8,128)(2,1)} %copy-done.7), custom_call_target="tpu_custom_call" | custom-call | tf_op jit(solution)/shard_map/pallas_call | solution.py:468
  64.6 1.5 %collective-permute-start.3 = (s16[160,128]{1,0:T(8,128)(2,1)}, s16[160,128]{1,0:T(8,128)(2,1)S(1)}, u32[]{:S(2)}, u32[]{:S(2)}) collective-permute-start(s16[160,128]{1,0:T(8,128)(2,1)} %get-tuple-element.17), channel_id=1, source_target_pairs={{0,16},{4,20},{8,24},{12,28},{16,0},{20,4},{24,8},{28,12},{1,17},{... | collective-permute-start | bytes 122888 | tf_op jit(solution)/shard_map/ppermute | solution.py:477
  66.1 1.8 %collective-permute-start.4 = (s16[160,128]{1,0:T(8,128)(2,1)}, s16[160,128]{1,0:T(8,128)(2,1)S(1)}, u32[]{:S(2)}, u32[]{:S(2)}) collective-permute-start(s16[160,128]{1,0:T(8,128)(2,1)} %get-tuple-element.18), channel_id=1, source_target_pairs={{0,20},{4,24},{8,28},{12,16},{16,4},{20,8},{24,12},{28,0},{1,21},{... | collective-permute-start | bytes 122888 | tf_op jit(solution)/shard_map/ppermute | solution.py:477
  67.9 2.4 %collective-permute-start.5 = (s16[160,128]{1,0:T(8,128)(2,1)}, s16[160,128]{1,0:T(8,128)(2,1)S(1)}, u32[]{:S(2)}, u32[]{:S(2)}) collective-permute-start(s16[160,128]{1,0:T(8,128)(2,1)} %get-tuple-element.19), channel_id=1, source_target_pairs={{0,24},{4,28},{8,16},{12,20},{16,8},{20,12},{24,0},{28,4},{1,25},{... | collective-permute-start | bytes 122888 | tf_op jit(solution)/shard_map/ppermute | solution.py:477
  70.3 1.7 %collective-permute-start.6 = (s16[160,128]{1,0:T(8,128)(2,1)}, s16[160,128]{1,0:T(8,128)(2,1)S(1)}, u32[]{:S(2)}, u32[]{:S(2)}) collective-permute-start(s16[160,128]{1,0:T(8,128)(2,1)} %get-tuple-element.20), channel_id=1, source_target_pairs={{0,28},{4,16},{8,20},{12,24},{16,12},{20,0},{24,4},{28,8},{1,29},{... | collective-permute-start | bytes 122888 | tf_op jit(solution)/shard_map/ppermute | solution.py:477
  72.0 0.0 collective-permute-done.3.in0
  72.0 0.0 copy-start.1
  72.0 1.4 %collective-permute-done.4.in1 = s16[160,128]{1,0:T(8,128)(2,1)S(1)} collective-permute-done((s16[160,128]{1,0:T(8,128)(2,1)}, s16[160,128]{1,0:T(8,128)(2,1)S(1)}, u32[]{:S(2)}, u32[]{:S(2)}) %collective-permute-start.4) | collective-permute-done | bytes 40992 | tf_op jit(solution)/shard_map/ppermute | solution.py:477
  73.4 0.0 copy-start.2
  73.4 1.2 %collective-permute-done.5.in2 = s16[160,128]{1,0:T(8,128)(2,1)S(1)} collective-permute-done((s16[160,128]{1,0:T(8,128)(2,1)}, s16[160,128]{1,0:T(8,128)(2,1)S(1)}, u32[]{:S(2)}, u32[]{:S(2)}) %collective-permute-start.5) | collective-permute-done | bytes 40992 | tf_op jit(solution)/shard_map/ppermute | solution.py:477
  74.5 0.0 copy-start.3
  74.5 0.8 %collective-permute-done.6.in3 = s16[160,128]{1,0:T(8,128)(2,1)S(1)} collective-permute-done((s16[160,128]{1,0:T(8,128)(2,1)}, s16[160,128]{1,0:T(8,128)(2,1)S(1)}, u32[]{:S(2)}, u32[]{:S(2)}) %collective-permute-start.6) | collective-permute-done | bytes 40992 | tf_op jit(solution)/shard_map/ppermute | solution.py:477
  75.4 0.0 copy-done.1
  75.4 0.0 copy-done.2
  75.4 0.0 copy-done.3
  75.4 0.0 copy-start.4
  75.4 0.6 copy-done.4
  76.0 1.9 %shard_map.67 = f32[1,2,19,4,512]{4,3,2,1,0:T(4,128)} custom-call(s16[160,128]{1,0:T(8,128)(2,1)} %copy-done.1, s16[160,128]{1,0:T(8,128)(2,1)} %copy-done.2, s16[160,128]{1,0:T(8,128)(2,1)} %copy-done.3, s16[160,128]{1,0:T(8,128)(2,1)} %copy-done.4, f32[1,2,19,4,512]{4,3,2,1,0:T(4,128)} %state.3, s32[4,512]{1,0:T(4,128)} %land_sea.3, s32[4,512]{1,0:T(4,128)} %depth_index.3), custom_call_target="tpu_custom_call" | custom-call | tf_op jit(solution)/shard_map/pallas_call | solution.py:488
Async XLA Ops:
  2.7 7.5 %copy-start.8 = (bf16[2,76,76]{2,0,1:T(2,128)(2,1)S(1)}, bf16[2,76,76]{2,0,1:T(2,128)(2,1)}, u32[]{:S(2)}) copy-start(bf16[2,76,76]{2,0,1:T(2,128)(2,1)} %param.11) | copy-start | bytes 69316
  2.7 24.1 %all-to-all-start = ((s16[16,160,128]{2,1,0:T(8,128)(2,1)}), s16[16,160,128]{2,1,0:T(8,128)(2,1)S(1)}, u32[]{:S(2)}, u32[]{:S(2)}) async-start(s16[16,160,128]{2,1,0:T(8,128)(2,1)} %shard_map.64), calls=%async_computation | async-start | bytes 1310720 | tf_op jit(solution)/shard_map/all_to_all | solution.py:448
  26.8 0.9 %copy-start = (s16[16,160,128]{2,1,0:T(8,128)(2,1)}, s16[16,160,128]{2,1,0:T(8,128)(2,1)S(1)}, u32[]{:S(2)}) copy-start(s16[16,160,128]{2,1,0:T(8,128)(2,1)S(1)} %all-to-all-done.recv) | copy-start | bytes 1966084
  56.6 1.9 %collective-permute-start = (s16[160,128]{1,0:T(8,128)(2,1)}, s16[160,128]{1,0:T(8,128)(2,1)S(1)}, u32[]{:S(2)}, u32[]{:S(2)}) collective-permute-start(s16[160,128]{1,0:T(8,128)(2,1)} %get-tuple-element.14), channel_id=1, source_target_pairs={{0,1},{1,0},{2,3},{3,2},{4,5},{5,4},{6,7},{7,6},{8,9},{9,8},{10,11... | collective-permute-start | bytes 122888 | tf_op jit(solution)/shard_map/ppermute | solution.py:466
  56.7 4.2 %collective-permute-start.1 = (s16[160,128]{1,0:T(8,128)(2,1)}, s16[160,128]{1,0:T(8,128)(2,1)S(1)}, u32[]{:S(2)}, u32[]{:S(2)}) collective-permute-start(s16[160,128]{1,0:T(8,128)(2,1)} %get-tuple-element.15), channel_id=1, source_target_pairs={{0,2},{1,3},{2,0},{3,1},{4,6},{5,7},{6,4},{7,5},{8,10},{9,11},{10,... | collective-permute-start | bytes 122888 | tf_op jit(solution)/shard_map/ppermute | solution.py:466
  58.1 4.0 %collective-permute-start.2 = (s16[160,128]{1,0:T(8,128)(2,1)}, s16[160,128]{1,0:T(8,128)(2,1)S(1)}, u32[]{:S(2)}, u32[]{:S(2)}) collective-permute-start(s16[160,128]{1,0:T(8,128)(2,1)} %get-tuple-element.16), channel_id=1, source_target_pairs={{0,3},{1,2},{2,1},{3,0},{4,7},{5,6},{6,5},{7,4},{8,11},{9,10},{10,... | collective-permute-start | bytes 122888 | tf_op jit(solution)/shard_map/ppermute | solution.py:466
  58.5 3.6 %copy-start.5 = (s16[160,128]{1,0:T(8,128)(2,1)}, s16[160,128]{1,0:T(8,128)(2,1)S(1)}, u32[]{:S(2)}) copy-start(s16[160,128]{1,0:T(8,128)(2,1)S(1)} %collective-permute-done.in1) | copy-start | bytes 122884
  60.9 1.2 %copy-start.6 = (s16[160,128]{1,0:T(8,128)(2,1)}, s16[160,128]{1,0:T(8,128)(2,1)S(1)}, u32[]{:S(2)}) copy-start(s16[160,128]{1,0:T(8,128)(2,1)S(1)} %collective-permute-done.1.in2) | copy-start | bytes 122884
  62.1 0.6 copy-start.7
  64.6 7.4 %collective-permute-start.3 = (s16[160,128]{1,0:T(8,128)(2,1)}, s16[160,128]{1,0:T(8,128)(2,1)S(1)}, u32[]{:S(2)}, u32[]{:S(2)}) collective-permute-start(s16[160,128]{1,0:T(8,128)(2,1)} %get-tuple-element.17), channel_id=1, source_target_pairs={{0,16},{4,20},{8,24},{12,28},{16,0},{20,4},{24,8},{28,12},{1,17},{... | collective-permute-start | bytes 122888 | tf_op jit(solution)/shard_map/ppermute | solution.py:477
  66.1 7.3 %collective-permute-start.4 = (s16[160,128]{1,0:T(8,128)(2,1)}, s16[160,128]{1,0:T(8,128)(2,1)S(1)}, u32[]{:S(2)}, u32[]{:S(2)}) collective-permute-start(s16[160,128]{1,0:T(8,128)(2,1)} %get-tuple-element.18), channel_id=1, source_target_pairs={{0,20},{4,24},{8,28},{12,16},{16,4},{20,8},{24,12},{28,0},{1,21},{... | collective-permute-start | bytes 122888 | tf_op jit(solution)/shard_map/ppermute | solution.py:477
  67.9 6.7 %collective-permute-start.5 = (s16[160,128]{1,0:T(8,128)(2,1)}, s16[160,128]{1,0:T(8,128)(2,1)S(1)}, u32[]{:S(2)}, u32[]{:S(2)}) collective-permute-start(s16[160,128]{1,0:T(8,128)(2,1)} %get-tuple-element.19), channel_id=1, source_target_pairs={{0,24},{4,28},{8,16},{12,20},{16,8},{20,12},{24,0},{28,4},{1,25},{... | collective-permute-start | bytes 122888 | tf_op jit(solution)/shard_map/ppermute | solution.py:477
  70.3 5.1 %collective-permute-start.6 = (s16[160,128]{1,0:T(8,128)(2,1)}, s16[160,128]{1,0:T(8,128)(2,1)S(1)}, u32[]{:S(2)}, u32[]{:S(2)}) collective-permute-start(s16[160,128]{1,0:T(8,128)(2,1)} %get-tuple-element.20), channel_id=1, source_target_pairs={{0,28},{4,16},{8,20},{12,24},{16,12},{20,0},{24,4},{28,8},{1,29},{... | collective-permute-start | bytes 122888 | tf_op jit(solution)/shard_map/ppermute | solution.py:477
  72.0 3.4 %copy-start.1 = (s16[160,128]{1,0:T(8,128)(2,1)}, s16[160,128]{1,0:T(8,128)(2,1)S(1)}, u32[]{:S(2)}) copy-start(s16[160,128]{1,0:T(8,128)(2,1)S(1)} %collective-permute-done.3.in0) | copy-start | bytes 122884
  73.4 2.0 %copy-start.2 = (s16[160,128]{1,0:T(8,128)(2,1)}, s16[160,128]{1,0:T(8,128)(2,1)S(1)}, u32[]{:S(2)}) copy-start(s16[160,128]{1,0:T(8,128)(2,1)S(1)} %collective-permute-done.4.in1) | copy-start | bytes 122884
  74.5 0.9 %copy-start.3 = (s16[160,128]{1,0:T(8,128)(2,1)}, s16[160,128]{1,0:T(8,128)(2,1)S(1)}, u32[]{:S(2)}) copy-start(s16[160,128]{1,0:T(8,128)(2,1)S(1)} %collective-permute-done.5.in2) | copy-start | bytes 122884
  75.4 0.6 copy-start.4

commit v2 on v1

--- a/solution.py
+++ b/solution.py
@@ -203,7 +203,6 @@
     sub = index((8, 128), 0)
     lane = index((8, 128), 1)
     left = lane < 64
-    row = sub + 8 * (lane // 64)
 
     def spread(d, pair):
         sent = [
@@ -239,20 +238,18 @@
                         value * unit[which]
                     )
                 elif which < 4:
-                    flow[which - 2, OWN_LEVELS * d + k] = value * (FASTEST / CODE)
+                    at = pl.ds((which - 2) * 8 * PITCH + OWN_LEVELS * d + k, 8, stride=PITCH)
+                    flow[at, :] = value * (FASTEST / CODE)
         return carry
 
     lax.fori_loop(0, BLOCKS, take, 0)
 
-    wet_levels = plane[1]
-
-    def north(x, by):
-        y = pltpu.roll(x, 64, 1)
-        return pltpu.roll(jnp.where(sub < by, y, x), 8 - by, 0)
-
-    def south(x, by):
-        y = pltpu.roll(x, 64, 1)
-        return pltpu.roll(jnp.where(sub >= 8 - by, y, x), by, 0)
+    for field in (cells, flow):
+        for s in range(16):
+            field[s * PITCH + LEVELS : (s + 1) * PITCH, :] = jnp.zeros((PITCH - LEVELS, 128), F32)
+
+    def block(base, g):
+        return pl.ds(pl.multiple_of(base * PITCH + 8 * g, 8), 8)
 
     def faces(w):
         size = jnp.abs(w)
@@ -263,56 +260,75 @@
             (size - w) * (1.0 / 12.0),
         )
 
-    def prepare(k, carry):
-        wet = jnp.where(wet_levels > k.astype(F32), 1.0, 0.0)
+    def prepare(g, carry):
+        level = (sub + 8 * g).astype(F32)
+        wet = [jnp.where(plane[1, s : s + 1, :] > level, 1.0, 0.0) for s in range(8)]
         for t in range(2):
-            at = pl.ds(t * 8 * PITCH + k, 8, stride=PITCH)
-            cells[at, :] = wet * cells[at, :]
-        east_w = flow[0, k] * wet * pltpu.roll(wet, 127, 1)
-        north_w = jnp.where(row == 15, 0.0, flow[1, k] * wet * north(wet, 1))
-        west_w = pltpu.roll(east_w, 1, 1)
-        south_w = jnp.where(row == 0, 0.0, south(north_w, 1))
-        a, b, d, e = faces(east_w)
-        a1, b1, d1, e1 = faces(west_w)
-        p, q, r, s = faces(north_w)
-        p1, q1, r1, s1 = faces(south_w)
-        coef[k, 0] = wet * (1.0 + (d1 - b) + (r1 - q))
-        coef[k, 1] = wet * a1
-        coef[k, 2] = wet * (b1 - a)
-        coef[k, 3] = wet * (e1 - d)
-        coef[k, 4] = -wet * e
-        coef[k, 5] = jnp.where(row <= 1, 0.0, wet * p1)
-        coef[k, 6] = jnp.where(row == 0, 0.0, wet * (q1 - p))
-        coef[k, 7] = jnp.where(row == 15, 0.0, wet * (s1 - r))
-        coef[k, 8] = jnp.where(row >= 14, 0.0, -wet * s)
+            for s in range(8):
+                at = block(8 * t + s, g)
+                cells[at, :] = wet[s] * cells[at, :]
+        beyond = jnp.where(left, pltpu.roll(wet[0], 64, 1), 0.0)
+        north_w = [
+            flow[block(8 + s, g), :] * wet[s] * (wet[s + 1] if s < 7 else beyond) for s in range(8)
+        ]
+        first = jnp.where(left, 0.0, pltpu.roll(north_w[7], 64, 1))
+        merid = [faces(w) for w in [first] + north_w]
+        for s in range(8):
+            east_w = flow[block(s, g), :] * wet[s] * pltpu.roll(wet[s], 127, 1)
+            a, b, d, e = faces(east_w)
+            a1, b1, d1, e1 = faces(pltpu.roll(east_w, 1, 1))
+            p1, q1, r1, s1 = merid[s]
+            p, q, r, s0 = merid[s + 1]
+            south = [wet[s] * p1, wet[s] * (q1 - p)]
+            north = [wet[s] * (s1 - r), -wet[s] * s0]
+            if s < 2:
+                south[0] = jnp.where(left, 0.0, south[0])
+            if s < 1:
+                south[1] = jnp.where(left, 0.0, south[1])
+            if s > 6:
+                north[0] = jnp.where(left, north[0], 0.0)
+            if s > 5:
+                north[1] = jnp.where(left, north[1], 0.0)
+            coef[g, s, 0] = wet[s] * (1.0 + (d1 - b) + (r1 - q))
+            coef[g, s, 1] = wet[s] * a1
+            coef[g, s, 2] = wet[s] * (b1 - a)
+            coef[g, s, 3] = wet[s] * (e1 - d)
+            coef[g, s, 4] = -wet[s] * e
+            coef[g, s, 5], coef[g, s, 6] = south
+            coef[g, s, 7], coef[g, s, 8] = north
         return carry
 
-    lax.fori_loop(0, LEVELS, prepare, 0, unroll=2)
+    lax.fori_loop(0, PITCH // 8, prepare, 0)
 
     deep = index((LEVELS, 128), 0)
     light[...] = jnp.exp(deep.astype(F32) * (-4.0 / LEVELS))
 
-    def stage(x, c):
-        y = pltpu.roll(x, 64, 1)
-        total = c[0] * x
-        total += c[1] * pltpu.roll(x, 2, 1) + c[2] * pltpu.roll(x, 1, 1)
-        total += c[3] * pltpu.roll(x, 127, 1) + c[4] * pltpu.roll(x, 126, 1)
-        total += c[5] * pltpu.roll(jnp.where(sub >= 6, y, x), 2, 0)
-        total += c[6] * pltpu.roll(jnp.where(sub >= 7, y, x), 1, 0)
-        total += c[7] * pltpu.roll(jnp.where(sub < 1, y, x), 7, 0)
-        total += c[8] * pltpu.roll(jnp.where(sub < 2, y, x), 6, 0)
-        return total
-
-    def transport(k, carry):
-        c = [coef[k, i] for i in range(9)]
+    def stage(x, g):
+        turned = [pltpu.roll(x[s], 64, 1) for s in (6, 7, 0, 1)]
+        column = turned[:2] + x + turned[2:]
+        results = []
+        for s in range(8):
+            c = [coef[g, s, i] for i in range(9)]
+            near, far = column[s + 1 : s + 4], (column[s], column[s + 4])
+            centre = near[1]
+            results.append(
+                (c[0] * centre + c[6] * near[0] + c[7] * near[2])
+                + (c[5] * far[0] + c[8] * far[1])
+                + (c[2] * pltpu.roll(centre, 1, 1) + c[3] * pltpu.roll(centre, 127, 1))
+                + (c[1] * pltpu.roll(centre, 2, 1) + c[4] * pltpu.roll(centre, 126, 1))
+            )
+        return results
+
+    def transport(g, carry):
         for t in range(2):
-            at = pl.ds(t * 8 * PITCH + k, 8, stride=PITCH)
-            x = cells[at, :]
-            moved[at, :] = 0.5 * (x + stage(stage(x, c), c))
+            x = [cells[block(8 * t + s, g), :] for s in range(8)]
+            y = stage(stage(x, g), g)
+            for s in range(8):
+                moved[block(8 * t + s, g), :] = 0.5 * (x[s] + y[s])
         return carry
 
     def step(n, carry):
-        lax.fori_loop(0, LEVELS, transport, 0, unroll=4)
+        lax.fori_loop(0, PITCH // 8, transport, 0)
         for pair in range(4):
             mixed = []
             for t in range(2):
@@ -435,43 +451,57 @@
                 )
 
 
+def near(*arrays):
+    return [pltpu.with_memory_space_constraint(x, pltpu.VMEM) for x in arrays]
+
+
+def call(kernel, outs, scratch, *args, reserve=8, place=near):
+    return pl.pallas_call(
+        kernel,
+        out_shape=outs,
+        in_specs=[VMEM] * len(args),
+        out_specs=jax.tree.map(lambda _: VMEM, outs),
+        scratch_shapes=scratch,
+        compiler_params=pltpu.CompilerParams(vmem_limit_bytes=reserve << 20),
+    )(*place(*args))
+
+
 def window_shards(initial_states, velocity, growth, land_sea, depth_index, column_ops):
-    group = ("tile", "depth")
-    devices = TILES * BLOCKS
-    chunk = (2 * FIELDS, 128)
-    packed = pl.pallas_call(
+    message = pltpu.VMEM((4 * ENDS, 128), I16)
+    slots = pltpu.VMEM((4, 4 * ENDS, 128), I16)
+    cells = pltpu.VMEM((2 * 8 * PITCH, 128), F32)
+    packed = call(
         pack_kernel,
-        out_shape=jax.ShapeDtypeStruct((devices,) + chunk, I16),
-        in_specs=[VMEM] * 5,
-        out_specs=VMEM,
-    )(initial_states, velocity, growth, land_sea, depth_index)
-    received = lax.all_to_all(packed, group, 0, 0, tiled=True)
-    message = jax.ShapeDtypeStruct((4 * ENDS, 128), I16)
-    out = pl.pallas_call(
+        pltpu.VMEM((TILES * BLOCKS, 2 * FIELDS, 128), I16),
+        [],
+        initial_states,
+        velocity,
+        growth,
+        land_sea,
+        depth_index,
+        place=lambda *args: args,
+    )
+    received = lax.all_to_all(packed, ("tile", "depth"), 0, 0, tiled=True)
+    out = call(
         steps_kernel,
-        out_shape=[message] * 4,
-        in_specs=[VMEM] * 2,
-        out_specs=[VMEM] * 4,
-        scratch_shapes=[
-            pltpu.VMEM((2 * 8 * PITCH, 128), F32),
-            pltpu.VMEM((2 * 8 * PITCH, 128), F32),
-            pltpu.VMEM((2, LEVELS, 8, 128), F32),
-            pltpu.VMEM((LEVELS, 9, 8, 128), F32),
+        [message] * 4,
+        [
+            cells,
+            cells,
+            cells,
+            pltpu.VMEM((PITCH // 8, 8, 9, 8, 128), F32),
             pltpu.VMEM((2, 8, 128), F32),
             pltpu.VMEM((LEVELS, 128), F32),
-            pltpu.VMEM((4, 4 * ENDS, 128), I16),
+            slots,
         ],
-    )(received, column_ops)
+        received,
+        column_ops,
+        reserve=16,
+    )
     got = [out[0]] + [
         lax.ppermute(out[n], "depth", [(i, i ^ n) for i in range(BLOCKS)]) for n in range(1, 4)
     ]
-    turned = pl.pallas_call(
-        turn_kernel,
-        out_shape=[message] * 4,
-        in_specs=[VMEM] * 4,
-        out_specs=[VMEM] * 4,
-        scratch_shapes=[pltpu.VMEM((4, 4 * ENDS, 128), I16)] * 2,
-    )(*got)
+    turned = call(turn_kernel, [message] * 4, [slots] * 2, *got)
     segs = lax.axis_size("seg")
     last = [
         lax.ppermute(
@@ -485,13 +515,15 @@
         )
         for n in range(4)
     ]
-    return pl.pallas_call(
+    return call(
         finish_kernel,
-        out_shape=jax.ShapeDtypeStruct(initial_states.shape, F32),
-        in_specs=[VMEM] * 7,
-        out_specs=VMEM,
-        scratch_shapes=[pltpu.VMEM((4, 4 * ENDS, 128), I16)],
-    )(*last, initial_states, land_sea, depth_index)
+        jax.ShapeDtypeStruct(initial_states.shape, F32),
+        [slots],
+        *last,
+        initial_states,
+        land_sea,
+        depth_index,
+    )
 
 
 def shards(initial_states, velocity, growth, land_sea, depth_index, column_ops):

time: 78.3 us -> 65 us (0.83)
  Pallas kernels: 35.5 us -> 20.3 us
  local copies, waits for them, and re-layouts: 2.71 us -> 4.05 us
    pallas_call x4, Pallas kernels: 35.5 us -> 20.3 us  [call(): pl.pallas_call(kernel, out_shape=outs, in_specs=[VMEM] * len(args), out_s...]
    unnamed x19, local copies, waits for them, and re-layouts: 2.71 us -> 4.05 us
  transfers between devices with their start and end apart: 8 -> 8, of which waited for: 6 -> 6; matrix products, arithmetic and copies ran while one was open for 1% -> 0% of each run, Pallas kernels for 0% -> 0%
where the time goes in v2:
time: 65 us; the launch traced here: 64.5 us
  waiting for transfers between devices  23.3 us (36%)
  Pallas kernels  20.3 us (31%)
  starting transfers between devices  16.8 us (26%)
  local copies, waits for them, and re-layouts  4.05 us (6%)
    pallas_call x4, Pallas kernels, call(): pl.pallas_call(kernel, out_shape=outs, in_specs=[VMEM] * len(args), out_s...  20.3 us
    all_to_all x1, waiting for transfers between devices, window_shards(): received = lax.all_to_all(packed, ('tile', 'depth'), 0, 0, tiled=True)  16.6 us
    all_to_all x1, starting transfers between devices, window_shards(): received = lax.all_to_all(packed, ('tile', 'depth'), 0, 0, tiled=True)  7.49 us
    ppermute x4, starting transfers between devices, window_shards(): lax.ppermute(turned[n], ('seg', 'tile'), [(s * TILES + t, (s + 1) % segs...  7.36 us
    unnamed x19, local copies, waits for them, and re-layouts  4.05 us
    ppermute x3, waiting for transfers between devices, window_shards(): lax.ppermute(out[n], 'depth', [(i, i ^ n) for i in range(BLOCKS)])  3.49 us
    ppermute x4, waiting for transfers between devices, window_shards(): lax.ppermute(turned[n], ('seg', 'tile'), [(s * TILES + t, (s + 1) % segs...  3.23 us
    ppermute x3, starting transfers between devices, window_shards(): lax.ppermute(out[n], 'depth', [(i, i ^ n) for i in range(BLOCKS)])  1.94 us
  transfers between devices with their start and end apart: 8, of which 6 were waited for; matrix products, arithmetic and copies ran while one was open for 0% of the time, Pallas kernels for 0%

profile of v2, /device:TPU:0, one launch (start us, length us, event | category | flops | bytes accessed | tf_op | source)
XLA Modules:
  0.0 64.5 jit_solution(9694023340086873477)
XLA Ops:
  0.0 0.0 copy-start
  0.0 1.0 %copy-done = f32[1,2,19,4,512]{4,3,2,1,0:T(4,128)S(1)} copy-done((f32[1,2,19,4,512]{4,3,2,1,0:T(4,128)S(1)}, f32[1,2,19,4,512]{4,3,2,1,0:T(4,128)}, u32[]{:S(2)}) %copy-start) | copy-done | bytes 311320
  1.0 0.0 copy-start.2
  1.0 1.0 %copy-done.2 = f32[1,2,19,4,512]{4,3,2,1,0:T(4,128)S(1)} copy-done((f32[1,2,19,4,512]{4,3,2,1,0:T(4,128)S(1)}, f32[1,2,19,4,512]{4,3,2,1,0:T(4,128)}, u32[]{:S(2)}) %copy-start.2) | copy-done | bytes 311320
  1.9 0.0 copy-start.3
  1.9 0.7 %copy-done.3 = s32[4,512]{1,0:T(4,128)S(1)} copy-done((s32[4,512]{1,0:T(4,128)S(1)}, s32[4,512]{1,0:T(4,128)}, u32[]{:S(2)}) %copy-start.3) | copy-done | bytes 8216
  2.6 0.0 copy-start.5
  2.6 0.7 %copy-done.5 = s32[4,512]{1,0:T(4,128)S(1)} copy-done((s32[4,512]{1,0:T(4,128)S(1)}, s32[4,512]{1,0:T(4,128)}, u32[]{:S(2)}) %copy-start.5) | copy-done | bytes 8216
  3.3 0.0 copy-start.7
  3.3 0.7 %copy-done.7 = f32[1,4,512]{2,1,0:T(4,128)S(1)} copy-done((f32[1,4,512]{2,1,0:T(4,128)S(1)}, f32[1,4,512]{2,1,0:T(4,128)}, u32[]{:S(2)}) %copy-start.7) | copy-done | bytes 8216
  4.0 1.6 %shard_map.64 = s16[16,160,128]{2,1,0:T(8,128)(2,1)} custom-call(f32[1,2,19,4,512]{4,3,2,1,0:T(4,128)S(1)} %copy-done, f32[1,2,19,4,512]{4,3,2,1,0:T(4,128)S(1)} %copy-done.2, f32[1,4,512]{2,1,0:T(4,128)S(1)} %copy-done.7, s32[4,512]{1,0:T(4,128)S(1)} %copy-done.3, s32[4,512]{1,0:T(4,128)S(1)} %copy-done.5), custom_call_target="tpu_custom_call" | custom-call | tf_op jit(solution)/shard_map/pallas_call | solution.py:459
  5.7 0.0 copy-start.8
  5.7 7.5 %all-to-all-start = ((s16[16,160,128]{2,1,0:T(8,128)(2,1)}), s16[16,160,128]{2,1,0:T(8,128)(2,1)S(1)}, u32[]{:S(2)}, u32[]{:S(2)}) async-start(s16[16,160,128]{2,1,0:T(8,128)(2,1)} %shard_map.64), calls=%async_computation | async-start | bytes 1310720 | tf_op jit(solution)/shard_map/all_to_all | solution.py:484
  13.2 0.0 copy-done.8
  13.2 0.0 copy-start.1
  13.2 16.6 %all-to-all-done.recv = s16[16,160,128]{2,1,0:T(8,128)(2,1)S(1)} async-done(((s16[16,160,128]{2,1,0:T(8,128)(2,1)}), s16[16,160,128]{2,1,0:T(8,128)(2,1)S(1)}, u32[]{:S(2)}, u32[]{:S(2)}) %all-to-all-start) | async-done | bytes 655392 | tf_op jit(solution)/shard_map/all_to_all | solution.py:484
  29.8 17.5 %shard_map.65 = (s16[160,128]{1,0:T(8,128)(2,1)S(1)}, s16[160,128]{1,0:T(8,128)(2,1)S(1)}, s16[160,128]{1,0:T(8,128)(2,1)S(1)}, s16[160,128]{1,0:T(8,128)(2,1)S(1)}) custom-call(s16[16,160,128]{2,1,0:T(8,128)(2,1)S(1)} %all-to-all-done.recv, bf16[2,76,76]{2,1,0:T(8,128)(2,1)S(1)} %copy.7.ops), custom_call_target="tpu_custom_call" | custom-call | tf_op jit(solution)/shard_map/pallas_call | solution.py:459
  47.3 0.1 collective-permute-start
  47.4 1.4 %collective-permute-start.1 = (s16[160,128]{1,0:T(8,128)(2,1)S(1)}, s16[160,128]{1,0:T(8,128)(2,1)S(1)}, u32[]{:S(2)}, u32[]{:S(2)}) collective-permute-start(s16[160,128]{1,0:T(8,128)(2,1)S(1)} %get-tuple-element.15), channel_id=1, source_target_pairs={{0,2},{1,3},{2,0},{3,1},{4,6},{5,7},{6,4},{7,5},{8,10},{9,11},{10,... | collective-permute-start | bytes 122888 | tf_op jit(solution)/shard_map/ppermute | solution.py:502
  48.8 0.4 collective-permute-start.2
  49.2 0.0 collective-permute-done.in1
  49.2 2.2 %collective-permute-done.1.in2 = s16[160,128]{1,0:T(8,128)(2,1)S(1)} collective-permute-done((s16[160,128]{1,0:T(8,128)(2,1)S(1)}, s16[160,128]{1,0:T(8,128)(2,1)S(1)}, u32[]{:S(2)}, u32[]{:S(2)}) %collective-permute-start.1) | collective-permute-done | bytes 40992 | tf_op jit(solution)/shard_map/ppermute | solution.py:502
  51.4 1.3 %collective-permute-done.2.in3 = s16[160,128]{1,0:T(8,128)(2,1)S(1)} collective-permute-done((s16[160,128]{1,0:T(8,128)(2,1)S(1)}, s16[160,128]{1,0:T(8,128)(2,1)S(1)}, u32[]{:S(2)}, u32[]{:S(2)}) %collective-permute-start.2) | collective-permute-done | bytes 40992 | tf_op jit(solution)/shard_map/ppermute | solution.py:502
  52.7 0.0 copy-start.4
  52.7 0.0 copy-start.6
  52.7 0.4 shard_map.66
  53.1 1.6 %collective-permute-start.3 = (s16[160,128]{1,0:T(8,128)(2,1)S(1)}, s16[160,128]{1,0:T(8,128)(2,1)S(1)}, u32[]{:S(2)}, u32[]{:S(2)}) collective-permute-start(s16[160,128]{1,0:T(8,128)(2,1)S(1)} %get-tuple-element.17), channel_id=1, source_target_pairs={{0,16},{4,20},{8,24},{12,28},{16,0},{20,4},{24,8},{28,12},{1,17},{... | collective-permute-start | bytes 122888 | tf_op jit(solution)/shard_map/ppermute | solution.py:507
  54.6 1.7 %collective-permute-start.4 = (s16[160,128]{1,0:T(8,128)(2,1)S(1)}, s16[160,128]{1,0:T(8,128)(2,1)S(1)}, u32[]{:S(2)}, u32[]{:S(2)}) collective-permute-start(s16[160,128]{1,0:T(8,128)(2,1)S(1)} %get-tuple-element.18), channel_id=1, source_target_pairs={{0,20},{4,24},{8,28},{12,16},{16,4},{20,8},{24,12},{28,0},{1,21},{... | collective-permute-start | bytes 122888 | tf_op jit(solution)/shard_map/ppermute | solution.py:507
  56.4 2.4 %collective-permute-start.5 = (s16[160,128]{1,0:T(8,128)(2,1)S(1)}, s16[160,128]{1,0:T(8,128)(2,1)S(1)}, u32[]{:S(2)}, u32[]{:S(2)}) collective-permute-start(s16[160,128]{1,0:T(8,128)(2,1)S(1)} %get-tuple-element.19), channel_id=1, source_target_pairs={{0,24},{4,28},{8,16},{12,20},{16,8},{20,12},{24,0},{28,4},{1,25},{... | collective-permute-start | bytes 122888 | tf_op jit(solution)/shard_map/ppermute | solution.py:507
  58.7 1.7 %collective-permute-start.6 = (s16[160,128]{1,0:T(8,128)(2,1)S(1)}, s16[160,128]{1,0:T(8,128)(2,1)S(1)}, u32[]{:S(2)}, u32[]{:S(2)}) collective-permute-start(s16[160,128]{1,0:T(8,128)(2,1)S(1)} %get-tuple-element.20), channel_id=1, source_target_pairs={{0,28},{4,16},{8,20},{12,24},{16,12},{20,0},{24,4},{28,8},{1,29},{... | collective-permute-start | bytes 122888 | tf_op jit(solution)/shard_map/ppermute | solution.py:507
  60.4 0.0 collective-permute-done.3.in0
  60.4 1.2 %collective-permute-done.4.in1 = s16[160,128]{1,0:T(8,128)(2,1)S(1)} collective-permute-done((s16[160,128]{1,0:T(8,128)(2,1)S(1)}, s16[160,128]{1,0:T(8,128)(2,1)S(1)}, u32[]{:S(2)}, u32[]{:S(2)}) %collective-permute-start.4) | collective-permute-done | bytes 40992 | tf_op jit(solution)/shard_map/ppermute | solution.py:507
  61.6 1.2 %collective-permute-done.5.in2 = s16[160,128]{1,0:T(8,128)(2,1)S(1)} collective-permute-done((s16[160,128]{1,0:T(8,128)(2,1)S(1)}, s16[160,128]{1,0:T(8,128)(2,1)S(1)}, u32[]{:S(2)}, u32[]{:S(2)}) %collective-permute-start.5) | collective-permute-done | bytes 40992 | tf_op jit(solution)/shard_map/ppermute | solution.py:507
  62.8 0.8 %collective-permute-done.6.in3 = s16[160,128]{1,0:T(8,128)(2,1)S(1)} collective-permute-done((s16[160,128]{1,0:T(8,128)(2,1)S(1)}, s16[160,128]{1,0:T(8,128)(2,1)S(1)}, u32[]{:S(2)}, u32[]{:S(2)}) %collective-permute-start.6) | collective-permute-done | bytes 40992 | tf_op jit(solution)/shard_map/ppermute | solution.py:507
  63.6 0.0 copy-done.1
  63.6 0.0 copy-done.4
  63.6 0.0 copy-done.6
  63.7 0.9 %shard_map.67 = f32[1,2,19,4,512]{4,3,2,1,0:T(4,128)} custom-call(s16[160,128]{1,0:T(8,128)(2,1)S(1)} %collective-permute-done.3.in0, s16[160,128]{1,0:T(8,128)(2,1)S(1)} %collective-permute-done.4.in1, s16[160,128]{1,0:T(8,128)(2,1)S(1)} %collective-permute-done.5.in2, s16[160,128]{1,0:T(8,128)(2,1)S(1)} %collective-permute-done.6.in3, ...), custom_call_target="tpu_custom_call" | custom-call | tf_op jit(solution)/shard_map/pallas_call | solution.py:459
  (1 shorter events, 0.0 us)
Async XLA Ops:
  0.0 1.0 %copy-start = (f32[1,2,19,4,512]{4,3,2,1,0:T(4,128)S(1)}, f32[1,2,19,4,512]{4,3,2,1,0:T(4,128)}, u32[]{:S(2)}) copy-start(f32[1,2,19,4,512]{4,3,2,1,0:T(4,128)} %state.3) | copy-start | bytes 933892
  1.0 1.0 %copy-start.2 = (f32[1,2,19,4,512]{4,3,2,1,0:T(4,128)S(1)}, f32[1,2,19,4,512]{4,3,2,1,0:T(4,128)}, u32[]{:S(2)}) copy-start(f32[1,2,19,4,512]{4,3,2,1,0:T(4,128)} %velocity.1) | copy-start | bytes 933892
  1.9 0.7 %copy-start.3 = (s32[4,512]{1,0:T(4,128)S(1)}, s32[4,512]{1,0:T(4,128)}, u32[]{:S(2)}) copy-start(s32[4,512]{1,0:T(4,128)} %land_sea.3) | copy-start | bytes 24580
  2.6 0.7 %copy-start.5 = (s32[4,512]{1,0:T(4,128)S(1)}, s32[4,512]{1,0:T(4,128)}, u32[]{:S(2)}) copy-start(s32[4,512]{1,0:T(4,128)} %depth_index.3) | copy-start | bytes 24580
  3.3 0.7 %copy-start.7 = (f32[1,4,512]{2,1,0:T(4,128)S(1)}, f32[1,4,512]{2,1,0:T(4,128)}, u32[]{:S(2)}) copy-start(f32[1,4,512]{2,1,0:T(4,128)} %growth.1) | copy-start | bytes 24580
  5.7 7.5 %copy-start.8 = (bf16[2,76,76]{2,0,1:T(2,128)(2,1)S(1)}, bf16[2,76,76]{2,0,1:T(2,128)(2,1)}, u32[]{:S(2)}) copy-start(bf16[2,76,76]{2,0,1:T(2,128)(2,1)} %param.11) | copy-start | bytes 69316
  5.7 24.1 %all-to-all-start = ((s16[16,160,128]{2,1,0:T(8,128)(2,1)}), s16[16,160,128]{2,1,0:T(8,128)(2,1)S(1)}, u32[]{:S(2)}, u32[]{:S(2)}) async-start(s16[16,160,128]{2,1,0:T(8,128)(2,1)} %shard_map.64), calls=%async_computation | async-start | bytes 1310720 | tf_op jit(solution)/shard_map/all_to_all | solution.py:484
  13.2 50.5 %copy-start.1 = (f32[1,2,19,4,512]{4,3,2,1,0:T(4,128)S(1)}, f32[1,2,19,4,512]{4,3,2,1,0:T(4,128)}, u32[]{:S(2)}) copy-start(f32[1,2,19,4,512]{4,3,2,1,0:T(4,128)} %state.3) | copy-start | bytes 933892
  47.3 1.9 %collective-permute-start = (s16[160,128]{1,0:T(8,128)(2,1)S(1)}, s16[160,128]{1,0:T(8,128)(2,1)S(1)}, u32[]{:S(2)}, u32[]{:S(2)}) collective-permute-start(s16[160,128]{1,0:T(8,128)(2,1)S(1)} %get-tuple-element.14), channel_id=1, source_target_pairs={{0,1},{1,0},{2,3},{3,2},{4,5},{5,4},{6,7},{7,6},{8,9},{9,8},{10,11... | collective-permute-start | bytes 122888 | tf_op jit(solution)/shard_map/ppermute | solution.py:502
  47.4 4.0 %collective-permute-start.1 = (s16[160,128]{1,0:T(8,128)(2,1)S(1)}, s16[160,128]{1,0:T(8,128)(2,1)S(1)}, u32[]{:S(2)}, u32[]{:S(2)}) collective-permute-start(s16[160,128]{1,0:T(8,128)(2,1)S(1)} %get-tuple-element.15), channel_id=1, source_target_pairs={{0,2},{1,3},{2,0},{3,1},{4,6},{5,7},{6,4},{7,5},{8,10},{9,11},{10,... | collective-permute-start | bytes 122888 | tf_op jit(solution)/shard_map/ppermute | solution.py:502
  48.8 3.8 %collective-permute-start.2 = (s16[160,128]{1,0:T(8,128)(2,1)S(1)}, s16[160,128]{1,0:T(8,128)(2,1)S(1)}, u32[]{:S(2)}, u32[]{:S(2)}) collective-permute-start(s16[160,128]{1,0:T(8,128)(2,1)S(1)} %get-tuple-element.16), channel_id=1, source_target_pairs={{0,3},{1,2},{2,1},{3,0},{4,7},{5,6},{6,5},{7,4},{8,11},{9,10},{10,... | collective-permute-start | bytes 122888 | tf_op jit(solution)/shard_map/ppermute | solution.py:502
  52.7 11.0 %copy-start.4 = (s32[4,512]{1,0:T(4,128)S(1)}, s32[4,512]{1,0:T(4,128)}, u32[]{:S(2)}) copy-start(s32[4,512]{1,0:T(4,128)} %land_sea.3) | copy-start | bytes 24580
  52.7 11.0 %copy-start.6 = (s32[4,512]{1,0:T(4,128)S(1)}, s32[4,512]{1,0:T(4,128)}, u32[]{:S(2)}) copy-start(s32[4,512]{1,0:T(4,128)} %depth_index.3) | copy-start | bytes 24580
  53.1 7.4 %collective-permute-start.3 = (s16[160,128]{1,0:T(8,128)(2,1)S(1)}, s16[160,128]{1,0:T(8,128)(2,1)S(1)}, u32[]{:S(2)}, u32[]{:S(2)}) collective-permute-start(s16[160,128]{1,0:T(8,128)(2,1)S(1)} %get-tuple-element.17), channel_id=1, source_target_pairs={{0,16},{4,20},{8,24},{12,28},{16,0},{20,4},{24,8},{28,12},{1,17},{... | collective-permute-start | bytes 122888 | tf_op jit(solution)/shard_map/ppermute | solution.py:507
  54.6 7.0 %collective-permute-start.4 = (s16[160,128]{1,0:T(8,128)(2,1)S(1)}, s16[160,128]{1,0:T(8,128)(2,1)S(1)}, u32[]{:S(2)}, u32[]{:S(2)}) collective-permute-start(s16[160,128]{1,0:T(8,128)(2,1)S(1)} %get-tuple-element.18), channel_id=1, source_target_pairs={{0,20},{4,24},{8,28},{12,16},{16,4},{20,8},{24,12},{28,0},{1,21},{... | collective-permute-start | bytes 122888 | tf_op jit(solution)/shard_map/ppermute | solution.py:507
  56.4 6.4 %collective-permute-start.5 = (s16[160,128]{1,0:T(8,128)(2,1)S(1)}, s16[160,128]{1,0:T(8,128)(2,1)S(1)}, u32[]{:S(2)}, u32[]{:S(2)}) collective-permute-start(s16[160,128]{1,0:T(8,128)(2,1)S(1)} %get-tuple-element.19), channel_id=1, source_target_pairs={{0,24},{4,28},{8,16},{12,20},{16,8},{20,12},{24,0},{28,4},{1,25},{... | collective-permute-start | bytes 122888 | tf_op jit(solution)/shard_map/ppermute | solution.py:507
  58.7 4.9 %collective-permute-start.6 = (s16[160,128]{1,0:T(8,128)(2,1)S(1)}, s16[160,128]{1,0:T(8,128)(2,1)S(1)}, u32[]{:S(2)}, u32[]{:S(2)}) collective-permute-start(s16[160,128]{1,0:T(8,128)(2,1)S(1)} %get-tuple-element.20), channel_id=1, source_target_pairs={{0,28},{4,16},{8,20},{12,24},{16,12},{20,0},{24,4},{28,8},{1,29},{... | collective-permute-start | bytes 122888 | tf_op jit(solution)/shard_map/ppermute | solution.py:507

commit v3 on v2

--- a/solution.py
+++ b/solution.py
@@ -199,7 +199,9 @@
                 out[4 * q + m, 16 * pair : 16 * pair + 16, :] = coded(block)
 
 
-def steps_kernel(recv, ops, out0, out1, out2, out3, cells, moved, flow, coef, plane, light, ends):
+def steps_kernel(
+    recv, ops, out0, out1, out2, out3, cells, firsts, moved, flow, coef, plane, light, ends
+):
     sub = index((8, 128), 0)
     lane = index((8, 128), 1)
     left = lane < 64
@@ -298,37 +300,53 @@
             coef[g, s, 7], coef[g, s, 8] = north
         return carry
 
-    lax.fori_loop(0, PITCH // 8, prepare, 0)
+    lax.fori_loop(0, PITCH // 8, prepare, 0, unroll=5)
 
     deep = index((LEVELS, 128), 0)
     light[...] = jnp.exp(deep.astype(F32) * (-4.0 / LEVELS))
 
-    def stage(x, g):
-        turned = [pltpu.roll(x[s], 64, 1) for s in (6, 7, 0, 1)]
-        column = turned[:2] + x + turned[2:]
-        results = []
+    def combine(c, near, far):
+        centre = near[1]
+        return (
+            (c[0] * centre + c[6] * near[0] + c[7] * near[2])
+            + (c[5] * far[0] + c[8] * far[1])
+            + (c[2] * pltpu.roll(centre, 1, 1) + c[3] * pltpu.roll(centre, 127, 1))
+            + (c[1] * pltpu.roll(centre, 2, 1) + c[4] * pltpu.roll(centre, 126, 1))
+        )
+
+    def stage(source, g, emit):
+        def at(t, s):
+            return source[block(8 * t + s, g), :]
+
+        columns = []
+        for t in range(2):
+            inner = [at(t, s) for s in range(8)]
+            turned = [pltpu.roll(inner[s], 64, 1) for s in (6, 7, 0, 1)]
+            columns.append(turned[:2] + inner + turned[2:])
         for s in range(8):
             c = [coef[g, s, i] for i in range(9)]
-            near, far = column[s + 1 : s + 4], (column[s], column[s + 4])
-            centre = near[1]
-            results.append(
-                (c[0] * centre + c[6] * near[0] + c[7] * near[2])
-                + (c[5] * far[0] + c[8] * far[1])
-                + (c[2] * pltpu.roll(centre, 1, 1) + c[3] * pltpu.roll(centre, 127, 1))
-                + (c[1] * pltpu.roll(centre, 2, 1) + c[4] * pltpu.roll(centre, 126, 1))
-            )
-        return results
-
-    def transport(g, carry):
-        for t in range(2):
-            x = [cells[block(8 * t + s, g), :] for s in range(8)]
-            y = stage(stage(x, g), g)
-            for s in range(8):
-                moved[block(8 * t + s, g), :] = 0.5 * (x[s] + y[s])
+            for t in range(2):
+                k = columns[t]
+                emit(t, s, combine(c, k[s + 1 : s + 4], (k[s], k[s + 4])))
+
+    def first_stage(g, carry):
+        def emit(t, s, value):
+            firsts[block(8 * t + s, g), :] = value
+
+        stage(cells, g, emit)
         return carry
 
+    def second_stage(g, carry):
+        def emit(t, s, value):
+            at = block(8 * t + s, g)
+            moved[at, :] = 0.5 * (cells[at, :] + value)
+
+        stage(firsts, g, emit)
+        return carry
+
     def step(n, carry):
-        lax.fori_loop(0, PITCH // 8, transport, 0)
+        lax.fori_loop(0, PITCH // 8, first_stage, 0, unroll=True)
+        lax.fori_loop(0, PITCH // 8, second_stage, 0, unroll=True)
         for pair in range(4):
             mixed = []
             for t in range(2):
@@ -479,6 +497,7 @@
         growth,
         land_sea,
         depth_index,
+        reserve=60,
         place=lambda *args: args,
     )
     received = lax.all_to_all(packed, ("tile", "depth"), 0, 0, tiled=True)
@@ -486,6 +505,7 @@
         steps_kernel,
         [message] * 4,
         [
+            cells,
             cells,
             cells,
             cells,

time: 65 us -> 53.9 us (0.83)
  Pallas kernels: 20.3 us -> 13.5 us
  local copies, waits for them, and re-layouts: 4.05 us -> 0.03 us
    pallas_call x4, Pallas kernels: 20.3 us -> 13.5 us  [call(): pl.pallas_call(kernel, out_shape=outs, in_specs=[VMEM] * len(args), out_s...]
    unnamed x19 -> x9, local copies, waits for them, and re-layouts: 4.05 us -> 0.03 us
where the time goes in v3:
time: 53.9 us; the launch traced here: 53.6 us
  waiting for transfers between devices  23.3 us (43%)
  starting transfers between devices  16.8 us (31%)
  Pallas kernels  13.5 us (25%)
    all_to_all x1, waiting for transfers between devices, window_shards(): received = lax.all_to_all(packed, ('tile', 'depth'), 0, 0, tiled=True)  16.6 us
    pallas_call x4, Pallas kernels, call(): pl.pallas_call(kernel, out_shape=outs, in_specs=[VMEM] * len(args), out_s...  13.5 us
    all_to_all x1, starting transfers between devices, window_shards(): received = lax.all_to_all(packed, ('tile', 'depth'), 0, 0, tiled=True)  7.49 us
    ppermute x4, starting transfers between devices, window_shards(): lax.ppermute(turned[n], ('seg', 'tile'), [(s * TILES + t, (s + 1) % segs...  7.36 us
    ppermute x3, waiting for transfers between devices, window_shards(): lax.ppermute(out[n], 'depth', [(i, i ^ n) for i in range(BLOCKS)])  3.49 us
    ppermute x4, waiting for transfers between devices, window_shards(): lax.ppermute(turned[n], ('seg', 'tile'), [(s * TILES + t, (s + 1) % segs...  3.23 us
    ppermute x3, starting transfers between devices, window_shards(): lax.ppermute(out[n], 'depth', [(i, i ^ n) for i in range(BLOCKS)])  1.94 us
  transfers between devices with their start and end apart: 8, of which 6 were waited for; matrix products, arithmetic and copies ran while one was open for 0% of the time, Pallas kernels for 0%

profile of v3, /device:TPU:0, one launch (start us, length us, event | category | flops | bytes accessed | tf_op | source)
XLA Modules:
  0.0 53.6 jit_solution(14159683035185682252)
XLA Ops:
  0.0 2.7 %shard_map.64 = s16[16,160,128]{2,1,0:T(8,128)(2,1)} custom-call(f32[1,2,19,4,512]{4,3,2,1,0:T(4,128)} %state.3, f32[1,2,19,4,512]{4,3,2,1,0:T(4,128)} %velocity.1, f32[1,4,512]{2,1,0:T(4,128)} %growth.1, s32[4,512]{1,0:T(4,128)} %land_sea.3, s32[4,512]{1,0:T(4,128)} %depth_index.3), custom_call_target="tpu_custom_call" | custom-call | tf_op jit(solution)/shard_map/pallas_call | solution.py:477
  2.7 0.0 copy-start.3
  2.7 7.5 %all-to-all-start = ((s16[16,160,128]{2,1,0:T(8,128)(2,1)}), s16[16,160,128]{2,1,0:T(8,128)(2,1)S(1)}, u32[]{:S(2)}, u32[]{:S(2)}) async-start(s16[16,160,128]{2,1,0:T(8,128)(2,1)} %shard_map.64), calls=%async_computation | async-start | bytes 1310720 | tf_op jit(solution)/shard_map/all_to_all | solution.py:503
  10.2 0.0 copy-done.3
  10.2 0.0 copy-start
  10.2 16.6 %all-to-all-done.recv = s16[16,160,128]{2,1,0:T(8,128)(2,1)S(1)} async-done(((s16[16,160,128]{2,1,0:T(8,128)(2,1)}), s16[16,160,128]{2,1,0:T(8,128)(2,1)S(1)}, u32[]{:S(2)}, u32[]{:S(2)}) %all-to-all-start) | async-done | bytes 655392 | tf_op jit(solution)/shard_map/all_to_all | solution.py:503
  26.8 9.5 %shard_map.65 = (s16[160,128]{1,0:T(8,128)(2,1)S(1)}, s16[160,128]{1,0:T(8,128)(2,1)S(1)}, s16[160,128]{1,0:T(8,128)(2,1)S(1)}, s16[160,128]{1,0:T(8,128)(2,1)S(1)}) custom-call(s16[16,160,128]{2,1,0:T(8,128)(2,1)S(1)} %all-to-all-done.recv, bf16[2,76,76]{2,1,0:T(8,128)(2,1)S(1)} %copy.7.ops), custom_call_target="tpu_custom_call" | custom-call | tf_op jit(solution)/shard_map/pallas_call | solution.py:477
  36.3 0.1 collective-permute-start
  36.5 1.4 %collective-permute-start.1 = (s16[160,128]{1,0:T(8,128)(2,1)S(1)}, s16[160,128]{1,0:T(8,128)(2,1)S(1)}, u32[]{:S(2)}, u32[]{:S(2)}) collective-permute-start(s16[160,128]{1,0:T(8,128)(2,1)S(1)} %get-tuple-element.15), channel_id=1, source_target_pairs={{0,2},{1,3},{2,0},{3,1},{4,6},{5,7},{6,4},{7,5},{8,10},{9,11},{10,... | collective-permute-start | bytes 122888 | tf_op jit(solution)/shard_map/ppermute | solution.py:522
  37.9 0.4 collective-permute-start.2
  38.3 0.0 collective-permute-done.in1
  38.3 2.2 %collective-permute-done.1.in2 = s16[160,128]{1,0:T(8,128)(2,1)S(1)} collective-permute-done((s16[160,128]{1,0:T(8,128)(2,1)S(1)}, s16[160,128]{1,0:T(8,128)(2,1)S(1)}, u32[]{:S(2)}, u32[]{:S(2)}) %collective-permute-start.1) | collective-permute-done | bytes 40992 | tf_op jit(solution)/shard_map/ppermute | solution.py:522
  40.5 1.3 %collective-permute-done.2.in3 = s16[160,128]{1,0:T(8,128)(2,1)S(1)} collective-permute-done((s16[160,128]{1,0:T(8,128)(2,1)S(1)}, s16[160,128]{1,0:T(8,128)(2,1)S(1)}, u32[]{:S(2)}, u32[]{:S(2)}) %collective-permute-start.2) | collective-permute-done | bytes 40992 | tf_op jit(solution)/shard_map/ppermute | solution.py:522
  41.8 0.0 copy-start.1
  41.8 0.0 copy-start.2
  41.8 0.4 shard_map.66
  42.1 1.6 %collective-permute-start.3 = (s16[160,128]{1,0:T(8,128)(2,1)S(1)}, s16[160,128]{1,0:T(8,128)(2,1)S(1)}, u32[]{:S(2)}, u32[]{:S(2)}) collective-permute-start(s16[160,128]{1,0:T(8,128)(2,1)S(1)} %get-tuple-element.17), channel_id=1, source_target_pairs={{0,16},{4,20},{8,24},{12,28},{16,0},{20,4},{24,8},{28,12},{1,17},{... | collective-permute-start | bytes 122888 | tf_op jit(solution)/shard_map/ppermute | solution.py:527
  43.7 1.7 %collective-permute-start.4 = (s16[160,128]{1,0:T(8,128)(2,1)S(1)}, s16[160,128]{1,0:T(8,128)(2,1)S(1)}, u32[]{:S(2)}, u32[]{:S(2)}) collective-permute-start(s16[160,128]{1,0:T(8,128)(2,1)S(1)} %get-tuple-element.18), channel_id=1, source_target_pairs={{0,20},{4,24},{8,28},{12,16},{16,4},{20,8},{24,12},{28,0},{1,21},{... | collective-permute-start | bytes 122888 | tf_op jit(solution)/shard_map/ppermute | solution.py:527
  45.4 2.4 %collective-permute-start.5 = (s16[160,128]{1,0:T(8,128)(2,1)S(1)}, s16[160,128]{1,0:T(8,128)(2,1)S(1)}, u32[]{:S(2)}, u32[]{:S(2)}) collective-permute-start(s16[160,128]{1,0:T(8,128)(2,1)S(1)} %get-tuple-element.19), channel_id=1, source_target_pairs={{0,24},{4,28},{8,16},{12,20},{16,8},{20,12},{24,0},{28,4},{1,25},{... | collective-permute-start | bytes 122888 | tf_op jit(solution)/shard_map/ppermute | solution.py:527
  47.8 1.7 %collective-permute-start.6 = (s16[160,128]{1,0:T(8,128)(2,1)S(1)}, s16[160,128]{1,0:T(8,128)(2,1)S(1)}, u32[]{:S(2)}, u32[]{:S(2)}) collective-permute-start(s16[160,128]{1,0:T(8,128)(2,1)S(1)} %get-tuple-element.20), channel_id=1, source_target_pairs={{0,28},{4,16},{8,20},{12,24},{16,12},{20,0},{24,4},{28,8},{1,29},{... | collective-permute-start | bytes 122888 | tf_op jit(solution)/shard_map/ppermute | solution.py:527
  49.5 0.0 collective-permute-done.3.in0
  49.5 1.2 %collective-permute-done.4.in1 = s16[160,128]{1,0:T(8,128)(2,1)S(1)} collective-permute-done((s16[160,128]{1,0:T(8,128)(2,1)S(1)}, s16[160,128]{1,0:T(8,128)(2,1)S(1)}, u32[]{:S(2)}, u32[]{:S(2)}) %collective-permute-start.4) | collective-permute-done | bytes 40992 | tf_op jit(solution)/shard_map/ppermute | solution.py:527
  50.7 1.2 %collective-permute-done.5.in2 = s16[160,128]{1,0:T(8,128)(2,1)S(1)} collective-permute-done((s16[160,128]{1,0:T(8,128)(2,1)S(1)}, s16[160,128]{1,0:T(8,128)(2,1)S(1)}, u32[]{:S(2)}, u32[]{:S(2)}) %collective-permute-start.5) | collective-permute-done | bytes 40992 | tf_op jit(solution)/shard_map/ppermute | solution.py:527
  51.9 0.8 %collective-permute-done.6.in3 = s16[160,128]{1,0:T(8,128)(2,1)S(1)} collective-permute-done((s16[160,128]{1,0:T(8,128)(2,1)S(1)}, s16[160,128]{1,0:T(8,128)(2,1)S(1)}, u32[]{:S(2)}, u32[]{:S(2)}) %collective-permute-start.6) | collective-permute-done | bytes 40992 | tf_op jit(solution)/shard_map/ppermute | solution.py:527
  52.7 0.0 copy-done
  52.7 0.0 copy-done.1
  52.7 0.0 copy-done.2
  52.7 0.9 %shard_map.67 = f32[1,2,19,4,512]{4,3,2,1,0:T(4,128)} custom-call(s16[160,128]{1,0:T(8,128)(2,1)S(1)} %collective-permute-done.3.in0, s16[160,128]{1,0:T(8,128)(2,1)S(1)} %collective-permute-done.4.in1, s16[160,128]{1,0:T(8,128)(2,1)S(1)} %collective-permute-done.5.in2, s16[160,128]{1,0:T(8,128)(2,1)S(1)} %collective-permute-done.6.in3, ...), custom_call_target="tpu_custom_call" | custom-call | tf_op jit(solution)/shard_map/pallas_call | solution.py:477
  (1 shorter events, 0.0 us)
Async XLA Ops:
  2.7 7.5 %copy-start.3 = (bf16[2,76,76]{2,0,1:T(2,128)(2,1)S(1)}, bf16[2,76,76]{2,0,1:T(2,128)(2,1)}, u32[]{:S(2)}) copy-start(bf16[2,76,76]{2,0,1:T(2,128)(2,1)} %param.11) | copy-start | bytes 69316
  2.7 24.1 %all-to-all-start = ((s16[16,160,128]{2,1,0:T(8,128)(2,1)}), s16[16,160,128]{2,1,0:T(8,128)(2,1)S(1)}, u32[]{:S(2)}, u32[]{:S(2)}) async-start(s16[16,160,128]{2,1,0:T(8,128)(2,1)} %shard_map.64), calls=%async_computation | async-start | bytes 1310720 | tf_op jit(solution)/shard_map/all_to_all | solution.py:503
  10.2 42.5 %copy-start = (f32[1,2,19,4,512]{4,3,2,1,0:T(4,128)S(1)}, f32[1,2,19,4,512]{4,3,2,1,0:T(4,128)}, u32[]{:S(2)}) copy-start(f32[1,2,19,4,512]{4,3,2,1,0:T(4,128)} %state.3) | copy-start | bytes 933892
  36.3 1.9 %collective-permute-start = (s16[160,128]{1,0:T(8,128)(2,1)S(1)}, s16[160,128]{1,0:T(8,128)(2,1)S(1)}, u32[]{:S(2)}, u32[]{:S(2)}) collective-permute-start(s16[160,128]{1,0:T(8,128)(2,1)S(1)} %get-tuple-element.14), channel_id=1, source_target_pairs={{0,1},{1,0},{2,3},{3,2},{4,5},{5,4},{6,7},{7,6},{8,9},{9,8},{10,11... | collective-permute-start | bytes 122888 | tf_op jit(solution)/shard_map/ppermute | solution.py:522
  36.5 4.0 %collective-permute-start.1 = (s16[160,128]{1,0:T(8,128)(2,1)S(1)}, s16[160,128]{1,0:T(8,128)(2,1)S(1)}, u32[]{:S(2)}, u32[]{:S(2)}) collective-permute-start(s16[160,128]{1,0:T(8,128)(2,1)S(1)} %get-tuple-element.15), channel_id=1, source_target_pairs={{0,2},{1,3},{2,0},{3,1},{4,6},{5,7},{6,4},{7,5},{8,10},{9,11},{10,... | collective-permute-start | bytes 122888 | tf_op jit(solution)/shard_map/ppermute | solution.py:522
  37.9 3.8 %collective-permute-start.2 = (s16[160,128]{1,0:T(8,128)(2,1)S(1)}, s16[160,128]{1,0:T(8,128)(2,1)S(1)}, u32[]{:S(2)}, u32[]{:S(2)}) collective-permute-start(s16[160,128]{1,0:T(8,128)(2,1)S(1)} %get-tuple-element.16), channel_id=1, source_target_pairs={{0,3},{1,2},{2,1},{3,0},{4,7},{5,6},{6,5},{7,4},{8,11},{9,10},{10,... | collective-permute-start | bytes 122888 | tf_op jit(solution)/shard_map/ppermute | solution.py:522
  41.8 11.0 %copy-start.1 = (s32[4,512]{1,0:T(4,128)S(1)}, s32[4,512]{1,0:T(4,128)}, u32[]{:S(2)}) copy-start(s32[4,512]{1,0:T(4,128)} %land_sea.3) | copy-start | bytes 24580
  41.8 11.0 %copy-start.2 = (s32[4,512]{1,0:T(4,128)S(1)}, s32[4,512]{1,0:T(4,128)}, u32[]{:S(2)}) copy-start(s32[4,512]{1,0:T(4,128)} %depth_index.3) | copy-start | bytes 24580
  42.1 7.4 %collective-permute-start.3 = (s16[160,128]{1,0:T(8,128)(2,1)S(1)}, s16[160,128]{1,0:T(8,128)(2,1)S(1)}, u32[]{:S(2)}, u32[]{:S(2)}) collective-permute-start(s16[160,128]{1,0:T(8,128)(2,1)S(1)} %get-tuple-element.17), channel_id=1, source_target_pairs={{0,16},{4,20},{8,24},{12,28},{16,0},{20,4},{24,8},{28,12},{1,17},{... | collective-permute-start | bytes 122888 | tf_op jit(solution)/shard_map/ppermute | solution.py:527
  43.7 7.0 %collective-permute-start.4 = (s16[160,128]{1,0:T(8,128)(2,1)S(1)}, s16[160,128]{1,0:T(8,128)(2,1)S(1)}, u32[]{:S(2)}, u32[]{:S(2)}) collective-permute-start(s16[160,128]{1,0:T(8,128)(2,1)S(1)} %get-tuple-element.18), channel_id=1, source_target_pairs={{0,20},{4,24},{8,28},{12,16},{16,4},{20,8},{24,12},{28,0},{1,21},{... | collective-permute-start | bytes 122888 | tf_op jit(solution)/shard_map/ppermute | solution.py:527
  45.4 6.4 %collective-permute-start.5 = (s16[160,128]{1,0:T(8,128)(2,1)S(1)}, s16[160,128]{1,0:T(8,128)(2,1)S(1)}, u32[]{:S(2)}, u32[]{:S(2)}) collective-permute-start(s16[160,128]{1,0:T(8,128)(2,1)S(1)} %get-tuple-element.19), channel_id=1, source_target_pairs={{0,24},{4,28},{8,16},{12,20},{16,8},{20,12},{24,0},{28,4},{1,25},{... | collective-permute-start | bytes 122888 | tf_op jit(solution)/shard_map/ppermute | solution.py:527
  47.8 4.9 %collective-permute-start.6 = (s16[160,128]{1,0:T(8,128)(2,1)S(1)}, s16[160,128]{1,0:T(8,128)(2,1)S(1)}, u32[]{:S(2)}, u32[]{:S(2)}) collective-permute-start(s16[160,128]{1,0:T(8,128)(2,1)S(1)} %get-tuple-element.20), channel_id=1, source_target_pairs={{0,28},{4,16},{8,20},{12,24},{16,12},{20,0},{24,4},{28,8},{1,29},{... | collective-permute-start | bytes 122888 | tf_op jit(solution)/shard_map/ppermute | solution.py:527

commit v4 on v3

--- a/solution.py
+++ b/solution.py
@@ -138,6 +138,9 @@
 FASTEST = 0.35
 FIELDS = 4 * OWN_LEVELS + 4
 ENDS = 2 * OWN_LEVELS + 2
+PIECE = 2 * FIELDS
+MAIN = 4 * FIELDS
+NEAR, FAR = (0, 1, 3), (2,)
 
 F32 = jnp.float32
 I16 = jnp.int16
@@ -156,7 +159,8 @@
     return lax.broadcasted_iota(jnp.int32, shape, dim)
 
 
-def pack_kernel(state, velocity, growth, land_sea, depth_index, out):
+def pack_kernel(state, velocity, growth, land_sea, depth_index, *refs):
+    outs, turned = refs[:-1], refs[-1]
     scales = []
     for t in range(2):
         largest = jnp.abs(state[0, t, 0])
@@ -174,34 +178,88 @@
             return velocity[0, which - 2, k] * (CODE / FASTEST)
         return [growth[0] * CODE, wet_levels, scales[0], scales[1]][k]
 
+    for pair in range(FIELDS // 2):
+        rows = jnp.concatenate([field(2 * pair), field(2 * pair + 1)], axis=0)
+        turned[8 * pair : 8 * pair + 8, :] = pltpu.roll(rows, REACH, 1)
+    tile = lax.axis_index("tile")
+    chunk = index((8, 128), 1) // 32
+
+    def part(row, count, q):
+        lanes = pl.ds(pl.multiple_of(128 * (q % TILES), 128), 128)
+        return turned[row : row + count, lanes]
+
+    for n, out in enumerate(outs):
+        q = tile + n
+        for row in range(0, MAIN, 16):
+            out[row : row + 16, :] = coded(part(row, 16, q))
+        for pair in range(FIELDS // 16):
+            halves = []
+            for group in (2 * pair, 2 * pair + 1):
+                late = group + FIELDS // 8
+                tails = [part(8 * i, 8, q + 1) for i in (2 * late, 2 * group, 2 * late + 1, 2 * group + 1)]
+                tails = [tails[0]] + [pltpu.roll(tails[i], 32 * i, 1) for i in (1, 2, 3)]
+                halves.append(by_chunk(chunk, tails))
+            row = MAIN + 16 * pair
+            out[row : row + 16, :] = coded(jnp.concatenate(halves, axis=0))
+
+
+def by_chunk(chunk, values):
+    return jnp.where(
+        chunk == 0,
+        values[0],
+        jnp.where(chunk == 1, values[1], jnp.where(chunk == 2, values[2], values[3])),
+    )
+
+
+def wide(values):
+    return values.astype(jnp.int32).astype(F32)
+
+
+def narrow(values):
+    return values.astype(jnp.int32).astype(I16)
+
+
+def split_kernel(*refs):
+    count = len(refs) - BLOCKS - 1
+    sources, outs, sent = refs[:count], refs[count:-1], refs[-1]
+    block = lax.axis_index("depth")
     left = index((8, 128), 1) < 64
-    for pair in range(FIELDS // 8):
-        rows = []
-        for group in (2 * pair, 2 * pair + 1):
-            lo, hi = (
-                jnp.concatenate([field(4 * group + 2 * g), field(4 * group + 2 * g + 1)], axis=0)
-                for g in range(2)
-            )
-            quarter = []
-            for m in range(4):
-                a = pltpu.roll(lo, (REACH - OWN * m) % 512, 1)
-                b = pltpu.roll(hi, (REACH - OWN * m + 64) % 512, 1)
-                quarter.append(
-                    [
-                        jnp.where(left, a[:, 128 * q : 128 * q + 128], b[:, 128 * q : 128 * q + 128])
-                        for q in range(4)
-                    ]
-                )
-            rows.append(quarter)
-        for q in range(4):
-            for m in range(4):
-                block = jnp.concatenate([rows[0][m][q], rows[1][m][q]], axis=0)
-                out[4 * q + m, 16 * pair : 16 * pair + 16, :] = coded(block)
-
-
-def steps_kernel(
-    recv, ops, out0, out1, out2, out3, cells, firsts, moved, flow, coef, plane, light, ends
-):
+    chunk = index((8, 128), 1) // 32
+    odd = chunk % 2 == 1
+    for i, ref in enumerate(sources):
+        for pair in range(FIELDS // 8):
+            pieces = [[] for _ in range(BLOCKS)]
+            both = wide(ref[32 * pair : 32 * pair + 16, :]), wide(ref[32 * pair + 16 : 32 * pair + 32, :])
+            late = pair // (FIELDS // 16)
+            row = MAIN + 16 * (pair % (FIELDS // 16))
+            tails = wide(ref[row : row + 16, :])
+            for part in range(2):
+                lo, hi = both[part][0:8], both[part][8:16]
+                tail = tails[8 * part : 8 * part + 8]
+                if late:
+                    tail = pltpu.roll(tail, 32, 1)
+                pieces[0].append(jnp.where(left, lo, pltpu.roll(hi, 64, 1)))
+                pieces[1].append(jnp.where(left, pltpu.roll(lo, 96, 1), pltpu.roll(hi, 32, 1)))
+                pieces[2].append(jnp.where(left, pltpu.roll(lo, 64, 1), hi))
+                last = jnp.where(left, pltpu.roll(lo, 32, 1), pltpu.roll(hi, 96, 1))
+                pieces[3].append(jnp.where(odd, tail, last))
+            row = PIECE * i + 16 * pair
+            for d in range(BLOCKS):
+                sent[d, row : row + 16, :] = narrow(jnp.concatenate(pieces[d], axis=0))
+    for n, out in enumerate(outs):
+        out[...] = sent[block ^ n]
+
+
+def steps_kernel(*refs):
+    arrived, (ops, out0, out1, out2, out3, recv), scratch = refs[:8], refs[8:14], refs[14:]
+    cells, firsts, moved, flow, coef, plane, light, ends = scratch
+    own = lax.axis_index("depth")
+    tile = lax.axis_index("tile")
+    for n in range(BLOCKS):
+        for ref, distances in ((arrived[n], NEAR), (arrived[BLOCKS + n], FAR)):
+            for i, distance in enumerate(distances):
+                source = (tile + TILES - distance) % TILES
+                recv[4 * source + (own ^ n)] = ref[PIECE * i : PIECE * i + PIECE, :]
     sub = index((8, 128), 0)
     lane = index((8, 128), 1)
     left = lane < 64
@@ -372,7 +430,6 @@
 
     lax.fori_loop(0, STEPS, step, 0)
 
-    own = lax.axis_index("depth")
     chunk = lane // 32
 
     def send(n, carry):
@@ -484,14 +541,21 @@
     )(*place(*args))
 
 
+def across_depth(messages):
+    return [messages[0]] + [
+        lax.ppermute(messages[n], "depth", [(i, i ^ n) for i in range(BLOCKS)])
+        for n in range(1, BLOCKS)
+    ]
+
+
 def window_shards(initial_states, velocity, growth, land_sea, depth_index, column_ops):
     message = pltpu.VMEM((4 * ENDS, 128), I16)
     slots = pltpu.VMEM((4, 4 * ENDS, 128), I16)
     cells = pltpu.VMEM((2 * 8 * PITCH, 128), F32)
     packed = call(
         pack_kernel,
-        pltpu.VMEM((TILES * BLOCKS, 2 * FIELDS, 128), I16),
-        [],
+        [pltpu.VMEM((MAIN + FIELDS, 128), I16)] * TILES,
+        [pltpu.VMEM((MAIN, 512), F32)],
         initial_states,
         velocity,
         growth,
@@ -500,11 +564,26 @@
         reserve=60,
         place=lambda *args: args,
     )
-    received = lax.all_to_all(packed, ("tile", "depth"), 0, 0, tiled=True)
+    tiles = {0: packed[0]}
+    for distance in (1, 3, 2):
+        route = [(i, (i + distance) % TILES) for i in range(TILES)]
+        tiles[distance] = lax.ppermute(packed[distance], "tile", route)
+    received = []
+    for distances in (NEAR, FAR):
+        rows = PIECE * len(distances)
+        received += across_depth(
+            call(
+                split_kernel,
+                [pltpu.VMEM((rows, 128), I16)] * BLOCKS,
+                [pltpu.VMEM((BLOCKS, rows, 128), I16)],
+                *[tiles[distance] for distance in distances],
+            )
+        )
     out = call(
         steps_kernel,
         [message] * 4,
         [
+            pltpu.VMEM((TILES * BLOCKS, PIECE, 128), I16),
             cells,
             cells,
             cells,
@@ -514,14 +593,11 @@
             pltpu.VMEM((LEVELS, 128), F32),
             slots,
         ],
-        received,
+        *received,
         column_ops,
         reserve=16,
     )
-    got = [out[0]] + [
-        lax.ppermute(out[n], "depth", [(i, i ^ n) for i in range(BLOCKS)]) for n in range(1, 4)
-    ]
-    turned = call(turn_kernel, [message] * 4, [slots] * 2, *got)
+    turned = call(turn_kernel, [message] * 4, [slots] * 2, *across_depth(out))
     segs = lax.axis_size("seg")
     last = [
         lax.ppermute(

time: 53.9 us -> 49.3 us (0.915)
  waiting for transfers between devices: 23.3 us -> 14.4 us
  starting transfers between devices: 16.8 us -> 21.5 us
    all_to_all x1 -> x0, waiting for transfers between devices: 16.6 us -> none  [window_shards(): received = lax.all_to_all(packed, ('tile', 'depth'), 0, 0, tiled=True)]
    ppermute x3 -> x12, starting transfers between devices: 1.94 us -> 12.8 us  [the longest x9 6.68 us: across_depth(): lax.ppermute(messages[n], 'depth', [(i, i ^ n) for i in range(BLOCKS)])]
    ppermute x3 -> x12, waiting for transfers between devices: 3.49 us -> 11.8 us  [the longest x3 5.99 us: window_shards(): tiles[distance] = lax.ppermute(packed[distance], 'tile', route)]
    all_to_all x1 -> x0, starting transfers between devices: 7.49 us -> none  [window_shards(): received = lax.all_to_all(packed, ('tile', 'depth'), 0, 0, tiled=True)]
    ppermute x4, starting transfers between devices: 7.36 us -> 8.73 us  [window_shards(): lax.ppermute(turned[n], ('seg', 'tile'), [(s * TILES + t, (s + 1) % segs...]
    ppermute x4, waiting for transfers between devices: 3.23 us -> 2.57 us  [window_shards(): lax.ppermute(turned[n], ('seg', 'tile'), [(s * TILES + t, (s + 1) % segs...]
    pallas_call x4 -> x6, Pallas kernels: 13.5 us -> 13.1 us  [call(): pl.pallas_call(kernel, out_shape=outs, in_specs=[VMEM] * len(args), out_s...]
  transfers between devices with their start and end apart: 8 -> 16, of which waited for: 6 -> 9; matrix products, arithmetic and copies ran while one was open for 0% -> 0% of each run, Pallas kernels for 0% -> 1%
where the time goes in v4:
time: 49.3 us; the launch traced here: 49.2 us
  starting transfers between devices  21.5 us (44%)
  waiting for transfers between devices  14.4 us (29%)
  Pallas kernels  13.1 us (27%)
    pallas_call x6, Pallas kernels, call(): pl.pallas_call(kernel, out_shape=outs, in_specs=[VMEM] * len(args), out_s...  13.1 us
    ppermute x4, starting transfers between devices, window_shards(): lax.ppermute(turned[n], ('seg', 'tile'), [(s * TILES + t, (s + 1) % segs...  8.73 us
    ppermute x9, starting transfers between devices, across_depth(): lax.ppermute(messages[n], 'depth', [(i, i ^ n) for i in range(BLOCKS)])  6.68 us
    ppermute x3, starting transfers between devices, window_shards(): tiles[distance] = lax.ppermute(packed[distance], 'tile', route)  6.11 us
    ppermute x3, waiting for transfers between devices, window_shards(): tiles[distance] = lax.ppermute(packed[distance], 'tile', route)  5.99 us
    ppermute x9, waiting for transfers between devices, across_depth(): lax.ppermute(messages[n], 'depth', [(i, i ^ n) for i in range(BLOCKS)])  5.83 us
    ppermute x4, waiting for transfers between devices, window_shards(): lax.ppermute(turned[n], ('seg', 'tile'), [(s * TILES + t, (s + 1) % segs...  2.57 us
  transfers between devices with their start and end apart: 16, of which 9 were waited for; matrix products, arithmetic and copies ran while one was open for 0% of the time, Pallas kernels for 1%

profile of v4, /device:TPU:0, one launch (start us, length us, event | category | flops | bytes accessed | tf_op | source)
XLA Modules:
  0.0 49.2 jit_solution(6617701123067535758)
XLA Ops:
  0.0 1.6 %shard_map.64 = (s16[400,128]{1,0:T(8,128)(2,1)S(1)}, s16[400,128]{1,0:T(8,128)(2,1)S(1)}, s16[400,128]{1,0:T(8,128)(2,1)S(1)}, s16[400,128]{1,0:T(8,128)(2,1)S(1)}) custom-call(f32[1,2,19,4,512]{4,3,2,1,0:T(4,128)} %state.3, f32[1,2,19,4,512]{4,3,2,1,0:T(4,128)} %velocity.1, f32[1,4,512]{2,1,0:T(4,128)} %growth.1, s32[4,512]{1,0:T(4,128)} %land_sea.3, ...), custom_call_target="tpu_custom_call" | custom-call | tf_op jit(solution)/shard_map/pallas_call | solution.py:534
  1.6 3.1 %collective-permute-start = (s16[400,128]{1,0:T(8,128)(2,1)S(1)}, s16[400,128]{1,0:T(8,128)(2,1)S(1)}, u32[]{:S(2)}, u32[]{:S(2)}) collective-permute-start(s16[400,128]{1,0:T(8,128)(2,1)S(1)} %get-tuple-element.26), channel_id=1, source_target_pairs={{0,4},{4,8},{8,12},{12,0},{1,5},{5,9},{9,13},{13,1},{2,6},{6,10},{... | collective-permute-start | bytes 307208 | tf_op jit(solution)/shard_map/ppermute | solution.py:570
  4.6 2.1 %collective-permute-start.1 = (s16[400,128]{1,0:T(8,128)(2,1)S(1)}, s16[400,128]{1,0:T(8,128)(2,1)S(1)}, u32[]{:S(2)}, u32[]{:S(2)}) collective-permute-start(s16[400,128]{1,0:T(8,128)(2,1)S(1)} %get-tuple-element.27), channel_id=1, source_target_pairs={{0,12},{4,0},{8,4},{12,8},{1,13},{5,1},{9,5},{13,9},{2,14},{6,2},{... | collective-permute-start | bytes 307208 | tf_op jit(solution)/shard_map/ppermute | solution.py:570
  6.7 0.9 %collective-permute-start.5 = (s16[400,128]{1,0:T(8,128)(2,1)S(1)}, s16[400,128]{1,0:T(8,128)(2,1)S(1)}, u32[]{:S(2)}, u32[]{:S(2)}) collective-permute-start(s16[400,128]{1,0:T(8,128)(2,1)S(1)} %get-tuple-element.32), channel_id=1, source_target_pairs={{0,8},{4,12},{8,0},{12,4},{1,9},{5,13},{9,1},{13,5},{2,10},{6,14},... | collective-permute-start | bytes 307208 | tf_op jit(solution)/shard_map/ppermute | solution.py:570
  7.7 2.7 %collective-permute-done.refs_1_ = s16[400,128]{1,0:T(8,128)(2,1)S(1)} collective-permute-done((s16[400,128]{1,0:T(8,128)(2,1)S(1)}, s16[400,128]{1,0:T(8,128)(2,1)S(1)}, u32[]{:S(2)}, u32[]{:S(2)}) %collective-permute-start) | collective-permute-done | bytes 102432 | tf_op jit(solution)/shard_map/ppermute | solution.py:570
  10.3 0.8 %collective-permute-done.1.refs_2_ = s16[400,128]{1,0:T(8,128)(2,1)S(1)} collective-permute-done((s16[400,128]{1,0:T(8,128)(2,1)S(1)}, s16[400,128]{1,0:T(8,128)(2,1)S(1)}, u32[]{:S(2)}, u32[]{:S(2)}) %collective-permute-start.1) | collective-permute-done | bytes 102432 | tf_op jit(solution)/shard_map/ppermute | solution.py:570
  11.2 0.5 %shard_map.65 = (s16[480,128]{1,0:T(8,128)(2,1)S(1)}, s16[480,128]{1,0:T(8,128)(2,1)S(1)}, s16[480,128]{1,0:T(8,128)(2,1)S(1)}, s16[480,128]{1,0:T(8,128)(2,1)S(1)}) custom-call(s16[400,128]{1,0:T(8,128)(2,1)S(1)} %get-tuple-element.25.refs_0_, s16[400,128]{1,0:T(8,128)(2,1)S(1)} %collective-permute-done.refs_1_, ...), custom_call_target="tpu_custom_call" | custom-call | tf_op jit(solution)/shard_map/pallas_call | solution.py:534
  11.7 0.1 collective-permute-start.2
  11.8 1.6 %collective-permute-start.3 = (s16[480,128]{1,0:T(8,128)(2,1)S(1)}, s16[480,128]{1,0:T(8,128)(2,1)S(1)}, u32[]{:S(2)}, u32[]{:S(2)}) collective-permute-start(s16[480,128]{1,0:T(8,128)(2,1)S(1)} %get-tuple-element.30), channel_id=1, source_target_pairs={{0,2},{1,3},{2,0},{3,1},{4,6},{5,7},{6,4},{7,5},{8,10},{9,11},{10,... | collective-permute-start | bytes 368648 | tf_op jit(solution)/shard_map/ppermute | solution.py:546
  13.3 0.0 copy-start.3
  13.3 0.3 collective-permute-start.4
  13.6 2.5 %collective-permute-done.5.refs_0_ = s16[400,128]{1,0:T(8,128)(2,1)S(1)} collective-permute-done((s16[400,128]{1,0:T(8,128)(2,1)S(1)}, s16[400,128]{1,0:T(8,128)(2,1)S(1)}, u32[]{:S(2)}, u32[]{:S(2)}) %collective-permute-start.5) | collective-permute-done | bytes 102432 | tf_op jit(solution)/shard_map/ppermute | solution.py:570
  16.1 0.2 shard_map.66
  16.4 0.1 collective-permute-start.6
  16.4 1.6 %collective-permute-start.7 = (s16[160,128]{1,0:T(8,128)(2,1)S(1)}, s16[160,128]{1,0:T(8,128)(2,1)S(1)}, u32[]{:S(2)}, u32[]{:S(2)}) collective-permute-start(s16[160,128]{1,0:T(8,128)(2,1)S(1)} %get-tuple-element.35), channel_id=1, source_target_pairs={{0,2},{1,3},{2,0},{3,1},{4,6},{5,7},{6,4},{7,5},{8,10},{9,11},{10,... | collective-permute-start | bytes 122888 | tf_op jit(solution)/shard_map/ppermute | solution.py:546
  18.0 0.0 collective-permute-done.6.refs_5_
  18.0 0.9 %collective-permute-start.8 = (s16[160,128]{1,0:T(8,128)(2,1)S(1)}, s16[160,128]{1,0:T(8,128)(2,1)S(1)}, u32[]{:S(2)}, u32[]{:S(2)}) collective-permute-start(s16[160,128]{1,0:T(8,128)(2,1)S(1)} %get-tuple-element.36), channel_id=1, source_target_pairs={{0,3},{1,2},{2,1},{3,0},{4,7},{5,6},{6,5},{7,4},{8,11},{9,10},{10,... | collective-permute-start | bytes 122888 | tf_op jit(solution)/shard_map/ppermute | solution.py:546
  18.9 0.0 copy-done.3
  18.9 2.1 %collective-permute-done.7.refs_6_ = s16[160,128]{1,0:T(8,128)(2,1)S(1)} collective-permute-done((s16[160,128]{1,0:T(8,128)(2,1)S(1)}, s16[160,128]{1,0:T(8,128)(2,1)S(1)}, u32[]{:S(2)}, u32[]{:S(2)}) %collective-permute-start.7) | collective-permute-done | bytes 40992 | tf_op jit(solution)/shard_map/ppermute | solution.py:546
  21.0 0.6 %collective-permute-done.8.refs_7_ = s16[160,128]{1,0:T(8,128)(2,1)S(1)} collective-permute-done((s16[160,128]{1,0:T(8,128)(2,1)S(1)}, s16[160,128]{1,0:T(8,128)(2,1)S(1)}, u32[]{:S(2)}, u32[]{:S(2)}) %collective-permute-start.8) | collective-permute-done | bytes 40992 | tf_op jit(solution)/shard_map/ppermute | solution.py:546
  21.6 0.0 collective-permute-done.2.refs_1_
  21.6 0.0 collective-permute-done.3.refs_2_
  21.6 0.0 collective-permute-done.4.refs_3_
  21.6 0.0 copy-start
  21.6 9.6 %shard_map.67 = (s16[160,128]{1,0:T(8,128)(2,1)S(1)}, s16[160,128]{1,0:T(8,128)(2,1)S(1)}, s16[160,128]{1,0:T(8,128)(2,1)S(1)}, s16[160,128]{1,0:T(8,128)(2,1)S(1)}) custom-call(s16[480,128]{1,0:T(8,128)(2,1)S(1)} %get-tuple-element.28.refs_0_, s16[480,128]{1,0:T(8,128)(2,1)S(1)} %collective-permute-done.2.refs_1_, ...), custom_call_target="tpu_custom_call" | custom-call | tf_op jit(solution)/shard_map/pallas_call | solution.py:534
  31.2 1.5 %collective-permute-start.10 = (s16[160,128]{1,0:T(8,128)(2,1)S(1)}, s16[160,128]{1,0:T(8,128)(2,1)S(1)}, u32[]{:S(2)}, u32[]{:S(2)}) collective-permute-start(s16[160,128]{1,0:T(8,128)(2,1)S(1)} %get-tuple-element.39), channel_id=1, source_target_pairs={{0,2},{1,3},{2,0},{3,1},{4,6},{5,7},{6,4},{7,5},{8,10},{9,11},{10,... | collective-permute-start | bytes 122888 | tf_op jit(solution)/shard_map/ppermute | solution.py:546
  32.8 0.0 collective-permute-start.11
  32.8 0.6 %collective-permute-start.9 = (s16[160,128]{1,0:T(8,128)(2,1)S(1)}, s16[160,128]{1,0:T(8,128)(2,1)S(1)}, u32[]{:S(2)}, u32[]{:S(2)}) collective-permute-start(s16[160,128]{1,0:T(8,128)(2,1)S(1)} %get-tuple-element.38), channel_id=1, source_target_pairs={{0,1},{1,0},{2,3},{3,2},{4,5},{5,4},{6,7},{7,6},{8,9},{9,8},{10,11... | collective-permute-start | bytes 122888 | tf_op jit(solution)/shard_map/ppermute | solution.py:546
  33.4 1.9 %collective-permute-done.10.in2 = s16[160,128]{1,0:T(8,128)(2,1)S(1)} collective-permute-done((s16[160,128]{1,0:T(8,128)(2,1)S(1)}, s16[160,128]{1,0:T(8,128)(2,1)S(1)}, u32[]{:S(2)}, u32[]{:S(2)}) %collective-permute-start.10) | collective-permute-done | bytes 40992 | tf_op jit(solution)/shard_map/ppermute | solution.py:546
  35.3 1.3 %collective-permute-done.11.in3 = s16[160,128]{1,0:T(8,128)(2,1)S(1)} collective-permute-done((s16[160,128]{1,0:T(8,128)(2,1)S(1)}, s16[160,128]{1,0:T(8,128)(2,1)S(1)}, u32[]{:S(2)}, u32[]{:S(2)}) %collective-permute-start.11) | collective-permute-done | bytes 40992 | tf_op jit(solution)/shard_map/ppermute | solution.py:546
  36.6 0.0 collective-permute-done.9.in1
  36.6 0.0 copy-start.1
  36.6 0.0 copy-start.2
  36.6 0.4 shard_map.68
  37.0 1.6 %collective-permute-start.12 = (s16[160,128]{1,0:T(8,128)(2,1)S(1)}, s16[160,128]{1,0:T(8,128)(2,1)S(1)}, u32[]{:S(2)}, u32[]{:S(2)}) collective-permute-start(s16[160,128]{1,0:T(8,128)(2,1)S(1)} %get-tuple-element.41), channel_id=1, source_target_pairs={{0,16},{4,20},{8,24},{12,28},{16,0},{20,4},{24,8},{28,12},{1,17},{... | collective-permute-start | bytes 122888 | tf_op jit(solution)/shard_map/ppermute | solution.py:603
  38.5 3.3 %collective-permute-start.13 = (s16[160,128]{1,0:T(8,128)(2,1)S(1)}, s16[160,128]{1,0:T(8,128)(2,1)S(1)}, u32[]{:S(2)}, u32[]{:S(2)}) collective-permute-start(s16[160,128]{1,0:T(8,128)(2,1)S(1)} %get-tuple-element.42), channel_id=1, source_target_pairs={{0,20},{4,24},{8,28},{12,16},{16,4},{20,8},{24,12},{28,0},{1,21},{... | collective-permute-start | bytes 122888 | tf_op jit(solution)/shard_map/ppermute | solution.py:603
  41.9 1.2 %collective-permute-start.14 = (s16[160,128]{1,0:T(8,128)(2,1)S(1)}, s16[160,128]{1,0:T(8,128)(2,1)S(1)}, u32[]{:S(2)}, u32[]{:S(2)}) collective-permute-start(s16[160,128]{1,0:T(8,128)(2,1)S(1)} %get-tuple-element.43), channel_id=1, source_target_pairs={{0,24},{4,28},{8,16},{12,20},{16,8},{20,12},{24,0},{28,4},{1,25},{... | collective-permute-start | bytes 122888 | tf_op jit(solution)/shard_map/ppermute | solution.py:603
  43.0 2.7 %collective-permute-start.15 = (s16[160,128]{1,0:T(8,128)(2,1)S(1)}, s16[160,128]{1,0:T(8,128)(2,1)S(1)}, u32[]{:S(2)}, u32[]{:S(2)}) collective-permute-start(s16[160,128]{1,0:T(8,128)(2,1)S(1)} %get-tuple-element.44), channel_id=1, source_target_pairs={{0,28},{4,16},{8,20},{12,24},{16,12},{20,0},{24,4},{28,8},{1,29},{... | collective-permute-start | bytes 122888 | tf_op jit(solution)/shard_map/ppermute | solution.py:603
  45.7 0.0 collective-permute-done.12.in0
  45.7 0.0 collective-permute-done.13.in1
  45.7 2.5 %collective-permute-done.14.in2 = s16[160,128]{1,0:T(8,128)(2,1)S(1)} collective-permute-done((s16[160,128]{1,0:T(8,128)(2,1)S(1)}, s16[160,128]{1,0:T(8,128)(2,1)S(1)}, u32[]{:S(2)}, u32[]{:S(2)}) %collective-permute-start.14) | collective-permute-done | bytes 40992 | tf_op jit(solution)/shard_map/ppermute | solution.py:603
  48.2 0.1 collective-permute-done.15.in3
  48.3 0.0 copy-done
  48.3 0.0 copy-done.1
  48.3 0.0 copy-done.2
  48.3 0.9 %shard_map.69 = f32[1,2,19,4,512]{4,3,2,1,0:T(4,128)} custom-call(s16[160,128]{1,0:T(8,128)(2,1)S(1)} %collective-permute-done.12.in0, s16[160,128]{1,0:T(8,128)(2,1)S(1)} %collective-permute-done.13.in1, s16[160,128]{1,0:T(8,128)(2,1)S(1)} %collective-permute-done.14.in2, s16[160,128]{1,0:T(8,128)(2,1)S(1)} %collective-permute-done.15.in3, ...), custom_call_target="tpu_custom_call" | custom-call | tf_op jit(solution)/shard_map/pallas_call | solution.py:534
  (1 shorter events, 0.0 us)
Async XLA Ops:
  1.6 8.8 %collective-permute-start = (s16[400,128]{1,0:T(8,128)(2,1)S(1)}, s16[400,128]{1,0:T(8,128)(2,1)S(1)}, u32[]{:S(2)}, u32[]{:S(2)}) collective-permute-start(s16[400,128]{1,0:T(8,128)(2,1)S(1)} %get-tuple-element.26), channel_id=1, source_target_pairs={{0,4},{4,8},{8,12},{12,0},{1,5},{5,9},{9,13},{13,1},{2,6},{6,10},{... | collective-permute-start | bytes 307208 | tf_op jit(solution)/shard_map/ppermute | solution.py:570
  4.6 6.5 %collective-permute-start.1 = (s16[400,128]{1,0:T(8,128)(2,1)S(1)}, s16[400,128]{1,0:T(8,128)(2,1)S(1)}, u32[]{:S(2)}, u32[]{:S(2)}) collective-permute-start(s16[400,128]{1,0:T(8,128)(2,1)S(1)} %get-tuple-element.27), channel_id=1, source_target_pairs={{0,12},{4,0},{8,4},{12,8},{1,13},{5,1},{9,5},{13,9},{2,14},{6,2},{... | collective-permute-start | bytes 307208 | tf_op jit(solution)/shard_map/ppermute | solution.py:570
  6.7 9.4 %collective-permute-start.5 = (s16[400,128]{1,0:T(8,128)(2,1)S(1)}, s16[400,128]{1,0:T(8,128)(2,1)S(1)}, u32[]{:S(2)}, u32[]{:S(2)}) collective-permute-start(s16[400,128]{1,0:T(8,128)(2,1)S(1)} %get-tuple-element.32), channel_id=1, source_target_pairs={{0,8},{4,12},{8,0},{12,4},{1,9},{5,13},{9,1},{13,5},{2,10},{6,14},... | collective-permute-start | bytes 307208 | tf_op jit(solution)/shard_map/ppermute | solution.py:570
  11.7 9.9 %collective-permute-start.2 = (s16[480,128]{1,0:T(8,128)(2,1)S(1)}, s16[480,128]{1,0:T(8,128)(2,1)S(1)}, u32[]{:S(2)}, u32[]{:S(2)}) collective-permute-start(s16[480,128]{1,0:T(8,128)(2,1)S(1)} %get-tuple-element.29), channel_id=1, source_target_pairs={{0,1},{1,0},{2,3},{3,2},{4,5},{5,4},{6,7},{7,6},{8,9},{9,8},{10,11... | collective-permute-start | bytes 368648 | tf_op jit(solution)/shard_map/ppermute | solution.py:546
  11.8 9.8 %collective-permute-start.3 = (s16[480,128]{1,0:T(8,128)(2,1)S(1)}, s16[480,128]{1,0:T(8,128)(2,1)S(1)}, u32[]{:S(2)}, u32[]{:S(2)}) collective-permute-start(s16[480,128]{1,0:T(8,128)(2,1)S(1)} %get-tuple-element.30), channel_id=1, source_target_pairs={{0,2},{1,3},{2,0},{3,1},{4,6},{5,7},{6,4},{7,5},{8,10},{9,11},{10,... | collective-permute-start | bytes 368648 | tf_op jit(solution)/shard_map/ppermute | solution.py:546
  13.3 5.6 %copy-start.3 = (bf16[2,76,76]{2,0,1:T(2,128)(2,1)S(1)}, bf16[2,76,76]{2,0,1:T(2,128)(2,1)}, u32[]{:S(2)}) copy-start(bf16[2,76,76]{2,0,1:T(2,128)(2,1)} %param.11) | copy-start | bytes 69316
  13.3 8.3 %collective-permute-start.4 = (s16[480,128]{1,0:T(8,128)(2,1)S(1)}, s16[480,128]{1,0:T(8,128)(2,1)S(1)}, u32[]{:S(2)}, u32[]{:S(2)}) collective-permute-start(s16[480,128]{1,0:T(8,128)(2,1)S(1)} %get-tuple-element.31), channel_id=1, source_target_pairs={{0,3},{1,2},{2,1},{3,0},{4,7},{5,6},{6,5},{7,4},{8,11},{9,10},{10,... | collective-permute-start | bytes 368648 | tf_op jit(solution)/shard_map/ppermute | solution.py:546
  16.4 1.6 %collective-permute-start.6 = (s16[160,128]{1,0:T(8,128)(2,1)S(1)}, s16[160,128]{1,0:T(8,128)(2,1)S(1)}, u32[]{:S(2)}, u32[]{:S(2)}) collective-permute-start(s16[160,128]{1,0:T(8,128)(2,1)S(1)} %get-tuple-element.34), channel_id=1, source_target_pairs={{0,1},{1,0},{2,3},{3,2},{4,5},{5,4},{6,7},{7,6},{8,9},{9,8},{10,11... | collective-permute-start | bytes 122888 | tf_op jit(solution)/shard_map/ppermute | solution.py:546
  16.4 4.6 %collective-permute-start.7 = (s16[160,128]{1,0:T(8,128)(2,1)S(1)}, s16[160,128]{1,0:T(8,128)(2,1)S(1)}, u32[]{:S(2)}, u32[]{:S(2)}) collective-permute-start(s16[160,128]{1,0:T(8,128)(2,1)S(1)} %get-tuple-element.35), channel_id=1, source_target_pairs={{0,2},{1,3},{2,0},{3,1},{4,6},{5,7},{6,4},{7,5},{8,10},{9,11},{10,... | collective-permute-start | bytes 122888 | tf_op jit(solution)/shard_map/ppermute | solution.py:546
  18.0 3.6 %collective-permute-start.8 = (s16[160,128]{1,0:T(8,128)(2,1)S(1)}, s16[160,128]{1,0:T(8,128)(2,1)S(1)}, u32[]{:S(2)}, u32[]{:S(2)}) collective-permute-start(s16[160,128]{1,0:T(8,128)(2,1)S(1)} %get-tuple-element.36), channel_id=1, source_target_pairs={{0,3},{1,2},{2,1},{3,0},{4,7},{5,6},{6,5},{7,4},{8,11},{9,10},{10,... | collective-permute-start | bytes 122888 | tf_op jit(solution)/shard_map/ppermute | solution.py:546
  21.6 26.7 %copy-start = (f32[1,2,19,4,512]{4,3,2,1,0:T(4,128)S(1)}, f32[1,2,19,4,512]{4,3,2,1,0:T(4,128)}, u32[]{:S(2)}) copy-start(f32[1,2,19,4,512]{4,3,2,1,0:T(4,128)} %state.3) | copy-start | bytes 933892
  31.2 4.1 %collective-permute-start.10 = (s16[160,128]{1,0:T(8,128)(2,1)S(1)}, s16[160,128]{1,0:T(8,128)(2,1)S(1)}, u32[]{:S(2)}, u32[]{:S(2)}) collective-permute-start(s16[160,128]{1,0:T(8,128)(2,1)S(1)} %get-tuple-element.39), channel_id=1, source_target_pairs={{0,2},{1,3},{2,0},{3,1},{4,6},{5,7},{6,4},{7,5},{8,10},{9,11},{10,... | collective-permute-start | bytes 122888 | tf_op jit(solution)/shard_map/ppermute | solution.py:546
  32.8 3.8 %collective-permute-start.11 = (s16[160,128]{1,0:T(8,128)(2,1)S(1)}, s16[160,128]{1,0:T(8,128)(2,1)S(1)}, u32[]{:S(2)}, u32[]{:S(2)}) collective-permute-start(s16[160,128]{1,0:T(8,128)(2,1)S(1)} %get-tuple-element.40), channel_id=1, source_target_pairs={{0,3},{1,2},{2,1},{3,0},{4,7},{5,6},{6,5},{7,4},{8,11},{9,10},{10,... | collective-permute-start | bytes 122888 | tf_op jit(solution)/shard_map/ppermute | solution.py:546
  32.8 3.8 %collective-permute-start.9 = (s16[160,128]{1,0:T(8,128)(2,1)S(1)}, s16[160,128]{1,0:T(8,128)(2,1)S(1)}, u32[]{:S(2)}, u32[]{:S(2)}) collective-permute-start(s16[160,128]{1,0:T(8,128)(2,1)S(1)} %get-tuple-element.38), channel_id=1, source_target_pairs={{0,1},{1,0},{2,3},{3,2},{4,5},{5,4},{6,7},{7,6},{8,9},{9,8},{10,11... | collective-permute-start | bytes 122888 | tf_op jit(solution)/shard_map/ppermute | solution.py:546
  36.6 11.7 %copy-start.1 = (s32[4,512]{1,0:T(4,128)S(1)}, s32[4,512]{1,0:T(4,128)}, u32[]{:S(2)}) copy-start(s32[4,512]{1,0:T(4,128)} %land_sea.3) | copy-start | bytes 24580
  36.6 11.7 %copy-start.2 = (s32[4,512]{1,0:T(4,128)S(1)}, s32[4,512]{1,0:T(4,128)}, u32[]{:S(2)}) copy-start(s32[4,512]{1,0:T(4,128)} %depth_index.3) | copy-start | bytes 24580
  37.0 8.7 %collective-permute-start.12 = (s16[160,128]{1,0:T(8,128)(2,1)S(1)}, s16[160,128]{1,0:T(8,128)(2,1)S(1)}, u32[]{:S(2)}, u32[]{:S(2)}) collective-permute-start(s16[160,128]{1,0:T(8,128)(2,1)S(1)} %get-tuple-element.41), channel_id=1, source_target_pairs={{0,16},{4,20},{8,24},{12,28},{16,0},{20,4},{24,8},{28,12},{1,17},{... | collective-permute-start | bytes 122888 | tf_op jit(solution)/shard_map/ppermute | solution.py:603
  38.5 7.2 %collective-permute-start.13 = (s16[160,128]{1,0:T(8,128)(2,1)S(1)}, s16[160,128]{1,0:T(8,128)(2,1)S(1)}, u32[]{:S(2)}, u32[]{:S(2)}) collective-permute-start(s16[160,128]{1,0:T(8,128)(2,1)S(1)} %get-tuple-element.42), channel_id=1, source_target_pairs={{0,20},{4,24},{8,28},{12,16},{16,4},{20,8},{24,12},{28,0},{1,21},{... | collective-permute-start | bytes 122888 | tf_op jit(solution)/shard_map/ppermute | solution.py:603
  41.9 6.3 %collective-permute-start.14 = (s16[160,128]{1,0:T(8,128)(2,1)S(1)}, s16[160,128]{1,0:T(8,128)(2,1)S(1)}, u32[]{:S(2)}, u32[]{:S(2)}) collective-permute-start(s16[160,128]{1,0:T(8,128)(2,1)S(1)} %get-tuple-element.43), channel_id=1, source_target_pairs={{0,24},{4,28},{8,16},{12,20},{16,8},{20,12},{24,0},{28,4},{1,25},{... | collective-permute-start | bytes 122888 | tf_op jit(solution)/shard_map/ppermute | solution.py:603
  43.0 5.2 %collective-permute-start.15 = (s16[160,128]{1,0:T(8,128)(2,1)S(1)}, s16[160,128]{1,0:T(8,128)(2,1)S(1)}, u32[]{:S(2)}, u32[]{:S(2)}) collective-permute-start(s16[160,128]{1,0:T(8,128)(2,1)S(1)} %get-tuple-element.44), channel_id=1, source_target_pairs={{0,28},{4,16},{8,20},{12,24},{16,12},{20,0},{24,4},{28,8},{1,29},{... | collective-permute-start | bytes 122888 | tf_op jit(solution)/shard_map/ppermute | solution.py:603

commit v5 on v3

--- a/solution.py
+++ b/solution.py
@@ -138,6 +138,10 @@
 FASTEST = 0.35
 FIELDS = 4 * OWN_LEVELS + 4
 ENDS = 2 * OWN_LEVELS + 2
+PIECE = 2 * FIELDS
+MAIN = 4 * FIELDS
+BOTH = PIECE + FIELDS
+CORES = 2
 
 F32 = jnp.float32
 I16 = jnp.int16
@@ -156,7 +160,8 @@
     return lax.broadcasted_iota(jnp.int32, shape, dim)
 
 
-def pack_kernel(state, velocity, growth, land_sea, depth_index, out):
+def pack_kernel(state, velocity, growth, land_sea, depth_index, *refs):
+    (out, *outs), (turned, sent) = refs[:-2], refs[-2:]
     scales = []
     for t in range(2):
         largest = jnp.abs(state[0, t, 0])
@@ -174,34 +179,130 @@
             return velocity[0, which - 2, k] * (CODE / FASTEST)
         return [growth[0] * CODE, wet_levels, scales[0], scales[1]][k]
 
+    for pair in range(FIELDS // 2):
+        rows = jnp.concatenate([field(2 * pair), field(2 * pair + 1)], axis=0)
+        turned[8 * pair : 8 * pair + 8, :] = pltpu.roll(rows, REACH, 1)
+    half = lax.axis_index("depth") // CORES
+
+    def part_of(side):
+        def part(lanes, row, count):
+            at = pl.ds(pl.multiple_of(128 * ((2 * side + lanes) % 4), 128), 128)
+            return turned[row : row + count, at]
+
+        return part
+
+    other = part_of(1 - half)
+    for lanes in range(2):
+        for row in range(0, MAIN, 16):
+            out[MAIN * lanes + row : MAIN * lanes + row + 16, :] = coded(other(lanes, row, 16))
+    for pair in range(FIELDS // 16):
+        row = 2 * MAIN + 16 * pair
+        out[row : row + 16, :] = coded(tails(other, TILES - 1, pair))
+    windows(part_of(half), coded, None, sent, outs)
+
+
+def tails(part, t, pair):
+    chunk = index((8, 128), 1) // 32
+    lanes, first = (t + 1) // 2, 2 * ((t + 1) % 2)
+    blocks = []
+    for group in (2 * pair, 2 * pair + 1):
+        late = group + FIELDS // 8
+        rows = (2 * late, 2 * group, 2 * late + 1, 2 * group + 1)
+        blocks.append(
+            by_chunk(chunk, [turn(part(lanes, 8 * i, 8), n - first) for n, i in enumerate(rows)])
+        )
+    return jnp.concatenate(blocks, axis=0)
+
+
+def turn(block, chunks):
+    return pltpu.roll(block, (32 * chunks) % 128, 1) if chunks % 4 else block
+
+
+def windows(part, packed, last, sent, outs):
     left = index((8, 128), 1) < 64
-    for pair in range(FIELDS // 8):
-        rows = []
-        for group in (2 * pair, 2 * pair + 1):
-            lo, hi = (
-                jnp.concatenate([field(4 * group + 2 * g), field(4 * group + 2 * g + 1)], axis=0)
-                for g in range(2)
-            )
-            quarter = []
-            for m in range(4):
-                a = pltpu.roll(lo, (REACH - OWN * m) % 512, 1)
-                b = pltpu.roll(hi, (REACH - OWN * m + 64) % 512, 1)
-                quarter.append(
-                    [
-                        jnp.where(left, a[:, 128 * q : 128 * q + 128], b[:, 128 * q : 128 * q + 128])
-                        for q in range(4)
-                    ]
-                )
-            rows.append(quarter)
-        for q in range(4):
-            for m in range(4):
-                block = jnp.concatenate([rows[0][m][q], rows[1][m][q]], axis=0)
-                out[4 * q + m, 16 * pair : 16 * pair + 16, :] = coded(block)
-
-
-def steps_kernel(
-    recv, ops, out0, out1, out2, out3, cells, firsts, moved, flow, coef, plane, light, ends
-):
+    for t in range(TILES):
+        for pair in range(FIELDS // 8):
+            blocks = []
+            for group in (2 * pair, 2 * pair + 1):
+                lo, hi = (part(t // 2, 8 * i, 8) for i in (2 * group, 2 * group + 1))
+                lo, hi = turn(lo, 2 * (t % 2)), turn(hi, 2 - 2 * (t % 2))
+                blocks.append(jnp.where(left, lo, hi))
+            sent[t, 16 * pair : 16 * pair + 16, :] = packed(jnp.concatenate(blocks, axis=0))
+        for pair in range(FIELDS // 16):
+            row = PIECE + 16 * pair
+            if t == TILES - 1 and last is not None:
+                sent[t, row : row + 16, :] = last(pair)
+            else:
+                sent[t, row : row + 16, :] = packed(tails(part, t, pair))
+    tile = lax.axis_index("tile")
+    for n, out in enumerate(outs):
+        out[...] = sent[(tile + n) % TILES]
+
+
+def relay_kernel(ref, *refs):
+    outs, sent = refs[:-1], refs[-1]
+
+    def part(lanes, row, count):
+        base = MAIN * lanes + row // 16 * 16
+        skip = row % 16
+        return wide(ref[base : base + 16, :])[skip : skip + count]
+
+    def last(pair):
+        row = 2 * MAIN + 16 * pair
+        return ref[row : row + 16, :]
+
+    windows(part, narrow, last, sent, outs)
+
+
+def piece(ref, pair, core):
+    main = wide(ref[16 * pair : 16 * pair + 16, :])
+    row = PIECE + 16 * (pair % (FIELDS // 16))
+    tail = wide(ref[row : row + 16, :])
+    odd = index((16, 128), 1) // 32 % 2 == 1
+    if pair < FIELDS // 16:
+        second = jnp.where(odd, tail, turn(main, 3))
+    else:
+        second = jnp.where(odd, turn(tail, 1), turn(main, 3))
+    return narrow(jnp.where(core == 0, main, second))
+
+
+def core_kernel(*refs):
+    sources, out = refs[:-1], refs[-1]
+    core = lax.axis_index("depth") % CORES
+    for i, ref in enumerate(sources):
+        for pair in range(FIELDS // 8):
+            row = PIECE * i + 16 * pair
+            out[row : row + 16, :] = piece(ref, pair, 1 - core)
+
+
+def by_chunk(chunk, values):
+    return jnp.where(
+        chunk == 0,
+        values[0],
+        jnp.where(chunk == 1, values[1], jnp.where(chunk == 2, values[2], values[3])),
+    )
+
+
+def wide(values):
+    return values.astype(jnp.int32).astype(F32)
+
+
+def narrow(values):
+    return values.astype(jnp.int32).astype(I16)
+
+
+def steps_kernel(*refs):
+    arrived, (ops, out0, out1, out2, out3, recv), scratch = refs[:9], refs[9:15], refs[15:]
+    cells, firsts, moved, flow, coef, plane, light, ends = scratch
+    own = lax.axis_index("depth")
+    tile = lax.axis_index("tile")
+    core, half = own % CORES, own // CORES
+    for i in range(2 * TILES):
+        far, distance = divmod(i, TILES)
+        at = 4 * ((tile + TILES - distance) % TILES) + CORES * (half ^ far)
+        for pair in range(FIELDS // 8):
+            recv[at + core, 16 * pair : 16 * pair + 16, :] = piece(arrived[i], pair, core)
+        recv[at + 1 - core] = arrived[2 * TILES][PIECE * i : PIECE * i + PIECE, :]
     sub = index((8, 128), 0)
     lane = index((8, 128), 1)
     left = lane < 64
@@ -372,7 +473,6 @@
 
     lax.fori_loop(0, STEPS, step, 0)
 
-    own = lax.axis_index("depth")
     chunk = lane // 32
 
     def send(n, carry):
@@ -453,11 +553,14 @@
         got[(tile + TILES - n) % TILES] = ref[...]
     wet_levels = jnp.where(land_sea[...] == 1, depth_index[...], 0)
     first = block * OWN_LEVELS
+    left = index((16, 128), 1) < 64
     for q in range(4):
+        half, west = divmod(q, 2)
         lanes = slice(128 * q, 128 * q + 128)
         values = []
         for pair in range(ENDS // 4):
-            x = got[q, 16 * pair : 16 * pair + 16, :].astype(jnp.int32).astype(F32)
+            x, y = (wide(got[2 * west + i, 16 * pair : 16 * pair + 16, :]) for i in range(2))
+            x = jnp.where(left, turn(x, 2 * half), turn(y, 2 - 2 * half))
             values += [x[0:4], x[4:8], x[8:12], x[12:16]]
         for t in range(2):
             base = t * (OWN_LEVELS + 1)
@@ -484,14 +587,30 @@
     )(*place(*args))
 
 
+def across_depth(messages):
+    return [messages[0]] + [
+        lax.ppermute(messages[n], "depth", [(i, i ^ n) for i in range(BLOCKS)])
+        for n in range(1, BLOCKS)
+    ]
+
+
+def across_tiles(messages):
+    return [messages[0]] + [
+        lax.ppermute(messages[n], "tile", [(i, (i + n) % TILES) for i in range(TILES)])
+        for n in range(1, TILES)
+    ]
+
+
 def window_shards(initial_states, velocity, growth, land_sea, depth_index, column_ops):
     message = pltpu.VMEM((4 * ENDS, 128), I16)
     slots = pltpu.VMEM((4, 4 * ENDS, 128), I16)
     cells = pltpu.VMEM((2 * 8 * PITCH, 128), F32)
-    packed = call(
+    both = pltpu.VMEM((BOTH, 128), I16)
+    sent = pltpu.VMEM((TILES, BOTH, 128), I16)
+    across, *here = call(
         pack_kernel,
-        pltpu.VMEM((TILES * BLOCKS, 2 * FIELDS, 128), I16),
-        [],
+        [pltpu.VMEM((2 * MAIN + FIELDS, 128), I16)] + [both] * TILES,
+        [pltpu.VMEM((MAIN, 512), F32), sent],
         initial_states,
         velocity,
         growth,
@@ -500,11 +619,16 @@
         reserve=60,
         place=lambda *args: args,
     )
-    received = lax.all_to_all(packed, ("tile", "depth"), 0, 0, tiled=True)
+    across = lax.ppermute(across, "depth", [(i, i ^ CORES) for i in range(BLOCKS)])
+    received = across_tiles(here)
+    received += across_tiles(call(relay_kernel, [both] * TILES, [sent], across))
+    others = call(core_kernel, pltpu.VMEM((2 * TILES * PIECE, 128), I16), [], *received)
+    received.append(lax.ppermute(others, "depth", [(i, i ^ 1) for i in range(BLOCKS)]))
     out = call(
         steps_kernel,
         [message] * 4,
         [
+            pltpu.VMEM((TILES * BLOCKS, PIECE, 128), I16),
             cells,
             cells,
             cells,
@@ -514,14 +638,11 @@
             pltpu.VMEM((LEVELS, 128), F32),
             slots,
         ],
-        received,
+        *received,
         column_ops,
         reserve=16,
     )
-    got = [out[0]] + [
-        lax.ppermute(out[n], "depth", [(i, i ^ n) for i in range(BLOCKS)]) for n in range(1, 4)
-    ]
-    turned = call(turn_kernel, [message] * 4, [slots] * 2, *got)
+    turned = call(turn_kernel, [message] * 4, [slots] * 2, *across_depth(out))
     segs = lax.axis_size("seg")
     last = [
         lax.ppermute(

time: 53.9 us -> 48.5 us (0.90)
  waiting for transfers between devices: 23.3 us -> 12.4 us
  starting transfers between devices: 16.8 us -> 22 us
    all_to_all x1 -> x0, waiting for transfers between devices: 16.6 us -> none  [window_shards(): received = lax.all_to_all(packed, ('tile', 'depth'), 0, 0, tiled=True)]
    ppermute x3 -> x11, starting transfers between devices: 1.94 us -> 15.7 us  [the longest x6 10.4 us: across_tiles(): lax.ppermute(messages[n], 'tile', [(i, (i + n) % TILES) for i in range(TI...]
    all_to_all x1 -> x0, starting transfers between devices: 7.49 us -> none  [window_shards(): received = lax.all_to_all(packed, ('tile', 'depth'), 0, 0, tiled=True)]
    ppermute x3 -> x11, waiting for transfers between devices: 3.49 us -> 7.86 us  [the longest x6 3.37 us: across_tiles(): lax.ppermute(messages[n], 'tile', [(i, (i + n) % TILES) for i in range(TI...]
    ppermute x4, waiting for transfers between devices: 3.23 us -> 4.49 us  [window_shards(): lax.ppermute(turned[n], ('seg', 'tile'), [(s * TILES + t, (s + 1) % segs...]
    ppermute x4, starting transfers between devices: 7.36 us -> 6.31 us  [window_shards(): lax.ppermute(turned[n], ('seg', 'tile'), [(s * TILES + t, (s + 1) % segs...]
    pallas_call x4 -> x6, Pallas kernels: 13.5 us -> 13.5 us  [call(): pl.pallas_call(kernel, out_shape=outs, in_specs=[VMEM] * len(args), out_s...]
  transfers between devices with their start and end apart: 8 -> 15, of which waited for: 6 -> 8; matrix products, arithmetic and copies ran while one was open for 0% -> 0% of each run, Pallas kernels for 0% -> 1%
where the time goes in v5:
time: 48.5 us; the launch traced here: 48.3 us
  starting transfers between devices  22 us (45%)
  Pallas kernels  13.5 us (28%)
  waiting for transfers between devices  12.4 us (26%)
    pallas_call x6, Pallas kernels, call(): pl.pallas_call(kernel, out_shape=outs, in_specs=[VMEM] * len(args), out_s...  13.5 us
    ppermute x6, starting transfers between devices, across_tiles(): lax.ppermute(messages[n], 'tile', [(i, (i + n) % TILES) for i in range(TI...  10.4 us
    ppermute x4, starting transfers between devices, window_shards(): lax.ppermute(turned[n], ('seg', 'tile'), [(s * TILES + t, (s + 1) % segs...  6.31 us
    ppermute x4, waiting for transfers between devices, window_shards(): lax.ppermute(turned[n], ('seg', 'tile'), [(s * TILES + t, (s + 1) % segs...  4.49 us
    ppermute x6, waiting for transfers between devices, across_tiles(): lax.ppermute(messages[n], 'tile', [(i, (i + n) % TILES) for i in range(TI...  3.37 us
    ppermute x3, waiting for transfers between devices, across_depth(): lax.ppermute(messages[n], 'depth', [(i, i ^ n) for i in range(BLOCKS)])  3.25 us
    ppermute x1, starting transfers between devices, window_shards(): lax.ppermute(across, 'depth', [(i, i ^ CORES) for i in range(BLOCKS)])  3 us
    ppermute x3, starting transfers between devices, across_depth(): lax.ppermute(messages[n], 'depth', [(i, i ^ n) for i in range(BLOCKS)])  2.21 us
  transfers between devices with their start and end apart: 15, of which 8 were waited for; matrix products, arithmetic and copies ran while one was open for 0% of the time, Pallas kernels for 1%

profile of v5, /device:TPU:0, one launch (start us, length us, event | category | flops | bytes accessed | tf_op | source)
XLA Modules:
  0.0 48.3 jit_solution(16809416775702918501)
XLA Ops:
  0.0 1.7 %shard_map.64 = (s16[720,128]{1,0:T(8,128)(2,1)S(1)}, s16[240,128]{1,0:T(8,128)(2,1)S(1)}, s16[240,128]{1,0:T(8,128)(2,1)S(1)}, s16[240,128]{1,0:T(8,128)(2,1)S(1)}, s16[240,128]{1,0:T(8,128)(2,1)S(1)}) custom-call(f32[1,2,19,4,512]{4,3,2,1,0:T(4,128)} %state.3, f32[1,2,19,4,512]{4,3,2,1,0:T(4,128)} %velocity.1, f32[1,4,512]{2,1,0:T(4,128)} %growth.1, ...), custom_call_target="tpu_custom_call" | custom-call | tf_op jit(solution)/shard_map/pallas_call | solution.py:580
  1.7 3.0 %collective-permute-start.3 = (s16[720,128]{1,0:T(8,128)(2,1)S(1)}, s16[720,128]{1,0:T(8,128)(2,1)S(1)}, u32[]{:S(2)}, u32[]{:S(2)}) collective-permute-start(s16[720,128]{1,0:T(8,128)(2,1)S(1)} %get-tuple-element.26), channel_id=1, source_target_pairs={{0,2},{1,3},{2,0},{3,1},{4,6},{5,7},{6,4},{7,5},{8,10},{9,11},{10,... | collective-permute-start | bytes 552968 | tf_op jit(solution)/shard_map/ppermute | solution.py:622
  4.7 1.6 %collective-permute-start = (s16[240,128]{1,0:T(8,128)(2,1)S(1)}, s16[240,128]{1,0:T(8,128)(2,1)S(1)}, u32[]{:S(2)}, u32[]{:S(2)}) collective-permute-start(s16[240,128]{1,0:T(8,128)(2,1)S(1)} %get-tuple-element.23), channel_id=1, source_target_pairs={{0,4},{4,8},{8,12},{12,0},{1,5},{5,9},{9,13},{13,1},{2,6},{6,10},{... | collective-permute-start | bytes 184328 | tf_op jit(solution)/shard_map/ppermute | solution.py:599
  6.3 2.6 %collective-permute-start.1 = (s16[240,128]{1,0:T(8,128)(2,1)S(1)}, s16[240,128]{1,0:T(8,128)(2,1)S(1)}, u32[]{:S(2)}, u32[]{:S(2)}) collective-permute-start(s16[240,128]{1,0:T(8,128)(2,1)S(1)} %get-tuple-element.24), channel_id=1, source_target_pairs={{0,8},{4,12},{8,0},{12,4},{1,9},{5,13},{9,1},{13,5},{2,10},{6,14},... | collective-permute-start | bytes 184328 | tf_op jit(solution)/shard_map/ppermute | solution.py:599
  8.9 1.3 %collective-permute-start.2 = (s16[240,128]{1,0:T(8,128)(2,1)S(1)}, s16[240,128]{1,0:T(8,128)(2,1)S(1)}, u32[]{:S(2)}, u32[]{:S(2)}) collective-permute-start(s16[240,128]{1,0:T(8,128)(2,1)S(1)} %get-tuple-element.25), channel_id=1, source_target_pairs={{0,12},{4,0},{8,4},{12,8},{1,13},{5,1},{9,5},{13,9},{2,14},{6,2},{... | collective-permute-start | bytes 184328 | tf_op jit(solution)/shard_map/ppermute | solution.py:599
  10.2 0.0 collective-permute-done.3.ref
  10.2 0.3 shard_map.65
  10.5 1.0 %collective-permute-start.4 = (s16[240,128]{1,0:T(8,128)(2,1)S(1)}, s16[240,128]{1,0:T(8,128)(2,1)S(1)}, u32[]{:S(2)}, u32[]{:S(2)}) collective-permute-start(s16[240,128]{1,0:T(8,128)(2,1)S(1)} %get-tuple-element.28), channel_id=1, source_target_pairs={{0,4},{4,8},{8,12},{12,0},{1,5},{5,9},{9,13},{13,1},{2,6},{6,10},{... | collective-permute-start | bytes 184328 | tf_op jit(solution)/shard_map/ppermute | solution.py:599
  11.5 2.6 %collective-permute-start.5 = (s16[240,128]{1,0:T(8,128)(2,1)S(1)}, s16[240,128]{1,0:T(8,128)(2,1)S(1)}, u32[]{:S(2)}, u32[]{:S(2)}) collective-permute-start(s16[240,128]{1,0:T(8,128)(2,1)S(1)} %get-tuple-element.29), channel_id=1, source_target_pairs={{0,8},{4,12},{8,0},{12,4},{1,9},{5,13},{9,1},{13,5},{2,10},{6,14},... | collective-permute-start | bytes 184328 | tf_op jit(solution)/shard_map/ppermute | solution.py:599
  14.1 0.0 collective-permute-done.refs_1_
  14.1 1.3 %collective-permute-start.6 = (s16[240,128]{1,0:T(8,128)(2,1)S(1)}, s16[240,128]{1,0:T(8,128)(2,1)S(1)}, u32[]{:S(2)}, u32[]{:S(2)}) collective-permute-start(s16[240,128]{1,0:T(8,128)(2,1)S(1)} %get-tuple-element.30), channel_id=1, source_target_pairs={{0,12},{4,0},{8,4},{12,8},{1,13},{5,1},{9,5},{13,9},{2,14},{6,2},{... | collective-permute-start | bytes 184328 | tf_op jit(solution)/shard_map/ppermute | solution.py:599
  15.4 0.0 collective-permute-done.1.refs_2_
  15.4 0.0 collective-permute-done.2.refs_3_
  15.4 1.4 %collective-permute-done.4.refs_5_ = s16[240,128]{1,0:T(8,128)(2,1)S(1)} collective-permute-done((s16[240,128]{1,0:T(8,128)(2,1)S(1)}, s16[240,128]{1,0:T(8,128)(2,1)S(1)}, u32[]{:S(2)}, u32[]{:S(2)}) %collective-permute-start.4) | collective-permute-done | bytes 61472 | tf_op jit(solution)/shard_map/ppermute | solution.py:599
  16.8 1.9 %collective-permute-done.5.refs_6_ = s16[240,128]{1,0:T(8,128)(2,1)S(1)} collective-permute-done((s16[240,128]{1,0:T(8,128)(2,1)S(1)}, s16[240,128]{1,0:T(8,128)(2,1)S(1)}, u32[]{:S(2)}, u32[]{:S(2)}) %collective-permute-start.5) | collective-permute-done | bytes 61472 | tf_op jit(solution)/shard_map/ppermute | solution.py:599
  18.7 0.1 collective-permute-done.6.refs_7_
  18.8 0.0 copy-start.3
  18.8 0.3 shard_map.66
  19.1 0.1 collective-permute-start.7
  19.2 0.4 copy-done.3
  19.6 0.0 copy-start
  19.6 1.2 %collective-permute-done.7.refs_8_ = s16[1280,128]{1,0:T(8,128)(2,1)S(1)} collective-permute-done((s16[1280,128]{1,0:T(8,128)(2,1)S(1)}, s16[1280,128]{1,0:T(8,128)(2,1)S(1)}, u32[]{:S(2)}, u32[]{:S(2)}) %collective-permute-start.7) | collective-permute-done | bytes 327712 | tf_op jit(solution)/shard_map/ppermute | solution.py:626
  20.8 9.9 %shard_map.67 = (s16[160,128]{1,0:T(8,128)(2,1)S(1)}, s16[160,128]{1,0:T(8,128)(2,1)S(1)}, s16[160,128]{1,0:T(8,128)(2,1)S(1)}, s16[160,128]{1,0:T(8,128)(2,1)S(1)}) custom-call(s16[240,128]{1,0:T(8,128)(2,1)S(1)} %get-tuple-element.22.refs_0_, s16[240,128]{1,0:T(8,128)(2,1)S(1)} %collective-permute-done.refs_1_, ...), custom_call_target="tpu_custom_call" | custom-call | tf_op jit(solution)/shard_map/pallas_call | solution.py:580
  30.7 1.1 %collective-permute-start.10 = (s16[160,128]{1,0:T(8,128)(2,1)S(1)}, s16[160,128]{1,0:T(8,128)(2,1)S(1)}, u32[]{:S(2)}, u32[]{:S(2)}) collective-permute-start(s16[160,128]{1,0:T(8,128)(2,1)S(1)} %get-tuple-element.34), channel_id=1, source_target_pairs={{0,3},{1,2},{2,1},{3,0},{4,7},{5,6},{6,5},{7,4},{8,11},{9,10},{10,... | collective-permute-start | bytes 122888 | tf_op jit(solution)/shard_map/ppermute | solution.py:592
  31.8 0.4 collective-permute-start.8
  32.2 0.7 %collective-permute-start.9 = (s16[160,128]{1,0:T(8,128)(2,1)S(1)}, s16[160,128]{1,0:T(8,128)(2,1)S(1)}, u32[]{:S(2)}, u32[]{:S(2)}) collective-permute-start(s16[160,128]{1,0:T(8,128)(2,1)S(1)} %get-tuple-element.33), channel_id=1, source_target_pairs={{0,2},{1,3},{2,0},{3,1},{4,6},{5,7},{6,4},{7,5},{8,10},{9,11},{10,... | collective-permute-start | bytes 122888 | tf_op jit(solution)/shard_map/ppermute | solution.py:592
  32.9 1.4 %collective-permute-done.10.in3 = s16[160,128]{1,0:T(8,128)(2,1)S(1)} collective-permute-done((s16[160,128]{1,0:T(8,128)(2,1)S(1)}, s16[160,128]{1,0:T(8,128)(2,1)S(1)}, u32[]{:S(2)}, u32[]{:S(2)}) %collective-permute-start.10) | collective-permute-done | bytes 40992 | tf_op jit(solution)/shard_map/ppermute | solution.py:592
  34.3 0.0 collective-permute-done.8.in1
  34.3 1.8 %collective-permute-done.9.in2 = s16[160,128]{1,0:T(8,128)(2,1)S(1)} collective-permute-done((s16[160,128]{1,0:T(8,128)(2,1)S(1)}, s16[160,128]{1,0:T(8,128)(2,1)S(1)}, u32[]{:S(2)}, u32[]{:S(2)}) %collective-permute-start.9) | collective-permute-done | bytes 40992 | tf_op jit(solution)/shard_map/ppermute | solution.py:592
  36.2 0.0 copy-start.1
  36.2 0.0 copy-start.2
  36.2 0.4 shard_map.68
  36.6 1.6 %collective-permute-start.11 = (s16[160,128]{1,0:T(8,128)(2,1)S(1)}, s16[160,128]{1,0:T(8,128)(2,1)S(1)}, u32[]{:S(2)}, u32[]{:S(2)}) collective-permute-start(s16[160,128]{1,0:T(8,128)(2,1)S(1)} %get-tuple-element.35), channel_id=1, source_target_pairs={{0,16},{4,20},{8,24},{12,28},{16,0},{20,4},{24,8},{28,12},{1,17},{... | collective-permute-start | bytes 122888 | tf_op jit(solution)/shard_map/ppermute | solution.py:648
  38.1 0.5 %collective-permute-start.12 = (s16[160,128]{1,0:T(8,128)(2,1)S(1)}, s16[160,128]{1,0:T(8,128)(2,1)S(1)}, u32[]{:S(2)}, u32[]{:S(2)}) collective-permute-start(s16[160,128]{1,0:T(8,128)(2,1)S(1)} %get-tuple-element.36), channel_id=1, source_target_pairs={{0,20},{4,24},{8,28},{12,16},{16,4},{20,8},{24,12},{28,0},{1,21},{... | collective-permute-start | bytes 122888 | tf_op jit(solution)/shard_map/ppermute | solution.py:648
  38.7 3.8 %collective-permute-start.13 = (s16[160,128]{1,0:T(8,128)(2,1)S(1)}, s16[160,128]{1,0:T(8,128)(2,1)S(1)}, u32[]{:S(2)}, u32[]{:S(2)}) collective-permute-start(s16[160,128]{1,0:T(8,128)(2,1)S(1)} %get-tuple-element.37), channel_id=1, source_target_pairs={{0,24},{4,28},{8,16},{12,20},{16,8},{20,12},{24,0},{28,4},{1,25},{... | collective-permute-start | bytes 122888 | tf_op jit(solution)/shard_map/ppermute | solution.py:648
  42.5 0.4 collective-permute-start.14
  42.9 0.0 collective-permute-done.11.in0
  42.9 2.1 %collective-permute-done.12.in1 = s16[160,128]{1,0:T(8,128)(2,1)S(1)} collective-permute-done((s16[160,128]{1,0:T(8,128)(2,1)S(1)}, s16[160,128]{1,0:T(8,128)(2,1)S(1)}, u32[]{:S(2)}, u32[]{:S(2)}) %collective-permute-start.12) | collective-permute-done | bytes 40992 | tf_op jit(solution)/shard_map/ppermute | solution.py:648
  45.0 0.0 collective-permute-done.13.in2
  45.0 2.3 %collective-permute-done.14.in3 = s16[160,128]{1,0:T(8,128)(2,1)S(1)} collective-permute-done((s16[160,128]{1,0:T(8,128)(2,1)S(1)}, s16[160,128]{1,0:T(8,128)(2,1)S(1)}, u32[]{:S(2)}, u32[]{:S(2)}) %collective-permute-start.14) | collective-permute-done | bytes 40992 | tf_op jit(solution)/shard_map/ppermute | solution.py:648
  47.4 0.0 copy-done
  47.4 0.0 copy-done.1
  47.4 0.0 copy-done.2
  47.4 1.0 %shard_map.69 = f32[1,2,19,4,512]{4,3,2,1,0:T(4,128)} custom-call(s16[160,128]{1,0:T(8,128)(2,1)S(1)} %collective-permute-done.11.in0, s16[160,128]{1,0:T(8,128)(2,1)S(1)} %collective-permute-done.12.in1, s16[160,128]{1,0:T(8,128)(2,1)S(1)} %collective-permute-done.13.in2, s16[160,128]{1,0:T(8,128)(2,1)S(1)} %collective-permute-done.14.in3, ...), custom_call_target="tpu_custom_call" | custom-call | tf_op jit(solution)/shard_map/pallas_call | solution.py:580
  (1 shorter events, 0.0 us)
Async XLA Ops:
  1.7 8.5 %collective-permute-start.3 = (s16[720,128]{1,0:T(8,128)(2,1)S(1)}, s16[720,128]{1,0:T(8,128)(2,1)S(1)}, u32[]{:S(2)}, u32[]{:S(2)}) collective-permute-start(s16[720,128]{1,0:T(8,128)(2,1)S(1)} %get-tuple-element.26), channel_id=1, source_target_pairs={{0,2},{1,3},{2,0},{3,1},{4,6},{5,7},{6,4},{7,5},{8,10},{9,11},{10,... | collective-permute-start | bytes 552968 | tf_op jit(solution)/shard_map/ppermute | solution.py:622
  4.7 9.4 %collective-permute-start = (s16[240,128]{1,0:T(8,128)(2,1)S(1)}, s16[240,128]{1,0:T(8,128)(2,1)S(1)}, u32[]{:S(2)}, u32[]{:S(2)}) collective-permute-start(s16[240,128]{1,0:T(8,128)(2,1)S(1)} %get-tuple-element.23), channel_id=1, source_target_pairs={{0,4},{4,8},{8,12},{12,0},{1,5},{5,9},{9,13},{13,1},{2,6},{6,10},{... | collective-permute-start | bytes 184328 | tf_op jit(solution)/shard_map/ppermute | solution.py:599
  6.3 9.2 %collective-permute-start.1 = (s16[240,128]{1,0:T(8,128)(2,1)S(1)}, s16[240,128]{1,0:T(8,128)(2,1)S(1)}, u32[]{:S(2)}, u32[]{:S(2)}) collective-permute-start(s16[240,128]{1,0:T(8,128)(2,1)S(1)} %get-tuple-element.24), channel_id=1, source_target_pairs={{0,8},{4,12},{8,0},{12,4},{1,9},{5,13},{9,1},{13,5},{2,10},{6,14},... | collective-permute-start | bytes 184328 | tf_op jit(solution)/shard_map/ppermute | solution.py:599
  8.9 6.6 %collective-permute-start.2 = (s16[240,128]{1,0:T(8,128)(2,1)S(1)}, s16[240,128]{1,0:T(8,128)(2,1)S(1)}, u32[]{:S(2)}, u32[]{:S(2)}) collective-permute-start(s16[240,128]{1,0:T(8,128)(2,1)S(1)} %get-tuple-element.25), channel_id=1, source_target_pairs={{0,12},{4,0},{8,4},{12,8},{1,13},{5,1},{9,5},{13,9},{2,14},{6,2},{... | collective-permute-start | bytes 184328 | tf_op jit(solution)/shard_map/ppermute | solution.py:599
  10.5 6.3 %collective-permute-start.4 = (s16[240,128]{1,0:T(8,128)(2,1)S(1)}, s16[240,128]{1,0:T(8,128)(2,1)S(1)}, u32[]{:S(2)}, u32[]{:S(2)}) collective-permute-start(s16[240,128]{1,0:T(8,128)(2,1)S(1)} %get-tuple-element.28), channel_id=1, source_target_pairs={{0,4},{4,8},{8,12},{12,0},{1,5},{5,9},{9,13},{13,1},{2,6},{6,10},{... | collective-permute-start | bytes 184328 | tf_op jit(solution)/shard_map/ppermute | solution.py:599
  11.5 7.2 %collective-permute-start.5 = (s16[240,128]{1,0:T(8,128)(2,1)S(1)}, s16[240,128]{1,0:T(8,128)(2,1)S(1)}, u32[]{:S(2)}, u32[]{:S(2)}) collective-permute-start(s16[240,128]{1,0:T(8,128)(2,1)S(1)} %get-tuple-element.29), channel_id=1, source_target_pairs={{0,8},{4,12},{8,0},{12,4},{1,9},{5,13},{9,1},{13,5},{2,10},{6,14},... | collective-permute-start | bytes 184328 | tf_op jit(solution)/shard_map/ppermute | solution.py:599
  14.1 4.7 %collective-permute-start.6 = (s16[240,128]{1,0:T(8,128)(2,1)S(1)}, s16[240,128]{1,0:T(8,128)(2,1)S(1)}, u32[]{:S(2)}, u32[]{:S(2)}) collective-permute-start(s16[240,128]{1,0:T(8,128)(2,1)S(1)} %get-tuple-element.30), channel_id=1, source_target_pairs={{0,12},{4,0},{8,4},{12,8},{1,13},{5,1},{9,5},{13,9},{2,14},{6,2},{... | collective-permute-start | bytes 184328 | tf_op jit(solution)/shard_map/ppermute | solution.py:599
  18.8 0.8 %copy-start.3 = (bf16[2,76,76]{2,0,1:T(2,128)(2,1)S(1)}, bf16[2,76,76]{2,0,1:T(2,128)(2,1)}, u32[]{:S(2)}) copy-start(bf16[2,76,76]{2,0,1:T(2,128)(2,1)} %param.11) | copy-start | bytes 69316
  19.1 1.7 %collective-permute-start.7 = (s16[1280,128]{1,0:T(8,128)(2,1)S(1)}, s16[1280,128]{1,0:T(8,128)(2,1)S(1)}, u32[]{:S(2)}, u32[]{:S(2)}) collective-permute-start(s16[1280,128]{1,0:T(8,128)(2,1)S(1)} %shard_map.66), channel_id=1, source_target_pairs={{0,1},{1,0},{2,3},{3,2},{4,5},{5,4},{6,7},{7,6},{8,9},{9,8},{10,11... | collective-permute-start | bytes 983048 | tf_op jit(solution)/shard_map/ppermute | solution.py:626
  19.6 27.8 %copy-start = (f32[1,2,19,4,512]{4,3,2,1,0:T(4,128)S(1)}, f32[1,2,19,4,512]{4,3,2,1,0:T(4,128)}, u32[]{:S(2)}) copy-start(f32[1,2,19,4,512]{4,3,2,1,0:T(4,128)} %state.3) | copy-start | bytes 933892
  30.7 3.6 %collective-permute-start.10 = (s16[160,128]{1,0:T(8,128)(2,1)S(1)}, s16[160,128]{1,0:T(8,128)(2,1)S(1)}, u32[]{:S(2)}, u32[]{:S(2)}) collective-permute-start(s16[160,128]{1,0:T(8,128)(2,1)S(1)} %get-tuple-element.34), channel_id=1, source_target_pairs={{0,3},{1,2},{2,1},{3,0},{4,7},{5,6},{6,5},{7,4},{8,11},{9,10},{10,... | collective-permute-start | bytes 122888 | tf_op jit(solution)/shard_map/ppermute | solution.py:592
  31.8 2.5 %collective-permute-start.8 = (s16[160,128]{1,0:T(8,128)(2,1)S(1)}, s16[160,128]{1,0:T(8,128)(2,1)S(1)}, u32[]{:S(2)}, u32[]{:S(2)}) collective-permute-start(s16[160,128]{1,0:T(8,128)(2,1)S(1)} %get-tuple-element.32), channel_id=1, source_target_pairs={{0,1},{1,0},{2,3},{3,2},{4,5},{5,4},{6,7},{7,6},{8,9},{9,8},{10,11... | collective-permute-start | bytes 122888 | tf_op jit(solution)/shard_map/ppermute | solution.py:592
  32.2 4.0 %collective-permute-start.9 = (s16[160,128]{1,0:T(8,128)(2,1)S(1)}, s16[160,128]{1,0:T(8,128)(2,1)S(1)}, u32[]{:S(2)}, u32[]{:S(2)}) collective-permute-start(s16[160,128]{1,0:T(8,128)(2,1)S(1)} %get-tuple-element.33), channel_id=1, source_target_pairs={{0,2},{1,3},{2,0},{3,1},{4,6},{5,7},{6,4},{7,5},{8,10},{9,11},{10,... | collective-permute-start | bytes 122888 | tf_op jit(solution)/shard_map/ppermute | solution.py:592
  36.2 11.2 %copy-start.1 = (s32[4,512]{1,0:T(4,128)S(1)}, s32[4,512]{1,0:T(4,128)}, u32[]{:S(2)}) copy-start(s32[4,512]{1,0:T(4,128)} %land_sea.3) | copy-start | bytes 24580
  36.2 11.2 %copy-start.2 = (s32[4,512]{1,0:T(4,128)S(1)}, s32[4,512]{1,0:T(4,128)}, u32[]{:S(2)}) copy-start(s32[4,512]{1,0:T(4,128)} %depth_index.3) | copy-start | bytes 24580
  36.6 6.3 %collective-permute-start.11 = (s16[160,128]{1,0:T(8,128)(2,1)S(1)}, s16[160,128]{1,0:T(8,128)(2,1)S(1)}, u32[]{:S(2)}, u32[]{:S(2)}) collective-permute-start(s16[160,128]{1,0:T(8,128)(2,1)S(1)} %get-tuple-element.35), channel_id=1, source_target_pairs={{0,16},{4,20},{8,24},{12,28},{16,0},{20,4},{24,8},{28,12},{1,17},{... | collective-permute-start | bytes 122888 | tf_op jit(solution)/shard_map/ppermute | solution.py:648
  38.1 6.9 %collective-permute-start.12 = (s16[160,128]{1,0:T(8,128)(2,1)S(1)}, s16[160,128]{1,0:T(8,128)(2,1)S(1)}, u32[]{:S(2)}, u32[]{:S(2)}) collective-permute-start(s16[160,128]{1,0:T(8,128)(2,1)S(1)} %get-tuple-element.36), channel_id=1, source_target_pairs={{0,20},{4,24},{8,28},{12,16},{16,4},{20,8},{24,12},{28,0},{1,21},{... | collective-permute-start | bytes 122888 | tf_op jit(solution)/shard_map/ppermute | solution.py:648
  38.7 6.3 %collective-permute-start.13 = (s16[160,128]{1,0:T(8,128)(2,1)S(1)}, s16[160,128]{1,0:T(8,128)(2,1)S(1)}, u32[]{:S(2)}, u32[]{:S(2)}) collective-permute-start(s16[160,128]{1,0:T(8,128)(2,1)S(1)} %get-tuple-element.37), channel_id=1, source_target_pairs={{0,24},{4,28},{8,16},{12,20},{16,8},{20,12},{24,0},{28,4},{1,25},{... | collective-permute-start | bytes 122888 | tf_op jit(solution)/shard_map/ppermute | solution.py:648
  42.5 4.9 %collective-permute-start.14 = (s16[160,128]{1,0:T(8,128)(2,1)S(1)}, s16[160,128]{1,0:T(8,128)(2,1)S(1)}, u32[]{:S(2)}, u32[]{:S(2)}) collective-permute-start(s16[160,128]{1,0:T(8,128)(2,1)S(1)} %get-tuple-element.38), channel_id=1, source_target_pairs={{0,28},{4,16},{8,20},{12,24},{16,12},{20,0},{24,4},{28,8},{1,29},{... | collective-permute-start | bytes 122888 | tf_op jit(solution)/shard_map/ppermute | solution.py:648

commit v6 on v5

--- a/solution.py
+++ b/solution.py
@@ -131,6 +131,7 @@
 LEVELS = 76
 OWN_LEVELS = LEVELS // BLOCKS
 PITCH = 80
+HALF = PITCH // 2
 OWN = 32
 REACH = 4 * STEPS
 WINDOW = OWN + 2 * REACH
@@ -291,30 +292,28 @@
     return values.astype(jnp.int32).astype(I16)
 
 
-def steps_kernel(*refs):
-    arrived, (ops, out0, out1, out2, out3, recv), scratch = refs[:9], refs[9:15], refs[15:]
-    cells, firsts, moved, flow, coef, plane, light, ends = scratch
-    own = lax.axis_index("depth")
-    tile = lax.axis_index("tile")
-    core, half = own % CORES, own // CORES
-    for i in range(2 * TILES):
-        far, distance = divmod(i, TILES)
-        at = 4 * ((tile + TILES - distance) % TILES) + CORES * (half ^ far)
-        for pair in range(FIELDS // 8):
-            recv[at + core, 16 * pair : 16 * pair + 16, :] = piece(arrived[i], pair, core)
-        recv[at + 1 - core] = arrived[2 * TILES][PIECE * i : PIECE * i + PIECE, :]
+def levels_of(row, core):
+    level = row + OWN_LEVELS * core + jnp.where(row >= OWN_LEVELS, OWN_LEVELS, 0)
+    return jnp.where(row < 2 * OWN_LEVELS, level, 4 * LEVELS)
+
+
+def level_rows(shape, core):
+    row = index(shape, 0)
+    return jnp.where(
+        row < HALF, levels_of(row, core), levels_of(row - HALF, 1 - core)
+    )
+
+
+def load_half(recv, side, cells, pitch, base, flow, coef, plane, fresh):
     sub = index((8, 128), 0)
-    lane = index((8, 128), 1)
-    left = lane < 64
-
-    def spread(d, pair):
-        sent = [
-            recv[4 * t + d, 16 * pair : 16 * pair + 16, :].astype(jnp.int32).astype(F32)
-            for t in range(4)
-        ]
+    left = index((8, 128), 1) < 64
+    cells_at, flow_at = (pitch, base), (HALF, 0)
+
+    def spread(x, pair):
+        sent = [wide(recv[2 * t + x, 16 * pair : 16 * pair + 16, :]) for t in range(TILES)]
         fields = []
         for part in range(2):
-            m = [x[8 * part : 8 * part + 8] for x in sent]
+            m = [y[8 * part : 8 * part + 8] for y in sent]
             up, across = {}, {}
             for h in range(2):
                 a, b = m[2 * h], m[2 * h + 1]
@@ -327,32 +326,35 @@
             fields += [across[0, 0], across[1, 0], across[0, 1], across[1, 1]]
         return fields
 
-    def take(d, carry):
-        last = spread(d, FIELDS // 8 - 1)
-        plane[0] = last[4] * (1.0 / CODE)
-        plane[1] = last[5]
+    def take(x, carry):
+        last = spread(x, FIELDS // 8 - 1)
+        if fresh:
+            plane[0] = last[4] * (1.0 / CODE)
+            plane[1] = last[5]
         unit = [jnp.exp2(last[6 + t]) * (1.0 / CODE) for t in range(2)]
         for pair in range(FIELDS // 8):
-            fields = last if pair == FIELDS // 8 - 1 else spread(d, pair)
+            fields = last if pair == FIELDS // 8 - 1 else spread(x, pair)
             for i, value in enumerate(fields):
                 which, k = divmod(8 * pair + i, OWN_LEVELS)
+                row = OWN_LEVELS * x + k
                 if which < 2:
-                    cells[pl.ds(which * 8 * PITCH + OWN_LEVELS * d + k, 8, stride=PITCH), :] = (
-                        value * unit[which]
-                    )
+                    to = pl.ds(which * 8 * pitch + base + row, 8, stride=pitch)
+                    cells[to, :] = value * unit[which]
                 elif which < 4:
-                    at = pl.ds((which - 2) * 8 * PITCH + OWN_LEVELS * d + k, 8, stride=PITCH)
-                    flow[at, :] = value * (FASTEST / CODE)
+                    to = pl.ds((which - 2) * 8 * HALF + row, 8, stride=HALF)
+                    flow[to, :] = value * (FASTEST / CODE)
         return carry
 
-    lax.fori_loop(0, BLOCKS, take, 0)
-
-    for field in (cells, flow):
-        for s in range(16):
-            field[s * PITCH + LEVELS : (s + 1) * PITCH, :] = jnp.zeros((PITCH - LEVELS, 128), F32)
-
-    def block(base, g):
-        return pl.ds(pl.multiple_of(base * PITCH + 8 * g, 8), 8)
+    lax.fori_loop(0, BLOCKS // CORES, take, 0)
+
+    def at(where, row, g):
+        return pl.ds(pl.multiple_of(row * where[0] + where[1] + 8 * g, 8), 8)
+
+    spare = jnp.zeros((HALF - 2 * OWN_LEVELS, 128), F32)
+    for s in range(16):
+        for field, where in ((cells, cells_at), (flow, flow_at)):
+            end = s * where[0] + where[1] + HALF
+            field[end - spare.shape[0] : end, :] = spare
 
     def faces(w):
         size = jnp.abs(w)
@@ -364,20 +366,20 @@
         )
 
     def prepare(g, carry):
-        level = (sub + 8 * g).astype(F32)
+        level = levels_of(sub + 8 * g, side).astype(F32)
         wet = [jnp.where(plane[1, s : s + 1, :] > level, 1.0, 0.0) for s in range(8)]
         for t in range(2):
             for s in range(8):
-                at = block(8 * t + s, g)
-                cells[at, :] = wet[s] * cells[at, :]
+                here = at(cells_at, 8 * t + s, g)
+                cells[here, :] = wet[s] * cells[here, :]
         beyond = jnp.where(left, pltpu.roll(wet[0], 64, 1), 0.0)
         north_w = [
-            flow[block(8 + s, g), :] * wet[s] * (wet[s + 1] if s < 7 else beyond) for s in range(8)
+            flow[at(flow_at, 8 + s, g), :] * wet[s] * (wet[s + 1] if s < 7 else beyond) for s in range(8)
         ]
         first = jnp.where(left, 0.0, pltpu.roll(north_w[7], 64, 1))
         merid = [faces(w) for w in [first] + north_w]
         for s in range(8):
-            east_w = flow[block(s, g), :] * wet[s] * pltpu.roll(wet[s], 127, 1)
+            east_w = flow[at(flow_at, s, g), :] * wet[s] * pltpu.roll(wet[s], 127, 1)
             a, b, d, e = faces(east_w)
             a1, b1, d1, e1 = faces(pltpu.roll(east_w, 1, 1))
             p1, q1, r1, s1 = merid[s]
@@ -401,10 +403,49 @@
             coef[g, s, 7], coef[g, s, 8] = north
         return carry
 
-    lax.fori_loop(0, PITCH // 8, prepare, 0, unroll=5)
-
-    deep = index((LEVELS, 128), 0)
-    light[...] = jnp.exp(deep.astype(F32) * (-4.0 / LEVELS))
+    lax.fori_loop(0, HALF // 8, prepare, 0, unroll=True)
+
+
+def own_kernel(*refs):
+    arrived, (ops, cells, coef, plane, ordered, recv, flow) = refs[: 2 * TILES], refs[2 * TILES :]
+    own = lax.axis_index("depth")
+    tile = lax.axis_index("tile")
+    core, half = own % CORES, own // CORES
+    for i, ref in enumerate(arrived):
+        far, distance = divmod(i, TILES)
+        to = 2 * ((tile + TILES - distance) % TILES) + (half ^ far)
+        for pair in range(FIELDS // 8):
+            recv[to, 16 * pair : 16 * pair + 16, :] = piece(ref, pair, core)
+    load_half(recv, core, cells, HALF, 0, flow, coef, plane, True)
+    shape = (PITCH, LEVELS)
+    pick = jnp.where(level_rows(shape, core) == index(shape, 1), 1.0, 0.0).astype(jnp.bfloat16)
+    for t in range(2):
+        rows = jnp.dot(pick, ops[t], preferred_element_type=F32).astype(jnp.bfloat16)
+        both = lax.dot_general(rows, pick, (((1,), (1,)), ((), ())), preferred_element_type=F32)
+        ordered[t] = both.astype(jnp.bfloat16)
+
+
+def steps_kernel(
+    others, own_cells, own_coef, plane, ops, out0, out1, out2, out3,
+    recv, cells, firsts, moved, flow, coef, light, ends,
+):
+    own = lax.axis_index("depth")
+    tile = lax.axis_index("tile")
+    core, half = own % CORES, own // CORES
+    for i in range(2 * TILES):
+        far, distance = divmod(i, TILES)
+        to = 2 * ((tile + TILES - distance) % TILES) + (half ^ far)
+        recv[to] = others[PIECE * i : PIECE * i + PIECE, :]
+    load_half(recv, 1 - core, cells, PITCH, HALF, flow, coef, plane, False)
+    for s in range(16):
+        cells[PITCH * s : PITCH * s + HALF, :] = own_cells[HALF * s : HALF * s + HALF, :]
+    lane = index((8, 128), 1)
+
+    def block(base, g):
+        return slice(base * PITCH + 8 * g, base * PITCH + 8 * g + 8)
+
+    deep = level_rows((PITCH, 128), core).astype(F32)
+    light[...] = jnp.exp(deep * (-4.0 / LEVELS))
 
     def combine(c, near, far):
         centre = near[1]
@@ -425,41 +466,40 @@
             turned = [pltpu.roll(inner[s], 64, 1) for s in (6, 7, 0, 1)]
             columns.append(turned[:2] + inner + turned[2:])
         for s in range(8):
-            c = [coef[g, s, i] for i in range(9)]
+            stencil = own_coef.at[g, s] if g < HALF // 8 else coef.at[g - HALF // 8, s]
+            c = [stencil[i] for i in range(9)]
             for t in range(2):
                 k = columns[t]
                 emit(t, s, combine(c, k[s + 1 : s + 4], (k[s], k[s + 4])))
 
-    def first_stage(g, carry):
+    def first_stage(g):
         def emit(t, s, value):
             firsts[block(8 * t + s, g), :] = value
 
         stage(cells, g, emit)
-        return carry
-
-    def second_stage(g, carry):
+
+    def second_stage(g):
         def emit(t, s, value):
             at = block(8 * t + s, g)
             moved[at, :] = 0.5 * (cells[at, :] + value)
 
         stage(firsts, g, emit)
-        return carry
 
     def step(n, carry):
-        lax.fori_loop(0, PITCH // 8, first_stage, 0, unroll=True)
-        lax.fori_loop(0, PITCH // 8, second_stage, 0, unroll=True)
+        for part in (first_stage, second_stage):
+            for g in range(PITCH // 8):
+                part(g)
         for pair in range(4):
             mixed = []
             for t in range(2):
                 base = (t * 8 + 2 * pair) * PITCH
                 both = jnp.concatenate(
-                    [moved[base : base + LEVELS, :], moved[base + PITCH : base + PITCH + LEVELS, :]],
-                    axis=1,
+                    [moved[base : base + PITCH, :], moved[base + PITCH : base + 2 * PITCH, :]], axis=1
                 ).astype(jnp.bfloat16)
                 mixed.append(jnp.dot(ops[t], both, preferred_element_type=F32))
             for i in range(2):
                 s = 2 * pair + i
-                wet = deep.astype(F32) < plane[1, s : s + 1, :]
+                wet = deep < plane[1, s : s + 1, :]
                 p = jnp.where(wet, mixed[0][:, 128 * i : 128 * i + 128], 0.0)
                 q = jnp.where(wet, mixed[1][:, 128 * i : 128 * i + 128], 0.0)
                 square = p * p
@@ -467,8 +507,8 @@
                     square * p / (square + half_sat_sq)
                 )
                 gain = uptake - remin_rate * q
-                cells[s * PITCH : s * PITCH + LEVELS, :] = p - gain
-                cells[(8 + s) * PITCH : (8 + s) * PITCH + LEVELS, :] = q + gain
+                cells[s * PITCH : s * PITCH + PITCH, :] = p - gain
+                cells[(8 + s) * PITCH : (8 + s) * PITCH + PITCH, :] = q + gain
         return carry
 
     lax.fori_loop(0, STEPS, step, 0)
@@ -476,11 +516,11 @@
     chunk = lane // 32
 
     def send(n, carry):
-        to = own ^ n
+        first = HALF * (n % CORES) + OWN_LEVELS * (half ^ (n // CORES))
         blocks = []
         for t in range(2):
             def level(k):
-                return cells[pl.ds(t * 8 * PITCH + OWN_LEVELS * to + k, 8, stride=PITCH), :]
+                return cells[pl.ds(t * 8 * PITCH + first + k, 8, stride=PITCH), :]
 
             largest = jnp.abs(level(0))
             for k in range(1, OWN_LEVELS):
@@ -623,23 +663,23 @@
     received = across_tiles(here)
     received += across_tiles(call(relay_kernel, [both] * TILES, [sent], across))
     others = call(core_kernel, pltpu.VMEM((2 * TILES * PIECE, 128), I16), [], *received)
-    received.append(lax.ppermute(others, "depth", [(i, i ^ 1) for i in range(BLOCKS)]))
+    others = lax.ppermute(others, "depth", [(i, i ^ 1) for i in range(BLOCKS)])
+    pieces = pltpu.VMEM((2 * TILES, PIECE, 128), I16)
+    flow = pltpu.VMEM((2 * 8 * HALF, 128), F32)
+    coef = pltpu.VMEM((HALF // 8, 8, 9, 8, 128), F32)
+    loaded = call(
+        own_kernel,
+        [flow, coef, pltpu.VMEM((2, 8, 128), F32), pltpu.VMEM((2, PITCH, PITCH), jnp.bfloat16)],
+        [pieces, flow],
+        *received,
+        column_ops,
+    )
     out = call(
         steps_kernel,
         [message] * 4,
-        [
-            pltpu.VMEM((TILES * BLOCKS, PIECE, 128), I16),
-            cells,
-            cells,
-            cells,
-            cells,
-            pltpu.VMEM((PITCH // 8, 8, 9, 8, 128), F32),
-            pltpu.VMEM((2, 8, 128), F32),
-            pltpu.VMEM((LEVELS, 128), F32),
-            slots,
-        ],
-        *received,
-        column_ops,
+        [pieces, cells, cells, cells, flow, coef, pltpu.VMEM((PITCH, 128), F32), slots],
+        others,
+        *loaded,
         reserve=16,
     )
     turned = call(turn_kernel, [message] * 4, [slots] * 2, *across_depth(out))

time: 48.5 us -> 47.6 us (0.981)
  waiting for transfers between devices: 12.4 us -> 11.6 us
    ppermute x1, waiting for transfers between devices: 1.23 us -> 0.52 us  [window_shards(): others = lax.ppermute(others, 'depth', [(i, i ^ 1) for i in range(BLOCKS)])]
    pallas_call x6 -> x7, Pallas kernels: 13.5 us -> 13.6 us  [call(): pl.pallas_call(kernel, out_shape=outs, in_specs=[VMEM] * len(args), out_s...]
  transfers between devices with their start and end apart: 15 -> 15, of which waited for: 8 -> 8; matrix products, arithmetic and copies ran while one was open for 0% -> 0% of each run, Pallas kernels for 1% -> 3%
where the time goes in v6:
time: 47.6 us; the launch traced here: 47.4 us
  starting transfers between devices  22 us (46%)
  Pallas kernels  13.6 us (29%)
  waiting for transfers between devices  11.6 us (24%)
    pallas_call x7, Pallas kernels, call(): pl.pallas_call(kernel, out_shape=outs, in_specs=[VMEM] * len(args), out_s...  13.6 us
    ppermute x6, starting transfers between devices, across_tiles(): lax.ppermute(messages[n], 'tile', [(i, (i + n) % TILES) for i in range(TI...  10.4 us
    ppermute x4, starting transfers between devices, window_shards(): lax.ppermute(turned[n], ('seg', 'tile'), [(s * TILES + t, (s + 1) % segs...  6.31 us
    ppermute x4, waiting for transfers between devices, window_shards(): lax.ppermute(turned[n], ('seg', 'tile'), [(s * TILES + t, (s + 1) % segs...  4.49 us
    ppermute x6, waiting for transfers between devices, across_tiles(): lax.ppermute(messages[n], 'tile', [(i, (i + n) % TILES) for i in range(TI...  3.37 us
    ppermute x3, waiting for transfers between devices, across_depth(): lax.ppermute(messages[n], 'depth', [(i, i ^ n) for i in range(BLOCKS)])  3.25 us
    ppermute x1, starting transfers between devices, window_shards(): lax.ppermute(across, 'depth', [(i, i ^ CORES) for i in range(BLOCKS)])  3 us
    ppermute x3, starting transfers between devices, across_depth(): lax.ppermute(messages[n], 'depth', [(i, i ^ n) for i in range(BLOCKS)])  2.21 us
  transfers between devices with their start and end apart: 15, of which 8 were waited for; matrix products, arithmetic and copies ran while one was open for 0% of the time, Pallas kernels for 3%

profile of v6, /device:TPU:0, one launch (start us, length us, event | category | flops | bytes accessed | tf_op | source)
XLA Modules:
  0.0 47.4 jit_solution(17399157161544366435)
XLA Ops:
  0.0 0.0 copy-start.3
  0.0 1.7 %shard_map.64 = (s16[720,128]{1,0:T(8,128)(2,1)S(1)}, s16[240,128]{1,0:T(8,128)(2,1)S(1)}, s16[240,128]{1,0:T(8,128)(2,1)S(1)}, s16[240,128]{1,0:T(8,128)(2,1)S(1)}, s16[240,128]{1,0:T(8,128)(2,1)S(1)}) custom-call(f32[1,2,19,4,512]{4,3,2,1,0:T(4,128)} %state.3, f32[1,2,19,4,512]{4,3,2,1,0:T(4,128)} %velocity.1, f32[1,4,512]{2,1,0:T(4,128)} %growth.1, ...), custom_call_target="tpu_custom_call" | custom-call | tf_op jit(solution)/shard_map/pallas_call | solution.py:620
  1.7 3.0 %collective-permute-start.3 = (s16[720,128]{1,0:T(8,128)(2,1)S(1)}, s16[720,128]{1,0:T(8,128)(2,1)S(1)}, u32[]{:S(2)}, u32[]{:S(2)}) collective-permute-start(s16[720,128]{1,0:T(8,128)(2,1)S(1)} %get-tuple-element.30), channel_id=1, source_target_pairs={{0,2},{1,3},{2,0},{3,1},{4,6},{5,7},{6,4},{7,5},{8,10},{9,11},{10,... | collective-permute-start | bytes 552968 | tf_op jit(solution)/shard_map/ppermute | solution.py:662
  4.7 1.6 %collective-permute-start = (s16[240,128]{1,0:T(8,128)(2,1)S(1)}, s16[240,128]{1,0:T(8,128)(2,1)S(1)}, u32[]{:S(2)}, u32[]{:S(2)}) collective-permute-start(s16[240,128]{1,0:T(8,128)(2,1)S(1)} %get-tuple-element.27), channel_id=1, source_target_pairs={{0,4},{4,8},{8,12},{12,0},{1,5},{5,9},{9,13},{13,1},{2,6},{6,10},{... | collective-permute-start | bytes 184328 | tf_op jit(solution)/shard_map/ppermute | solution.py:639
  6.3 2.6 %collective-permute-start.1 = (s16[240,128]{1,0:T(8,128)(2,1)S(1)}, s16[240,128]{1,0:T(8,128)(2,1)S(1)}, u32[]{:S(2)}, u32[]{:S(2)}) collective-permute-start(s16[240,128]{1,0:T(8,128)(2,1)S(1)} %get-tuple-element.28), channel_id=1, source_target_pairs={{0,8},{4,12},{8,0},{12,4},{1,9},{5,13},{9,1},{13,5},{2,10},{6,14},... | collective-permute-start | bytes 184328 | tf_op jit(solution)/shard_map/ppermute | solution.py:639
  8.9 1.3 %collective-permute-start.2 = (s16[240,128]{1,0:T(8,128)(2,1)S(1)}, s16[240,128]{1,0:T(8,128)(2,1)S(1)}, u32[]{:S(2)}, u32[]{:S(2)}) collective-permute-start(s16[240,128]{1,0:T(8,128)(2,1)S(1)} %get-tuple-element.29), channel_id=1, source_target_pairs={{0,12},{4,0},{8,4},{12,8},{1,13},{5,1},{9,5},{13,9},{2,14},{6,2},{... | collective-permute-start | bytes 184328 | tf_op jit(solution)/shard_map/ppermute | solution.py:639
  10.2 0.0 collective-permute-done.3.ref
  10.2 0.3 shard_map.65
  10.5 1.0 %collective-permute-start.4 = (s16[240,128]{1,0:T(8,128)(2,1)S(1)}, s16[240,128]{1,0:T(8,128)(2,1)S(1)}, u32[]{:S(2)}, u32[]{:S(2)}) collective-permute-start(s16[240,128]{1,0:T(8,128)(2,1)S(1)} %get-tuple-element.32), channel_id=1, source_target_pairs={{0,4},{4,8},{8,12},{12,0},{1,5},{5,9},{9,13},{13,1},{2,6},{6,10},{... | collective-permute-start | bytes 184328 | tf_op jit(solution)/shard_map/ppermute | solution.py:639
  11.5 2.6 %collective-permute-start.5 = (s16[240,128]{1,0:T(8,128)(2,1)S(1)}, s16[240,128]{1,0:T(8,128)(2,1)S(1)}, u32[]{:S(2)}, u32[]{:S(2)}) collective-permute-start(s16[240,128]{1,0:T(8,128)(2,1)S(1)} %get-tuple-element.33), channel_id=1, source_target_pairs={{0,8},{4,12},{8,0},{12,4},{1,9},{5,13},{9,1},{13,5},{2,10},{6,14},... | collective-permute-start | bytes 184328 | tf_op jit(solution)/shard_map/ppermute | solution.py:639
  14.1 0.0 collective-permute-done.refs_1_
  14.1 1.3 %collective-permute-start.6 = (s16[240,128]{1,0:T(8,128)(2,1)S(1)}, s16[240,128]{1,0:T(8,128)(2,1)S(1)}, u32[]{:S(2)}, u32[]{:S(2)}) collective-permute-start(s16[240,128]{1,0:T(8,128)(2,1)S(1)} %get-tuple-element.34), channel_id=1, source_target_pairs={{0,12},{4,0},{8,4},{12,8},{1,13},{5,1},{9,5},{13,9},{2,14},{6,2},{... | collective-permute-start | bytes 184328 | tf_op jit(solution)/shard_map/ppermute | solution.py:639
  15.5 0.0 collective-permute-done.1.refs_2_
  15.5 0.0 collective-permute-done.2.refs_3_
  15.5 1.4 %collective-permute-done.4.refs_5_ = s16[240,128]{1,0:T(8,128)(2,1)S(1)} collective-permute-done((s16[240,128]{1,0:T(8,128)(2,1)S(1)}, s16[240,128]{1,0:T(8,128)(2,1)S(1)}, u32[]{:S(2)}, u32[]{:S(2)}) %collective-permute-start.4) | collective-permute-done | bytes 61472 | tf_op jit(solution)/shard_map/ppermute | solution.py:639
  16.8 1.9 %collective-permute-done.5.refs_6_ = s16[240,128]{1,0:T(8,128)(2,1)S(1)} collective-permute-done((s16[240,128]{1,0:T(8,128)(2,1)S(1)}, s16[240,128]{1,0:T(8,128)(2,1)S(1)}, u32[]{:S(2)}, u32[]{:S(2)}) %collective-permute-start.5) | collective-permute-done | bytes 61472 | tf_op jit(solution)/shard_map/ppermute | solution.py:639
  18.7 0.1 collective-permute-done.6.refs_7_
  18.8 0.3 shard_map.66
  19.2 0.0 copy-start
  19.2 0.0 copy-start.1
  19.2 0.0 copy-start.2
  19.2 0.1 collective-permute-start.7
  19.3 0.0 copy-done.3
  19.3 1.1 %shard_map.67 = (f32[640,128]{1,0:T(8,128)S(1)}, f32[5,8,9,8,128]{4,3,2,1,0:T(8,128)S(1)}, f32[2,8,128]{2,1,0:T(8,128)S(1)}, bf16[2,80,80]{2,1,0:T(8,128)(2,1)S(1)}) custom-call(s16[240,128]{1,0:T(8,128)(2,1)S(1)} %get-tuple-element.26.refs_0_, s16[240,128]{1,0:T(8,128)(2,1)S(1)} %collective-permute-done.refs_1_, ...), custom_call_target="tpu_custom_call" | custom-call | tf_op jit(solution)/shard_map/pallas_call | solution.py:620
  20.4 0.5 %collective-permute-done.7.others = s16[1280,128]{1,0:T(8,128)(2,1)S(1)} collective-permute-done((s16[1280,128]{1,0:T(8,128)(2,1)S(1)}, s16[1280,128]{1,0:T(8,128)(2,1)S(1)}, u32[]{:S(2)}, u32[]{:S(2)}) %collective-permute-start.7) | collective-permute-done | bytes 327712 | tf_op jit(solution)/shard_map/ppermute | solution.py:666
  20.9 8.9 %shard_map.68 = (s16[160,128]{1,0:T(8,128)(2,1)S(1)}, s16[160,128]{1,0:T(8,128)(2,1)S(1)}, s16[160,128]{1,0:T(8,128)(2,1)S(1)}, s16[160,128]{1,0:T(8,128)(2,1)S(1)}) custom-call(s16[1280,128]{1,0:T(8,128)(2,1)S(1)} %collective-permute-done.7.others, f32[640,128]{1,0:T(8,128)S(1)} %get-tuple-element.35.own_cells, ...), custom_call_target="tpu_custom_call" | custom-call | tf_op jit(solution)/shard_map/pallas_call | solution.py:620
  29.8 1.1 %collective-permute-start.10 = (s16[160,128]{1,0:T(8,128)(2,1)S(1)}, s16[160,128]{1,0:T(8,128)(2,1)S(1)}, u32[]{:S(2)}, u32[]{:S(2)}) collective-permute-start(s16[160,128]{1,0:T(8,128)(2,1)S(1)} %get-tuple-element.42), channel_id=1, source_target_pairs={{0,3},{1,2},{2,1},{3,0},{4,7},{5,6},{6,5},{7,4},{8,11},{9,10},{10,... | collective-permute-start | bytes 122888 | tf_op jit(solution)/shard_map/ppermute | solution.py:632
  30.9 0.4 collective-permute-start.8
  31.3 0.7 %collective-permute-start.9 = (s16[160,128]{1,0:T(8,128)(2,1)S(1)}, s16[160,128]{1,0:T(8,128)(2,1)S(1)}, u32[]{:S(2)}, u32[]{:S(2)}) collective-permute-start(s16[160,128]{1,0:T(8,128)(2,1)S(1)} %get-tuple-element.41), channel_id=1, source_target_pairs={{0,2},{1,3},{2,0},{3,1},{4,6},{5,7},{6,4},{7,5},{8,10},{9,11},{10,... | collective-permute-start | bytes 122888 | tf_op jit(solution)/shard_map/ppermute | solution.py:632
  32.0 1.4 %collective-permute-done.10.in3 = s16[160,128]{1,0:T(8,128)(2,1)S(1)} collective-permute-done((s16[160,128]{1,0:T(8,128)(2,1)S(1)}, s16[160,128]{1,0:T(8,128)(2,1)S(1)}, u32[]{:S(2)}, u32[]{:S(2)}) %collective-permute-start.10) | collective-permute-done | bytes 40992 | tf_op jit(solution)/shard_map/ppermute | solution.py:632
  33.5 0.0 collective-permute-done.8.in1
  33.5 1.8 %collective-permute-done.9.in2 = s16[160,128]{1,0:T(8,128)(2,1)S(1)} collective-permute-done((s16[160,128]{1,0:T(8,128)(2,1)S(1)}, s16[160,128]{1,0:T(8,128)(2,1)S(1)}, u32[]{:S(2)}, u32[]{:S(2)}) %collective-permute-start.9) | collective-permute-done | bytes 40992 | tf_op jit(solution)/shard_map/ppermute | solution.py:632
  35.3 0.4 shard_map.69
  35.7 1.6 %collective-permute-start.11 = (s16[160,128]{1,0:T(8,128)(2,1)S(1)}, s16[160,128]{1,0:T(8,128)(2,1)S(1)}, u32[]{:S(2)}, u32[]{:S(2)}) collective-permute-start(s16[160,128]{1,0:T(8,128)(2,1)S(1)} %get-tuple-element.43), channel_id=1, source_target_pairs={{0,16},{4,20},{8,24},{12,28},{16,0},{20,4},{24,8},{28,12},{1,17},{... | collective-permute-start | bytes 122888 | tf_op jit(solution)/shard_map/ppermute | solution.py:688
  37.2 0.5 %collective-permute-start.12 = (s16[160,128]{1,0:T(8,128)(2,1)S(1)}, s16[160,128]{1,0:T(8,128)(2,1)S(1)}, u32[]{:S(2)}, u32[]{:S(2)}) collective-permute-start(s16[160,128]{1,0:T(8,128)(2,1)S(1)} %get-tuple-element.44), channel_id=1, source_target_pairs={{0,20},{4,24},{8,28},{12,16},{16,4},{20,8},{24,12},{28,0},{1,21},{... | collective-permute-start | bytes 122888 | tf_op jit(solution)/shard_map/ppermute | solution.py:688
  37.8 3.8 %collective-permute-start.13 = (s16[160,128]{1,0:T(8,128)(2,1)S(1)}, s16[160,128]{1,0:T(8,128)(2,1)S(1)}, u32[]{:S(2)}, u32[]{:S(2)}) collective-permute-start(s16[160,128]{1,0:T(8,128)(2,1)S(1)} %get-tuple-element.45), channel_id=1, source_target_pairs={{0,24},{4,28},{8,16},{12,20},{16,8},{20,12},{24,0},{28,4},{1,25},{... | collective-permute-start | bytes 122888 | tf_op jit(solution)/shard_map/ppermute | solution.py:688
  41.6 0.4 collective-permute-start.14
  42.0 0.0 collective-permute-done.11.in0
  42.0 2.1 %collective-permute-done.12.in1 = s16[160,128]{1,0:T(8,128)(2,1)S(1)} collective-permute-done((s16[160,128]{1,0:T(8,128)(2,1)S(1)}, s16[160,128]{1,0:T(8,128)(2,1)S(1)}, u32[]{:S(2)}, u32[]{:S(2)}) %collective-permute-start.12) | collective-permute-done | bytes 40992 | tf_op jit(solution)/shard_map/ppermute | solution.py:688
  44.1 0.0 collective-permute-done.13.in2
  44.1 2.3 %collective-permute-done.14.in3 = s16[160,128]{1,0:T(8,128)(2,1)S(1)} collective-permute-done((s16[160,128]{1,0:T(8,128)(2,1)S(1)}, s16[160,128]{1,0:T(8,128)(2,1)S(1)}, u32[]{:S(2)}, u32[]{:S(2)}) %collective-permute-start.14) | collective-permute-done | bytes 40992 | tf_op jit(solution)/shard_map/ppermute | solution.py:688
  46.5 0.0 copy-done
  46.5 0.0 copy-done.1
  46.5 0.0 copy-done.2
  46.5 0.9 %shard_map.70 = f32[1,2,19,4,512]{4,3,2,1,0:T(4,128)} custom-call(s16[160,128]{1,0:T(8,128)(2,1)S(1)} %collective-permute-done.11.in0, s16[160,128]{1,0:T(8,128)(2,1)S(1)} %collective-permute-done.12.in1, s16[160,128]{1,0:T(8,128)(2,1)S(1)} %collective-permute-done.13.in2, s16[160,128]{1,0:T(8,128)(2,1)S(1)} %collective-permute-done.14.in3, ...), custom_call_target="tpu_custom_call" | custom-call | tf_op jit(solution)/shard_map/pallas_call | solution.py:620
  (1 shorter events, 0.0 us)
Async XLA Ops:
  0.0 19.3 %copy-start.3 = (bf16[2,76,76]{2,0,1:T(2,128)(2,1)S(1)}, bf16[2,76,76]{2,0,1:T(2,128)(2,1)}, u32[]{:S(2)}) copy-start(bf16[2,76,76]{2,0,1:T(2,128)(2,1)} %param.11) | copy-start | bytes 69316
  1.7 8.5 %collective-permute-start.3 = (s16[720,128]{1,0:T(8,128)(2,1)S(1)}, s16[720,128]{1,0:T(8,128)(2,1)S(1)}, u32[]{:S(2)}, u32[]{:S(2)}) collective-permute-start(s16[720,128]{1,0:T(8,128)(2,1)S(1)} %get-tuple-element.30), channel_id=1, source_target_pairs={{0,2},{1,3},{2,0},{3,1},{4,6},{5,7},{6,4},{7,5},{8,10},{9,11},{10,... | collective-permute-start | bytes 552968 | tf_op jit(solution)/shard_map/ppermute | solution.py:662
  4.7 9.4 %collective-permute-start = (s16[240,128]{1,0:T(8,128)(2,1)S(1)}, s16[240,128]{1,0:T(8,128)(2,1)S(1)}, u32[]{:S(2)}, u32[]{:S(2)}) collective-permute-start(s16[240,128]{1,0:T(8,128)(2,1)S(1)} %get-tuple-element.27), channel_id=1, source_target_pairs={{0,4},{4,8},{8,12},{12,0},{1,5},{5,9},{9,13},{13,1},{2,6},{6,10},{... | collective-permute-start | bytes 184328 | tf_op jit(solution)/shard_map/ppermute | solution.py:639
  6.3 9.2 %collective-permute-start.1 = (s16[240,128]{1,0:T(8,128)(2,1)S(1)}, s16[240,128]{1,0:T(8,128)(2,1)S(1)}, u32[]{:S(2)}, u32[]{:S(2)}) collective-permute-start(s16[240,128]{1,0:T(8,128)(2,1)S(1)} %get-tuple-element.28), channel_id=1, source_target_pairs={{0,8},{4,12},{8,0},{12,4},{1,9},{5,13},{9,1},{13,5},{2,10},{6,14},... | collective-permute-start | bytes 184328 | tf_op jit(solution)/shard_map/ppermute | solution.py:639
  8.9 6.6 %collective-permute-start.2 = (s16[240,128]{1,0:T(8,128)(2,1)S(1)}, s16[240,128]{1,0:T(8,128)(2,1)S(1)}, u32[]{:S(2)}, u32[]{:S(2)}) collective-permute-start(s16[240,128]{1,0:T(8,128)(2,1)S(1)} %get-tuple-element.29), channel_id=1, source_target_pairs={{0,12},{4,0},{8,4},{12,8},{1,13},{5,1},{9,5},{13,9},{2,14},{6,2},{... | collective-permute-start | bytes 184328 | tf_op jit(solution)/shard_map/ppermute | solution.py:639
  10.5 6.3 %collective-permute-start.4 = (s16[240,128]{1,0:T(8,128)(2,1)S(1)}, s16[240,128]{1,0:T(8,128)(2,1)S(1)}, u32[]{:S(2)}, u32[]{:S(2)}) collective-permute-start(s16[240,128]{1,0:T(8,128)(2,1)S(1)} %get-tuple-element.32), channel_id=1, source_target_pairs={{0,4},{4,8},{8,12},{12,0},{1,5},{5,9},{9,13},{13,1},{2,6},{6,10},{... | collective-permute-start | bytes 184328 | tf_op jit(solution)/shard_map/ppermute | solution.py:639
  11.5 7.2 %collective-permute-start.5 = (s16[240,128]{1,0:T(8,128)(2,1)S(1)}, s16[240,128]{1,0:T(8,128)(2,1)S(1)}, u32[]{:S(2)}, u32[]{:S(2)}) collective-permute-start(s16[240,128]{1,0:T(8,128)(2,1)S(1)} %get-tuple-element.33), channel_id=1, source_target_pairs={{0,8},{4,12},{8,0},{12,4},{1,9},{5,13},{9,1},{13,5},{2,10},{6,14},... | collective-permute-start | bytes 184328 | tf_op jit(solution)/shard_map/ppermute | solution.py:639
  14.1 4.7 %collective-permute-start.6 = (s16[240,128]{1,0:T(8,128)(2,1)S(1)}, s16[240,128]{1,0:T(8,128)(2,1)S(1)}, u32[]{:S(2)}, u32[]{:S(2)}) collective-permute-start(s16[240,128]{1,0:T(8,128)(2,1)S(1)} %get-tuple-element.34), channel_id=1, source_target_pairs={{0,12},{4,0},{8,4},{12,8},{1,13},{5,1},{9,5},{13,9},{2,14},{6,2},{... | collective-permute-start | bytes 184328 | tf_op jit(solution)/shard_map/ppermute | solution.py:639
  19.2 27.3 %copy-start = (f32[1,2,19,4,512]{4,3,2,1,0:T(4,128)S(1)}, f32[1,2,19,4,512]{4,3,2,1,0:T(4,128)}, u32[]{:S(2)}) copy-start(f32[1,2,19,4,512]{4,3,2,1,0:T(4,128)} %state.3) | copy-start | bytes 933892
  19.2 27.3 %copy-start.1 = (s32[4,512]{1,0:T(4,128)S(1)}, s32[4,512]{1,0:T(4,128)}, u32[]{:S(2)}) copy-start(s32[4,512]{1,0:T(4,128)} %land_sea.3) | copy-start | bytes 24580
  19.2 27.3 %copy-start.2 = (s32[4,512]{1,0:T(4,128)S(1)}, s32[4,512]{1,0:T(4,128)}, u32[]{:S(2)}) copy-start(s32[4,512]{1,0:T(4,128)} %depth_index.3) | copy-start | bytes 24580
  19.2 1.7 %collective-permute-start.7 = (s16[1280,128]{1,0:T(8,128)(2,1)S(1)}, s16[1280,128]{1,0:T(8,128)(2,1)S(1)}, u32[]{:S(2)}, u32[]{:S(2)}) collective-permute-start(s16[1280,128]{1,0:T(8,128)(2,1)S(1)} %shard_map.66), channel_id=1, source_target_pairs={{0,1},{1,0},{2,3},{3,2},{4,5},{5,4},{6,7},{7,6},{8,9},{9,8},{10,11... | collective-permute-start | bytes 983048 | tf_op jit(solution)/shard_map/ppermute | solution.py:666
  29.8 3.6 %collective-permute-start.10 = (s16[160,128]{1,0:T(8,128)(2,1)S(1)}, s16[160,128]{1,0:T(8,128)(2,1)S(1)}, u32[]{:S(2)}, u32[]{:S(2)}) collective-permute-start(s16[160,128]{1,0:T(8,128)(2,1)S(1)} %get-tuple-element.42), channel_id=1, source_target_pairs={{0,3},{1,2},{2,1},{3,0},{4,7},{5,6},{6,5},{7,4},{8,11},{9,10},{10,... | collective-permute-start | bytes 122888 | tf_op jit(solution)/shard_map/ppermute | solution.py:632
  30.9 2.5 %collective-permute-start.8 = (s16[160,128]{1,0:T(8,128)(2,1)S(1)}, s16[160,128]{1,0:T(8,128)(2,1)S(1)}, u32[]{:S(2)}, u32[]{:S(2)}) collective-permute-start(s16[160,128]{1,0:T(8,128)(2,1)S(1)} %get-tuple-element.40), channel_id=1, source_target_pairs={{0,1},{1,0},{2,3},{3,2},{4,5},{5,4},{6,7},{7,6},{8,9},{9,8},{10,11... | collective-permute-start | bytes 122888 | tf_op jit(solution)/shard_map/ppermute | solution.py:632
  31.3 4.0 %collective-permute-start.9 = (s16[160,128]{1,0:T(8,128)(2,1)S(1)}, s16[160,128]{1,0:T(8,128)(2,1)S(1)}, u32[]{:S(2)}, u32[]{:S(2)}) collective-permute-start(s16[160,128]{1,0:T(8,128)(2,1)S(1)} %get-tuple-element.41), channel_id=1, source_target_pairs={{0,2},{1,3},{2,0},{3,1},{4,6},{5,7},{6,4},{7,5},{8,10},{9,11},{10,... | collective-permute-start | bytes 122888 | tf_op jit(solution)/shard_map/ppermute | solution.py:632
  35.7 6.3 %collective-permute-start.11 = (s16[160,128]{1,0:T(8,128)(2,1)S(1)}, s16[160,128]{1,0:T(8,128)(2,1)S(1)}, u32[]{:S(2)}, u32[]{:S(2)}) collective-permute-start(s16[160,128]{1,0:T(8,128)(2,1)S(1)} %get-tuple-element.43), channel_id=1, source_target_pairs={{0,16},{4,20},{8,24},{12,28},{16,0},{20,4},{24,8},{28,12},{1,17},{... | collective-permute-start | bytes 122888 | tf_op jit(solution)/shard_map/ppermute | solution.py:688
  37.2 6.9 %collective-permute-start.12 = (s16[160,128]{1,0:T(8,128)(2,1)S(1)}, s16[160,128]{1,0:T(8,128)(2,1)S(1)}, u32[]{:S(2)}, u32[]{:S(2)}) collective-permute-start(s16[160,128]{1,0:T(8,128)(2,1)S(1)} %get-tuple-element.44), channel_id=1, source_target_pairs={{0,20},{4,24},{8,28},{12,16},{16,4},{20,8},{24,12},{28,0},{1,21},{... | collective-permute-start | bytes 122888 | tf_op jit(solution)/shard_map/ppermute | solution.py:688
  37.8 6.3 %collective-permute-start.13 = (s16[160,128]{1,0:T(8,128)(2,1)S(1)}, s16[160,128]{1,0:T(8,128)(2,1)S(1)}, u32[]{:S(2)}, u32[]{:S(2)}) collective-permute-start(s16[160,128]{1,0:T(8,128)(2,1)S(1)} %get-tuple-element.45), channel_id=1, source_target_pairs={{0,24},{4,28},{8,16},{12,20},{16,8},{20,12},{24,0},{28,4},{1,25},{... | collective-permute-start | bytes 122888 | tf_op jit(solution)/shard_map/ppermute | solution.py:688
  41.6 4.9 %collective-permute-start.14 = (s16[160,128]{1,0:T(8,128)(2,1)S(1)}, s16[160,128]{1,0:T(8,128)(2,1)S(1)}, u32[]{:S(2)}, u32[]{:S(2)}) collective-permute-start(s16[160,128]{1,0:T(8,128)(2,1)S(1)} %get-tuple-element.46), channel_id=1, source_target_pairs={{0,28},{4,16},{8,20},{12,24},{16,12},{20,0},{24,4},{28,8},{1,29},{... | collective-permute-start | bytes 122888 | tf_op jit(solution)/shard_map/ppermute | solution.py:688

commit v7 on v6

--- a/solution.py
+++ b/solution.py
@@ -447,18 +447,28 @@
     deep = level_rows((PITCH, 128), core).astype(F32)
     light[...] = jnp.exp(deep * (-4.0 / LEVELS))
 
-    def combine(c, near, far):
+    source_lane, lanes = index((256, 256), 0) % 128, index((256, 256), 1)
+    shifts = jnp.where(
+        lanes % 128 == (source_lane + jnp.where(lanes < 128, 2, 126)) % 128, 1.0, 0.0
+    ).astype(jnp.bfloat16)
+
+    def combine(c, near, far, two):
         centre = near[1]
         return (
             (c[0] * centre + c[6] * near[0] + c[7] * near[2])
             + (c[5] * far[0] + c[8] * far[1])
             + (c[2] * pltpu.roll(centre, 1, 1) + c[3] * pltpu.roll(centre, 127, 1))
-            + (c[1] * pltpu.roll(centre, 2, 1) + c[4] * pltpu.roll(centre, 126, 1))
+            + (c[1] * two[0] + c[4] * two[1])
         )
 
     def stage(source, g, emit):
         def at(t, s):
             return source[block(8 * t + s, g), :]
+
+        rows = jnp.concatenate([at(t, s) for t in range(2) for s in range(8)], axis=0)
+        high = rows.astype(jnp.bfloat16)
+        low = (rows - high.astype(F32)).astype(jnp.bfloat16)
+        moves = jnp.dot(jnp.concatenate([high, low], axis=1), shifts, preferred_element_type=F32)
 
         columns = []
         for t in range(2):
@@ -470,7 +480,9 @@
             c = [stencil[i] for i in range(9)]
             for t in range(2):
                 k = columns[t]
-                emit(t, s, combine(c, k[s + 1 : s + 4], (k[s], k[s + 4])))
+                row = slice(8 * (8 * t + s), 8 * (8 * t + s) + 8)
+                two = moves[row, :128], moves[row, 128:]
+                emit(t, s, combine(c, k[s + 1 : s + 4], (k[s], k[s + 4]), two))
 
     def first_stage(g):
         def emit(t, s, value):
@@ -486,9 +498,11 @@
         stage(firsts, g, emit)
 
     def step(n, carry):
-        for part in (first_stage, second_stage):
-            for g in range(PITCH // 8):
-                part(g)
+        for g in range(PITCH // 8 + 1):
+            if g < PITCH // 8:
+                first_stage(g)
+            if g > 0:
+                second_stage(g - 1)
         for pair in range(4):
             mixed = []
             for t in range(2):
@@ -546,7 +560,7 @@
             ends[n, 16 * pair : 16 * pair + 16, :] = coded(jnp.concatenate(halves, axis=0))
         return carry
 
-    lax.fori_loop(0, BLOCKS, send, 0)
+    lax.fori_loop(0, BLOCKS, send, 0, unroll=True)
     for n, out in enumerate((out0, out1, out2, out3)):
         out[...] = ends[n]
 

time: 47.6 us -> 45.1 us (0.947)
  Pallas kernels: 13.6 us -> 11.2 us
    pallas_call x7, Pallas kernels: 13.6 us -> 11.2 us  [call(): pl.pallas_call(kernel, out_shape=outs, in_specs=[VMEM] * len(args), out_s...]
where the time goes in v7:
time: 45.1 us; the launch traced here: 45 us
  starting transfers between devices  22 us (49%)
  waiting for transfers between devices  11.7 us (26%)
  Pallas kernels  11.2 us (25%)
    pallas_call x7, Pallas kernels, call(): pl.pallas_call(kernel, out_shape=outs, in_specs=[VMEM] * len(args), out_s...  11.2 us
    ppermute x6, starting transfers between devices, across_tiles(): lax.ppermute(messages[n], 'tile', [(i, (i + n) % TILES) for i in range(TI...  10.4 us
    ppermute x4, starting transfers between devices, window_shards(): lax.ppermute(turned[n], ('seg', 'tile'), [(s * TILES + t, (s + 1) % segs...  6.31 us
    ppermute x4, waiting for transfers between devices, window_shards(): lax.ppermute(turned[n], ('seg', 'tile'), [(s * TILES + t, (s + 1) % segs...  4.5 us
    ppermute x6, waiting for transfers between devices, across_tiles(): lax.ppermute(messages[n], 'tile', [(i, (i + n) % TILES) for i in range(TI...  3.37 us
    ppermute x3, waiting for transfers between devices, across_depth(): lax.ppermute(messages[n], 'depth', [(i, i ^ n) for i in range(BLOCKS)])  3.25 us
    ppermute x1, starting transfers between devices, window_shards(): lax.ppermute(across, 'depth', [(i, i ^ CORES) for i in range(BLOCKS)])  3 us
    ppermute x3, starting transfers between devices, across_depth(): lax.ppermute(messages[n], 'depth', [(i, i ^ n) for i in range(BLOCKS)])  2.21 us
  transfers between devices with their start and end apart: 15, of which 8 were waited for; matrix products, arithmetic and copies ran while one was open for 0% of the time, Pallas kernels for 3%

profile of v7, /device:TPU:0, one launch (start us, length us, event | category | flops | bytes accessed | tf_op | source)
XLA Modules:
  0.0 45.0 jit_solution(8327314786205137611)
XLA Ops:
  0.0 0.0 copy-start.3
  0.0 1.7 %shard_map.64 = (s16[720,128]{1,0:T(8,128)(2,1)S(1)}, s16[240,128]{1,0:T(8,128)(2,1)S(1)}, s16[240,128]{1,0:T(8,128)(2,1)S(1)}, s16[240,128]{1,0:T(8,128)(2,1)S(1)}, s16[240,128]{1,0:T(8,128)(2,1)S(1)}) custom-call(f32[1,2,19,4,512]{4,3,2,1,0:T(4,128)} %state.3, f32[1,2,19,4,512]{4,3,2,1,0:T(4,128)} %velocity.1, f32[1,4,512]{2,1,0:T(4,128)} %growth.1, ...), custom_call_target="tpu_custom_call" | custom-call | tf_op jit(solution)/shard_map/pallas_call | solution.py:634
  1.7 3.0 %collective-permute-start.3 = (s16[720,128]{1,0:T(8,128)(2,1)S(1)}, s16[720,128]{1,0:T(8,128)(2,1)S(1)}, u32[]{:S(2)}, u32[]{:S(2)}) collective-permute-start(s16[720,128]{1,0:T(8,128)(2,1)S(1)} %get-tuple-element.30), channel_id=1, source_target_pairs={{0,2},{1,3},{2,0},{3,1},{4,6},{5,7},{6,4},{7,5},{8,10},{9,11},{10,... | collective-permute-start | bytes 552968 | tf_op jit(solution)/shard_map/ppermute | solution.py:676
  4.7 1.6 %collective-permute-start = (s16[240,128]{1,0:T(8,128)(2,1)S(1)}, s16[240,128]{1,0:T(8,128)(2,1)S(1)}, u32[]{:S(2)}, u32[]{:S(2)}) collective-permute-start(s16[240,128]{1,0:T(8,128)(2,1)S(1)} %get-tuple-element.27), channel_id=1, source_target_pairs={{0,4},{4,8},{8,12},{12,0},{1,5},{5,9},{9,13},{13,1},{2,6},{6,10},{... | collective-permute-start | bytes 184328 | tf_op jit(solution)/shard_map/ppermute | solution.py:653
  6.3 2.6 %collective-permute-start.1 = (s16[240,128]{1,0:T(8,128)(2,1)S(1)}, s16[240,128]{1,0:T(8,128)(2,1)S(1)}, u32[]{:S(2)}, u32[]{:S(2)}) collective-permute-start(s16[240,128]{1,0:T(8,128)(2,1)S(1)} %get-tuple-element.28), channel_id=1, source_target_pairs={{0,8},{4,12},{8,0},{12,4},{1,9},{5,13},{9,1},{13,5},{2,10},{6,14},... | collective-permute-start | bytes 184328 | tf_op jit(solution)/shard_map/ppermute | solution.py:653
  8.9 1.3 %collective-permute-start.2 = (s16[240,128]{1,0:T(8,128)(2,1)S(1)}, s16[240,128]{1,0:T(8,128)(2,1)S(1)}, u32[]{:S(2)}, u32[]{:S(2)}) collective-permute-start(s16[240,128]{1,0:T(8,128)(2,1)S(1)} %get-tuple-element.29), channel_id=1, source_target_pairs={{0,12},{4,0},{8,4},{12,8},{1,13},{5,1},{9,5},{13,9},{2,14},{6,2},{... | collective-permute-start | bytes 184328 | tf_op jit(solution)/shard_map/ppermute | solution.py:653
  10.2 0.0 collective-permute-done.3.ref
  10.2 0.3 shard_map.65
  10.5 1.0 %collective-permute-start.4 = (s16[240,128]{1,0:T(8,128)(2,1)S(1)}, s16[240,128]{1,0:T(8,128)(2,1)S(1)}, u32[]{:S(2)}, u32[]{:S(2)}) collective-permute-start(s16[240,128]{1,0:T(8,128)(2,1)S(1)} %get-tuple-element.32), channel_id=1, source_target_pairs={{0,4},{4,8},{8,12},{12,0},{1,5},{5,9},{9,13},{13,1},{2,6},{6,10},{... | collective-permute-start | bytes 184328 | tf_op jit(solution)/shard_map/ppermute | solution.py:653
  11.5 2.6 %collective-permute-start.5 = (s16[240,128]{1,0:T(8,128)(2,1)S(1)}, s16[240,128]{1,0:T(8,128)(2,1)S(1)}, u32[]{:S(2)}, u32[]{:S(2)}) collective-permute-start(s16[240,128]{1,0:T(8,128)(2,1)S(1)} %get-tuple-element.33), channel_id=1, source_target_pairs={{0,8},{4,12},{8,0},{12,4},{1,9},{5,13},{9,1},{13,5},{2,10},{6,14},... | collective-permute-start | bytes 184328 | tf_op jit(solution)/shard_map/ppermute | solution.py:653
  14.1 0.0 collective-permute-done.refs_1_
  14.1 1.3 %collective-permute-start.6 = (s16[240,128]{1,0:T(8,128)(2,1)S(1)}, s16[240,128]{1,0:T(8,128)(2,1)S(1)}, u32[]{:S(2)}, u32[]{:S(2)}) collective-permute-start(s16[240,128]{1,0:T(8,128)(2,1)S(1)} %get-tuple-element.34), channel_id=1, source_target_pairs={{0,12},{4,0},{8,4},{12,8},{1,13},{5,1},{9,5},{13,9},{2,14},{6,2},{... | collective-permute-start | bytes 184328 | tf_op jit(solution)/shard_map/ppermute | solution.py:653
  15.5 0.0 collective-permute-done.1.refs_2_
  15.5 0.0 collective-permute-done.2.refs_3_
  15.5 1.4 %collective-permute-done.4.refs_5_ = s16[240,128]{1,0:T(8,128)(2,1)S(1)} collective-permute-done((s16[240,128]{1,0:T(8,128)(2,1)S(1)}, s16[240,128]{1,0:T(8,128)(2,1)S(1)}, u32[]{:S(2)}, u32[]{:S(2)}) %collective-permute-start.4) | collective-permute-done | bytes 61472 | tf_op jit(solution)/shard_map/ppermute | solution.py:653
  16.8 1.9 %collective-permute-done.5.refs_6_ = s16[240,128]{1,0:T(8,128)(2,1)S(1)} collective-permute-done((s16[240,128]{1,0:T(8,128)(2,1)S(1)}, s16[240,128]{1,0:T(8,128)(2,1)S(1)}, u32[]{:S(2)}, u32[]{:S(2)}) %collective-permute-start.5) | collective-permute-done | bytes 61472 | tf_op jit(solution)/shard_map/ppermute | solution.py:653
  18.7 0.1 collective-permute-done.6.refs_7_
  18.8 0.3 shard_map.66
  19.2 0.0 copy-start
  19.2 0.0 copy-start.1
  19.2 0.0 copy-start.2
  19.2 0.1 collective-permute-start.7
  19.3 0.0 copy-done.3
  19.3 1.1 %shard_map.67 = (f32[640,128]{1,0:T(8,128)S(1)}, f32[5,8,9,8,128]{4,3,2,1,0:T(8,128)S(1)}, f32[2,8,128]{2,1,0:T(8,128)S(1)}, bf16[2,80,80]{2,1,0:T(8,128)(2,1)S(1)}) custom-call(s16[240,128]{1,0:T(8,128)(2,1)S(1)} %get-tuple-element.26.refs_0_, s16[240,128]{1,0:T(8,128)(2,1)S(1)} %collective-permute-done.refs_1_, ...), custom_call_target="tpu_custom_call" | custom-call | tf_op jit(solution)/shard_map/pallas_call | solution.py:634
  20.4 0.5 %collective-permute-done.7.others = s16[1280,128]{1,0:T(8,128)(2,1)S(1)} collective-permute-done((s16[1280,128]{1,0:T(8,128)(2,1)S(1)}, s16[1280,128]{1,0:T(8,128)(2,1)S(1)}, u32[]{:S(2)}, u32[]{:S(2)}) %collective-permute-start.7) | collective-permute-done | bytes 327712 | tf_op jit(solution)/shard_map/ppermute | solution.py:680
  20.9 6.5 %shard_map.68 = (s16[160,128]{1,0:T(8,128)(2,1)S(1)}, s16[160,128]{1,0:T(8,128)(2,1)S(1)}, s16[160,128]{1,0:T(8,128)(2,1)S(1)}, s16[160,128]{1,0:T(8,128)(2,1)S(1)}) custom-call(s16[1280,128]{1,0:T(8,128)(2,1)S(1)} %collective-permute-done.7.others, f32[640,128]{1,0:T(8,128)S(1)} %get-tuple-element.35.own_cells, ...), custom_call_target="tpu_custom_call" | custom-call | tf_op jit(solution)/shard_map/pallas_call | solution.py:634
  27.4 1.1 %collective-permute-start.10 = (s16[160,128]{1,0:T(8,128)(2,1)S(1)}, s16[160,128]{1,0:T(8,128)(2,1)S(1)}, u32[]{:S(2)}, u32[]{:S(2)}) collective-permute-start(s16[160,128]{1,0:T(8,128)(2,1)S(1)} %get-tuple-element.42), channel_id=1, source_target_pairs={{0,3},{1,2},{2,1},{3,0},{4,7},{5,6},{6,5},{7,4},{8,11},{9,10},{10,... | collective-permute-start | bytes 122888 | tf_op jit(solution)/shard_map/ppermute | solution.py:646
  28.5 0.4 collective-permute-start.8
  28.9 0.7 %collective-permute-start.9 = (s16[160,128]{1,0:T(8,128)(2,1)S(1)}, s16[160,128]{1,0:T(8,128)(2,1)S(1)}, u32[]{:S(2)}, u32[]{:S(2)}) collective-permute-start(s16[160,128]{1,0:T(8,128)(2,1)S(1)} %get-tuple-element.41), channel_id=1, source_target_pairs={{0,2},{1,3},{2,0},{3,1},{4,6},{5,7},{6,4},{7,5},{8,10},{9,11},{10,... | collective-permute-start | bytes 122888 | tf_op jit(solution)/shard_map/ppermute | solution.py:646
  29.6 1.4 %collective-permute-done.10.in3 = s16[160,128]{1,0:T(8,128)(2,1)S(1)} collective-permute-done((s16[160,128]{1,0:T(8,128)(2,1)S(1)}, s16[160,128]{1,0:T(8,128)(2,1)S(1)}, u32[]{:S(2)}, u32[]{:S(2)}) %collective-permute-start.10) | collective-permute-done | bytes 40992 | tf_op jit(solution)/shard_map/ppermute | solution.py:646
  31.0 0.0 collective-permute-done.8.in1
  31.0 1.8 %collective-permute-done.9.in2 = s16[160,128]{1,0:T(8,128)(2,1)S(1)} collective-permute-done((s16[160,128]{1,0:T(8,128)(2,1)S(1)}, s16[160,128]{1,0:T(8,128)(2,1)S(1)}, u32[]{:S(2)}, u32[]{:S(2)}) %collective-permute-start.9) | collective-permute-done | bytes 40992 | tf_op jit(solution)/shard_map/ppermute | solution.py:646
  32.9 0.4 shard_map.69
  33.2 1.6 %collective-permute-start.11 = (s16[160,128]{1,0:T(8,128)(2,1)S(1)}, s16[160,128]{1,0:T(8,128)(2,1)S(1)}, u32[]{:S(2)}, u32[]{:S(2)}) collective-permute-start(s16[160,128]{1,0:T(8,128)(2,1)S(1)} %get-tuple-element.43), channel_id=1, source_target_pairs={{0,16},{4,20},{8,24},{12,28},{16,0},{20,4},{24,8},{28,12},{1,17},{... | collective-permute-start | bytes 122888 | tf_op jit(solution)/shard_map/ppermute | solution.py:702
  34.8 0.5 %collective-permute-start.12 = (s16[160,128]{1,0:T(8,128)(2,1)S(1)}, s16[160,128]{1,0:T(8,128)(2,1)S(1)}, u32[]{:S(2)}, u32[]{:S(2)}) collective-permute-start(s16[160,128]{1,0:T(8,128)(2,1)S(1)} %get-tuple-element.44), channel_id=1, source_target_pairs={{0,20},{4,24},{8,28},{12,16},{16,4},{20,8},{24,12},{28,0},{1,21},{... | collective-permute-start | bytes 122888 | tf_op jit(solution)/shard_map/ppermute | solution.py:702
  35.4 3.8 %collective-permute-start.13 = (s16[160,128]{1,0:T(8,128)(2,1)S(1)}, s16[160,128]{1,0:T(8,128)(2,1)S(1)}, u32[]{:S(2)}, u32[]{:S(2)}) collective-permute-start(s16[160,128]{1,0:T(8,128)(2,1)S(1)} %get-tuple-element.45), channel_id=1, source_target_pairs={{0,24},{4,28},{8,16},{12,20},{16,8},{20,12},{24,0},{28,4},{1,25},{... | collective-permute-start | bytes 122888 | tf_op jit(solution)/shard_map/ppermute | solution.py:702
  39.1 0.4 collective-permute-start.14
  39.5 0.0 collective-permute-done.11.in0
  39.5 2.1 %collective-permute-done.12.in1 = s16[160,128]{1,0:T(8,128)(2,1)S(1)} collective-permute-done((s16[160,128]{1,0:T(8,128)(2,1)S(1)}, s16[160,128]{1,0:T(8,128)(2,1)S(1)}, u32[]{:S(2)}, u32[]{:S(2)}) %collective-permute-start.12) | collective-permute-done | bytes 40992 | tf_op jit(solution)/shard_map/ppermute | solution.py:702
  41.7 0.0 collective-permute-done.13.in2
  41.7 2.4 %collective-permute-done.14.in3 = s16[160,128]{1,0:T(8,128)(2,1)S(1)} collective-permute-done((s16[160,128]{1,0:T(8,128)(2,1)S(1)}, s16[160,128]{1,0:T(8,128)(2,1)S(1)}, u32[]{:S(2)}, u32[]{:S(2)}) %collective-permute-start.14) | collective-permute-done | bytes 40992 | tf_op jit(solution)/shard_map/ppermute | solution.py:702
  44.0 0.0 copy-done
  44.0 0.0 copy-done.1
  44.0 0.0 copy-done.2
  44.1 0.9 %shard_map.70 = f32[1,2,19,4,512]{4,3,2,1,0:T(4,128)} custom-call(s16[160,128]{1,0:T(8,128)(2,1)S(1)} %collective-permute-done.11.in0, s16[160,128]{1,0:T(8,128)(2,1)S(1)} %collective-permute-done.12.in1, s16[160,128]{1,0:T(8,128)(2,1)S(1)} %collective-permute-done.13.in2, s16[160,128]{1,0:T(8,128)(2,1)S(1)} %collective-permute-done.14.in3, ...), custom_call_target="tpu_custom_call" | custom-call | tf_op jit(solution)/shard_map/pallas_call | solution.py:634
  (1 shorter events, 0.0 us)
Async XLA Ops:
  0.0 19.3 %copy-start.3 = (bf16[2,76,76]{2,0,1:T(2,128)(2,1)S(1)}, bf16[2,76,76]{2,0,1:T(2,128)(2,1)}, u32[]{:S(2)}) copy-start(bf16[2,76,76]{2,0,1:T(2,128)(2,1)} %param.11) | copy-start | bytes 69316
  1.7 8.5 %collective-permute-start.3 = (s16[720,128]{1,0:T(8,128)(2,1)S(1)}, s16[720,128]{1,0:T(8,128)(2,1)S(1)}, u32[]{:S(2)}, u32[]{:S(2)}) collective-permute-start(s16[720,128]{1,0:T(8,128)(2,1)S(1)} %get-tuple-element.30), channel_id=1, source_target_pairs={{0,2},{1,3},{2,0},{3,1},{4,6},{5,7},{6,4},{7,5},{8,10},{9,11},{10,... | collective-permute-start | bytes 552968 | tf_op jit(solution)/shard_map/ppermute | solution.py:676
  4.7 9.4 %collective-permute-start = (s16[240,128]{1,0:T(8,128)(2,1)S(1)}, s16[240,128]{1,0:T(8,128)(2,1)S(1)}, u32[]{:S(2)}, u32[]{:S(2)}) collective-permute-start(s16[240,128]{1,0:T(8,128)(2,1)S(1)} %get-tuple-element.27), channel_id=1, source_target_pairs={{0,4},{4,8},{8,12},{12,0},{1,5},{5,9},{9,13},{13,1},{2,6},{6,10},{... | collective-permute-start | bytes 184328 | tf_op jit(solution)/shard_map/ppermute | solution.py:653
  6.3 9.2 %collective-permute-start.1 = (s16[240,128]{1,0:T(8,128)(2,1)S(1)}, s16[240,128]{1,0:T(8,128)(2,1)S(1)}, u32[]{:S(2)}, u32[]{:S(2)}) collective-permute-start(s16[240,128]{1,0:T(8,128)(2,1)S(1)} %get-tuple-element.28), channel_id=1, source_target_pairs={{0,8},{4,12},{8,0},{12,4},{1,9},{5,13},{9,1},{13,5},{2,10},{6,14},... | collective-permute-start | bytes 184328 | tf_op jit(solution)/shard_map/ppermute | solution.py:653
  8.9 6.6 %collective-permute-start.2 = (s16[240,128]{1,0:T(8,128)(2,1)S(1)}, s16[240,128]{1,0:T(8,128)(2,1)S(1)}, u32[]{:S(2)}, u32[]{:S(2)}) collective-permute-start(s16[240,128]{1,0:T(8,128)(2,1)S(1)} %get-tuple-element.29), channel_id=1, source_target_pairs={{0,12},{4,0},{8,4},{12,8},{1,13},{5,1},{9,5},{13,9},{2,14},{6,2},{... | collective-permute-start | bytes 184328 | tf_op jit(solution)/shard_map/ppermute | solution.py:653
  10.5 6.3 %collective-permute-start.4 = (s16[240,128]{1,0:T(8,128)(2,1)S(1)}, s16[240,128]{1,0:T(8,128)(2,1)S(1)}, u32[]{:S(2)}, u32[]{:S(2)}) collective-permute-start(s16[240,128]{1,0:T(8,128)(2,1)S(1)} %get-tuple-element.32), channel_id=1, source_target_pairs={{0,4},{4,8},{8,12},{12,0},{1,5},{5,9},{9,13},{13,1},{2,6},{6,10},{... | collective-permute-start | bytes 184328 | tf_op jit(solution)/shard_map/ppermute | solution.py:653
  11.5 7.2 %collective-permute-start.5 = (s16[240,128]{1,0:T(8,128)(2,1)S(1)}, s16[240,128]{1,0:T(8,128)(2,1)S(1)}, u32[]{:S(2)}, u32[]{:S(2)}) collective-permute-start(s16[240,128]{1,0:T(8,128)(2,1)S(1)} %get-tuple-element.33), channel_id=1, source_target_pairs={{0,8},{4,12},{8,0},{12,4},{1,9},{5,13},{9,1},{13,5},{2,10},{6,14},... | collective-permute-start | bytes 184328 | tf_op jit(solution)/shard_map/ppermute | solution.py:653
  14.1 4.7 %collective-permute-start.6 = (s16[240,128]{1,0:T(8,128)(2,1)S(1)}, s16[240,128]{1,0:T(8,128)(2,1)S(1)}, u32[]{:S(2)}, u32[]{:S(2)}) collective-permute-start(s16[240,128]{1,0:T(8,128)(2,1)S(1)} %get-tuple-element.34), channel_id=1, source_target_pairs={{0,12},{4,0},{8,4},{12,8},{1,13},{5,1},{9,5},{13,9},{2,14},{6,2},{... | collective-permute-start | bytes 184328 | tf_op jit(solution)/shard_map/ppermute | solution.py:653
  19.2 24.9 %copy-start = (f32[1,2,19,4,512]{4,3,2,1,0:T(4,128)S(1)}, f32[1,2,19,4,512]{4,3,2,1,0:T(4,128)}, u32[]{:S(2)}) copy-start(f32[1,2,19,4,512]{4,3,2,1,0:T(4,128)} %state.3) | copy-start | bytes 933892
  19.2 24.9 %copy-start.1 = (s32[4,512]{1,0:T(4,128)S(1)}, s32[4,512]{1,0:T(4,128)}, u32[]{:S(2)}) copy-start(s32[4,512]{1,0:T(4,128)} %land_sea.3) | copy-start | bytes 24580
  19.2 24.9 %copy-start.2 = (s32[4,512]{1,0:T(4,128)S(1)}, s32[4,512]{1,0:T(4,128)}, u32[]{:S(2)}) copy-start(s32[4,512]{1,0:T(4,128)} %depth_index.3) | copy-start | bytes 24580
  19.2 1.7 %collective-permute-start.7 = (s16[1280,128]{1,0:T(8,128)(2,1)S(1)}, s16[1280,128]{1,0:T(8,128)(2,1)S(1)}, u32[]{:S(2)}, u32[]{:S(2)}) collective-permute-start(s16[1280,128]{1,0:T(8,128)(2,1)S(1)} %shard_map.66), channel_id=1, source_target_pairs={{0,1},{1,0},{2,3},{3,2},{4,5},{5,4},{6,7},{7,6},{8,9},{9,8},{10,11... | collective-permute-start | bytes 983048 | tf_op jit(solution)/shard_map/ppermute | solution.py:680
  27.4 3.6 %collective-permute-start.10 = (s16[160,128]{1,0:T(8,128)(2,1)S(1)}, s16[160,128]{1,0:T(8,128)(2,1)S(1)}, u32[]{:S(2)}, u32[]{:S(2)}) collective-permute-start(s16[160,128]{1,0:T(8,128)(2,1)S(1)} %get-tuple-element.42), channel_id=1, source_target_pairs={{0,3},{1,2},{2,1},{3,0},{4,7},{5,6},{6,5},{7,4},{8,11},{9,10},{10,... | collective-permute-start | bytes 122888 | tf_op jit(solution)/shard_map/ppermute | solution.py:646
  28.5 2.5 %collective-permute-start.8 = (s16[160,128]{1,0:T(8,128)(2,1)S(1)}, s16[160,128]{1,0:T(8,128)(2,1)S(1)}, u32[]{:S(2)}, u32[]{:S(2)}) collective-permute-start(s16[160,128]{1,0:T(8,128)(2,1)S(1)} %get-tuple-element.40), channel_id=1, source_target_pairs={{0,1},{1,0},{2,3},{3,2},{4,5},{5,4},{6,7},{7,6},{8,9},{9,8},{10,11... | collective-permute-start | bytes 122888 | tf_op jit(solution)/shard_map/ppermute | solution.py:646
  28.9 4.0 %collective-permute-start.9 = (s16[160,128]{1,0:T(8,128)(2,1)S(1)}, s16[160,128]{1,0:T(8,128)(2,1)S(1)}, u32[]{:S(2)}, u32[]{:S(2)}) collective-permute-start(s16[160,128]{1,0:T(8,128)(2,1)S(1)} %get-tuple-element.41), channel_id=1, source_target_pairs={{0,2},{1,3},{2,0},{3,1},{4,6},{5,7},{6,4},{7,5},{8,10},{9,11},{10,... | collective-permute-start | bytes 122888 | tf_op jit(solution)/shard_map/ppermute | solution.py:646
  33.2 6.3 %collective-permute-start.11 = (s16[160,128]{1,0:T(8,128)(2,1)S(1)}, s16[160,128]{1,0:T(8,128)(2,1)S(1)}, u32[]{:S(2)}, u32[]{:S(2)}) collective-permute-start(s16[160,128]{1,0:T(8,128)(2,1)S(1)} %get-tuple-element.43), channel_id=1, source_target_pairs={{0,16},{4,20},{8,24},{12,28},{16,0},{20,4},{24,8},{28,12},{1,17},{... | collective-permute-start | bytes 122888 | tf_op jit(solution)/shard_map/ppermute | solution.py:702
  34.8 6.9 %collective-permute-start.12 = (s16[160,128]{1,0:T(8,128)(2,1)S(1)}, s16[160,128]{1,0:T(8,128)(2,1)S(1)}, u32[]{:S(2)}, u32[]{:S(2)}) collective-permute-start(s16[160,128]{1,0:T(8,128)(2,1)S(1)} %get-tuple-element.44), channel_id=1, source_target_pairs={{0,20},{4,24},{8,28},{12,16},{16,4},{20,8},{24,12},{28,0},{1,21},{... | collective-permute-start | bytes 122888 | tf_op jit(solution)/shard_map/ppermute | solution.py:702
  35.4 6.3 %collective-permute-start.13 = (s16[160,128]{1,0:T(8,128)(2,1)S(1)}, s16[160,128]{1,0:T(8,128)(2,1)S(1)}, u32[]{:S(2)}, u32[]{:S(2)}) collective-permute-start(s16[160,128]{1,0:T(8,128)(2,1)S(1)} %get-tuple-element.45), channel_id=1, source_target_pairs={{0,24},{4,28},{8,16},{12,20},{16,8},{20,12},{24,0},{28,4},{1,25},{... | collective-permute-start | bytes 122888 | tf_op jit(solution)/shard_map/ppermute | solution.py:702
  39.1 4.9 %collective-permute-start.14 = (s16[160,128]{1,0:T(8,128)(2,1)S(1)}, s16[160,128]{1,0:T(8,128)(2,1)S(1)}, u32[]{:S(2)}, u32[]{:S(2)}) collective-permute-start(s16[160,128]{1,0:T(8,128)(2,1)S(1)} %get-tuple-element.46), channel_id=1, source_target_pairs={{0,28},{4,16},{8,20},{12,24},{16,12},{20,0},{24,4},{28,8},{1,29},{... | collective-permute-start | bytes 122888 | tf_op jit(solution)/shard_map/ppermute | solution.py:702

commit v8 on v7

--- a/solution.py
+++ b/solution.py
@@ -292,16 +292,23 @@
     return values.astype(jnp.int32).astype(I16)
 
 
-def levels_of(row, core):
-    level = row + OWN_LEVELS * core + jnp.where(row >= OWN_LEVELS, OWN_LEVELS, 0)
-    return jnp.where(row < 2 * OWN_LEVELS, level, 4 * LEVELS)
-
-
-def level_rows(shape, core):
+def levels_of(row, half):
+    return jnp.where(row < 2 * OWN_LEVELS, row + 2 * OWN_LEVELS * half, 4 * LEVELS)
+
+
+def level_rows(shape, half):
     row = index(shape, 0)
-    return jnp.where(
-        row < HALF, levels_of(row, core), levels_of(row - HALF, 1 - core)
-    )
+    return jnp.where(row < HALF, levels_of(row, half), levels_of(row - HALF, 1 - half))
+
+
+def gather(recv, tiles, others):
+    tile = lax.axis_index("tile")
+    core = lax.axis_index("depth") % CORES
+    for distance, ref in enumerate(tiles):
+        to = CORES * ((tile + TILES - distance) % TILES)
+        for pair in range(FIELDS // 8):
+            recv[to + core, 16 * pair : 16 * pair + 16, :] = piece(ref, pair, core)
+        recv[to + 1 - core] = others[PIECE * distance : PIECE * distance + PIECE, :]
 
 
 def load_half(recv, side, cells, pitch, base, flow, coef, plane, fresh):
@@ -407,36 +414,26 @@
 
 
 def own_kernel(*refs):
-    arrived, (ops, cells, coef, plane, ordered, recv, flow) = refs[: 2 * TILES], refs[2 * TILES :]
-    own = lax.axis_index("depth")
-    tile = lax.axis_index("tile")
-    core, half = own % CORES, own // CORES
-    for i, ref in enumerate(arrived):
-        far, distance = divmod(i, TILES)
-        to = 2 * ((tile + TILES - distance) % TILES) + (half ^ far)
-        for pair in range(FIELDS // 8):
-            recv[to, 16 * pair : 16 * pair + 16, :] = piece(ref, pair, core)
-    load_half(recv, core, cells, HALF, 0, flow, coef, plane, True)
+    tiles, (others, ops, cells, coef, plane, ordered, recv, flow) = refs[:TILES], refs[TILES:]
+    half = lax.axis_index("depth") // CORES
+    gather(recv, tiles, others)
+    load_half(recv, half, cells, HALF, 0, flow, coef, plane, True)
     shape = (PITCH, LEVELS)
-    pick = jnp.where(level_rows(shape, core) == index(shape, 1), 1.0, 0.0).astype(jnp.bfloat16)
+    pick = jnp.where(level_rows(shape, half) == index(shape, 1), 1.0, 0.0).astype(jnp.bfloat16)
     for t in range(2):
         rows = jnp.dot(pick, ops[t], preferred_element_type=F32).astype(jnp.bfloat16)
         both = lax.dot_general(rows, pick, (((1,), (1,)), ((), ())), preferred_element_type=F32)
         ordered[t] = both.astype(jnp.bfloat16)
 
 
-def steps_kernel(
-    others, own_cells, own_coef, plane, ops, out0, out1, out2, out3,
-    recv, cells, firsts, moved, flow, coef, light, ends,
-):
+def steps_kernel(*refs):
+    tiles, refs = refs[:TILES], refs[TILES:]
+    (others, own_cells, own_coef, plane, ops, out0, out1, out2, out3), scratch = refs[:9], refs[9:]
+    recv, cells, firsts, moved, flow, coef, light, ends = scratch
     own = lax.axis_index("depth")
-    tile = lax.axis_index("tile")
     core, half = own % CORES, own // CORES
-    for i in range(2 * TILES):
-        far, distance = divmod(i, TILES)
-        to = 2 * ((tile + TILES - distance) % TILES) + (half ^ far)
-        recv[to] = others[PIECE * i : PIECE * i + PIECE, :]
-    load_half(recv, 1 - core, cells, PITCH, HALF, flow, coef, plane, False)
+    gather(recv, tiles, others)
+    load_half(recv, 1 - half, cells, PITCH, HALF, flow, coef, plane, False)
     for s in range(16):
         cells[PITCH * s : PITCH * s + HALF, :] = own_cells[HALF * s : HALF * s + HALF, :]
     lane = index((8, 128), 1)
@@ -444,7 +441,7 @@
     def block(base, g):
         return slice(base * PITCH + 8 * g, base * PITCH + 8 * g + 8)
 
-    deep = level_rows((PITCH, 128), core).astype(F32)
+    deep = level_rows((PITCH, 128), half).astype(F32)
     light[...] = jnp.exp(deep * (-4.0 / LEVELS))
 
     source_lane, lanes = index((256, 256), 0) % 128, index((256, 256), 1)
@@ -530,7 +527,7 @@
     chunk = lane // 32
 
     def send(n, carry):
-        first = HALF * (n % CORES) + OWN_LEVELS * (half ^ (n // CORES))
+        first = HALF * (n // CORES) + OWN_LEVELS * (core ^ (n % CORES))
         blocks = []
         for t in range(2):
             def level(k):
@@ -674,26 +671,28 @@
         place=lambda *args: args,
     )
     across = lax.ppermute(across, "depth", [(i, i ^ CORES) for i in range(BLOCKS)])
-    received = across_tiles(here)
-    received += across_tiles(call(relay_kernel, [both] * TILES, [sent], across))
-    others = call(core_kernel, pltpu.VMEM((2 * TILES * PIECE, 128), I16), [], *received)
-    others = lax.ppermute(others, "depth", [(i, i ^ 1) for i in range(BLOCKS)])
-    pieces = pltpu.VMEM((2 * TILES, PIECE, 128), I16)
+    loaded = []
+    for messages in (here, call(relay_kernel, [both] * TILES, [sent], across)):
+        tiles = across_tiles(messages)
+        others = call(core_kernel, pltpu.VMEM((TILES * PIECE, 128), I16), [], *tiles)
+        others = lax.ppermute(others, "depth", [(i, i ^ 1) for i in range(BLOCKS)])
+        loaded.append((*tiles, others))
+    pieces = pltpu.VMEM((TILES * CORES, PIECE, 128), I16)
     flow = pltpu.VMEM((2 * 8 * HALF, 128), F32)
     coef = pltpu.VMEM((HALF // 8, 8, 9, 8, 128), F32)
-    loaded = call(
+    near_levels = call(
         own_kernel,
         [flow, coef, pltpu.VMEM((2, 8, 128), F32), pltpu.VMEM((2, PITCH, PITCH), jnp.bfloat16)],
         [pieces, flow],
-        *received,
+        *loaded[0],
         column_ops,
     )
     out = call(
         steps_kernel,
         [message] * 4,
         [pieces, cells, cells, cells, flow, coef, pltpu.VMEM((PITCH, 128), F32), slots],
-        others,
-        *loaded,
+        *loaded[1],
+        *near_levels,
         reserve=16,
     )
     turned = call(turn_kernel, [message] * 4, [slots] * 2, *across_depth(out))

time: 45.1 us -> 44.7 us (level)
  waiting for transfers between devices: 11.7 us -> 10.9 us
    pallas_call x7 -> x8, Pallas kernels: 11.2 us -> 11.3 us  [call(): pl.pallas_call(kernel, out_shape=outs, in_specs=[VMEM] * len(args), out_s...]
  transfers between devices with their start and end apart: 15 -> 16, of which waited for: 8 -> 9; matrix products, arithmetic and copies ran while one was open for 0% -> 0% of each run, Pallas kernels for 3% -> 4%
where the time goes in v8:
time: 44.7 us; the launch traced here: 44.5 us
  starting transfers between devices  22.1 us (49%)
  Pallas kernels  11.3 us (25%)
  waiting for transfers between devices  10.9 us (24%)
    pallas_call x8, Pallas kernels, call(): pl.pallas_call(kernel, out_shape=outs, in_specs=[VMEM] * len(args), out_s...  11.3 us
    ppermute x6, starting transfers between devices, across_tiles(): lax.ppermute(messages[n], 'tile', [(i, (i + n) % TILES) for i in range(TI...  10.4 us
    ppermute x4, starting transfers between devices, window_shards(): lax.ppermute(turned[n], ('seg', 'tile'), [(s * TILES + t, (s + 1) % segs...  6.32 us
    ppermute x4, waiting for transfers between devices, window_shards(): lax.ppermute(turned[n], ('seg', 'tile'), [(s * TILES + t, (s + 1) % segs...  4.5 us
    ppermute x6, waiting for transfers between devices, across_tiles(): lax.ppermute(messages[n], 'tile', [(i, (i + n) % TILES) for i in range(TI...  3.09 us
    ppermute x1, starting transfers between devices, window_shards(): lax.ppermute(across, 'depth', [(i, i ^ CORES) for i in range(BLOCKS)])  3 us
    ppermute x3, waiting for transfers between devices, across_depth(): lax.ppermute(messages[n], 'depth', [(i, i ^ n) for i in range(BLOCKS)])  2.95 us
    ppermute x3, starting transfers between devices, across_depth(): lax.ppermute(messages[n], 'depth', [(i, i ^ n) for i in range(BLOCKS)])  2.21 us
  transfers between devices with their start and end apart: 16, of which 9 were waited for; matrix products, arithmetic and copies ran while one was open for 0% of the time, Pallas kernels for 4%

profile of v8, /device:TPU:0, one launch (start us, length us, event | category | flops | bytes accessed | tf_op | source)
XLA Modules:
  0.0 44.5 jit_solution(3811243689799312772)
XLA Ops:
  0.0 0.0 copy-start.3
  0.0 1.7 %shard_map.64 = (s16[720,128]{1,0:T(8,128)(2,1)S(1)}, s16[240,128]{1,0:T(8,128)(2,1)S(1)}, s16[240,128]{1,0:T(8,128)(2,1)S(1)}, s16[240,128]{1,0:T(8,128)(2,1)S(1)}, s16[240,128]{1,0:T(8,128)(2,1)S(1)}) custom-call(f32[1,2,19,4,512]{4,3,2,1,0:T(4,128)} %state.3, f32[1,2,19,4,512]{4,3,2,1,0:T(4,128)} %velocity.1, f32[1,4,512]{2,1,0:T(4,128)} %growth.1, ...), custom_call_target="tpu_custom_call" | custom-call | tf_op jit(solution)/shard_map/pallas_call | solution.py:631
  1.7 3.0 %collective-permute-start = (s16[720,128]{1,0:T(8,128)(2,1)S(1)}, s16[720,128]{1,0:T(8,128)(2,1)S(1)}, u32[]{:S(2)}, u32[]{:S(2)}) collective-permute-start(s16[720,128]{1,0:T(8,128)(2,1)S(1)} %get-tuple-element.26), channel_id=1, source_target_pairs={{0,2},{1,3},{2,0},{3,1},{4,6},{5,7},{6,4},{7,5},{8,10},{9,11},{10,... | collective-permute-start | bytes 552968 | tf_op jit(solution)/shard_map/ppermute | solution.py:673
  4.7 1.6 %collective-permute-start.5 = (s16[240,128]{1,0:T(8,128)(2,1)S(1)}, s16[240,128]{1,0:T(8,128)(2,1)S(1)}, u32[]{:S(2)}, u32[]{:S(2)}) collective-permute-start(s16[240,128]{1,0:T(8,128)(2,1)S(1)} %get-tuple-element.32), channel_id=1, source_target_pairs={{0,4},{4,8},{8,12},{12,0},{1,5},{5,9},{9,13},{13,1},{2,6},{6,10},{... | collective-permute-start | bytes 184328 | tf_op jit(solution)/shard_map/ppermute | solution.py:650
  6.3 2.6 %collective-permute-start.6 = (s16[240,128]{1,0:T(8,128)(2,1)S(1)}, s16[240,128]{1,0:T(8,128)(2,1)S(1)}, u32[]{:S(2)}, u32[]{:S(2)}) collective-permute-start(s16[240,128]{1,0:T(8,128)(2,1)S(1)} %get-tuple-element.33), channel_id=1, source_target_pairs={{0,8},{4,12},{8,0},{12,4},{1,9},{5,13},{9,1},{13,5},{2,10},{6,14},... | collective-permute-start | bytes 184328 | tf_op jit(solution)/shard_map/ppermute | solution.py:650
  8.9 1.3 %collective-permute-start.7 = (s16[240,128]{1,0:T(8,128)(2,1)S(1)}, s16[240,128]{1,0:T(8,128)(2,1)S(1)}, u32[]{:S(2)}, u32[]{:S(2)}) collective-permute-start(s16[240,128]{1,0:T(8,128)(2,1)S(1)} %get-tuple-element.34), channel_id=1, source_target_pairs={{0,12},{4,0},{8,4},{12,8},{1,13},{5,1},{9,5},{13,9},{2,14},{6,2},{... | collective-permute-start | bytes 184328 | tf_op jit(solution)/shard_map/ppermute | solution.py:650
  10.2 0.0 collective-permute-done.ref
  10.2 0.3 shard_map.65
  10.5 1.0 %collective-permute-start.1 = (s16[240,128]{1,0:T(8,128)(2,1)S(1)}, s16[240,128]{1,0:T(8,128)(2,1)S(1)}, u32[]{:S(2)}, u32[]{:S(2)}) collective-permute-start(s16[240,128]{1,0:T(8,128)(2,1)S(1)} %get-tuple-element.28), channel_id=1, source_target_pairs={{0,4},{4,8},{8,12},{12,0},{1,5},{5,9},{9,13},{13,1},{2,6},{6,10},{... | collective-permute-start | bytes 184328 | tf_op jit(solution)/shard_map/ppermute | solution.py:650
  11.5 2.6 %collective-permute-start.2 = (s16[240,128]{1,0:T(8,128)(2,1)S(1)}, s16[240,128]{1,0:T(8,128)(2,1)S(1)}, u32[]{:S(2)}, u32[]{:S(2)}) collective-permute-start(s16[240,128]{1,0:T(8,128)(2,1)S(1)} %get-tuple-element.29), channel_id=1, source_target_pairs={{0,8},{4,12},{8,0},{12,4},{1,9},{5,13},{9,1},{13,5},{2,10},{6,14},... | collective-permute-start | bytes 184328 | tf_op jit(solution)/shard_map/ppermute | solution.py:650
  14.1 0.0 collective-permute-done.5.refs_1_
  14.1 1.3 %collective-permute-start.3 = (s16[240,128]{1,0:T(8,128)(2,1)S(1)}, s16[240,128]{1,0:T(8,128)(2,1)S(1)}, u32[]{:S(2)}, u32[]{:S(2)}) collective-permute-start(s16[240,128]{1,0:T(8,128)(2,1)S(1)} %get-tuple-element.30), channel_id=1, source_target_pairs={{0,12},{4,0},{8,4},{12,8},{1,13},{5,1},{9,5},{13,9},{2,14},{6,2},{... | collective-permute-start | bytes 184328 | tf_op jit(solution)/shard_map/ppermute | solution.py:650
  15.5 0.0 collective-permute-done.6.refs_2_
  15.5 0.0 collective-permute-done.7.refs_3_
  15.5 0.2 shard_map.67
  15.7 0.1 collective-permute-start.8
  15.7 1.1 %collective-permute-done.1.refs_1_ = s16[240,128]{1,0:T(8,128)(2,1)S(1)} collective-permute-done((s16[240,128]{1,0:T(8,128)(2,1)S(1)}, s16[240,128]{1,0:T(8,128)(2,1)S(1)}, u32[]{:S(2)}, u32[]{:S(2)}) %collective-permute-start.1) | collective-permute-done | bytes 61472 | tf_op jit(solution)/shard_map/ppermute | solution.py:650
  16.8 1.9 %collective-permute-done.2.refs_2_ = s16[240,128]{1,0:T(8,128)(2,1)S(1)} collective-permute-done((s16[240,128]{1,0:T(8,128)(2,1)S(1)}, s16[240,128]{1,0:T(8,128)(2,1)S(1)}, u32[]{:S(2)}, u32[]{:S(2)}) %collective-permute-start.2) | collective-permute-done | bytes 61472 | tf_op jit(solution)/shard_map/ppermute | solution.py:650
  18.7 0.1 collective-permute-done.3.refs_3_
  18.8 0.2 shard_map.66
  19.0 0.0 copy-start
  19.0 0.0 copy-start.1
  19.1 0.0 copy-start.2
  19.1 0.1 collective-permute-start.4
  19.1 0.0 copy-done.3
  19.2 0.0 collective-permute-done.8.refs_4_
  19.2 0.9 %shard_map.68 = (f32[640,128]{1,0:T(8,128)S(1)}, f32[5,8,9,8,128]{4,3,2,1,0:T(8,128)S(1)}, f32[2,8,128]{2,1,0:T(8,128)S(1)}, bf16[2,80,80]{2,1,0:T(8,128)(2,1)S(1)}) custom-call(s16[240,128]{1,0:T(8,128)(2,1)S(1)} %get-tuple-element.31.refs_0_, s16[240,128]{1,0:T(8,128)(2,1)S(1)} %collective-permute-done.5.refs_1_, ...), custom_call_target="tpu_custom_call" | custom-call | tf_op jit(solution)/shard_map/pallas_call | solution.py:631
  20.1 0.4 collective-permute-done.4.refs_4_
  20.5 6.7 %shard_map.69 = (s16[160,128]{1,0:T(8,128)(2,1)S(1)}, s16[160,128]{1,0:T(8,128)(2,1)S(1)}, s16[160,128]{1,0:T(8,128)(2,1)S(1)}, s16[160,128]{1,0:T(8,128)(2,1)S(1)}) custom-call(s16[240,128]{1,0:T(8,128)(2,1)S(1)} %get-tuple-element.27.refs_0_, s16[240,128]{1,0:T(8,128)(2,1)S(1)} %collective-permute-done.1.refs_1_, ...), custom_call_target="tpu_custom_call" | custom-call | tf_op jit(solution)/shard_map/pallas_call | solution.py:631
  27.2 1.3 %collective-permute-start.10 = (s16[160,128]{1,0:T(8,128)(2,1)S(1)}, s16[160,128]{1,0:T(8,128)(2,1)S(1)}, u32[]{:S(2)}, u32[]{:S(2)}) collective-permute-start(s16[160,128]{1,0:T(8,128)(2,1)S(1)} %get-tuple-element.41), channel_id=1, source_target_pairs={{0,2},{1,3},{2,0},{3,1},{4,6},{5,7},{6,4},{7,5},{8,10},{9,11},{10,... | collective-permute-start | bytes 122888 | tf_op jit(solution)/shard_map/ppermute | solution.py:643
  28.6 0.2 collective-permute-start.11
  28.8 0.6 %collective-permute-start.9 = (s16[160,128]{1,0:T(8,128)(2,1)S(1)}, s16[160,128]{1,0:T(8,128)(2,1)S(1)}, u32[]{:S(2)}, u32[]{:S(2)}) collective-permute-start(s16[160,128]{1,0:T(8,128)(2,1)S(1)} %get-tuple-element.40), channel_id=1, source_target_pairs={{0,1},{1,0},{2,3},{3,2},{4,5},{5,4},{6,7},{7,6},{8,9},{9,8},{10,11... | collective-permute-start | bytes 122888 | tf_op jit(solution)/shard_map/ppermute | solution.py:643
  29.4 1.9 %collective-permute-done.10.in2 = s16[160,128]{1,0:T(8,128)(2,1)S(1)} collective-permute-done((s16[160,128]{1,0:T(8,128)(2,1)S(1)}, s16[160,128]{1,0:T(8,128)(2,1)S(1)}, u32[]{:S(2)}, u32[]{:S(2)}) %collective-permute-start.10) | collective-permute-done | bytes 40992 | tf_op jit(solution)/shard_map/ppermute | solution.py:643
  31.3 1.1 %collective-permute-done.11.in3 = s16[160,128]{1,0:T(8,128)(2,1)S(1)} collective-permute-done((s16[160,128]{1,0:T(8,128)(2,1)S(1)}, s16[160,128]{1,0:T(8,128)(2,1)S(1)}, u32[]{:S(2)}, u32[]{:S(2)}) %collective-permute-start.11) | collective-permute-done | bytes 40992 | tf_op jit(solution)/shard_map/ppermute | solution.py:643
  32.4 0.0 collective-permute-done.9.in1
  32.4 0.4 shard_map.70
  32.8 1.6 %collective-permute-start.12 = (s16[160,128]{1,0:T(8,128)(2,1)S(1)}, s16[160,128]{1,0:T(8,128)(2,1)S(1)}, u32[]{:S(2)}, u32[]{:S(2)}) collective-permute-start(s16[160,128]{1,0:T(8,128)(2,1)S(1)} %get-tuple-element.43), channel_id=1, source_target_pairs={{0,16},{4,20},{8,24},{12,28},{16,0},{20,4},{24,8},{28,12},{1,17},{... | collective-permute-start | bytes 122888 | tf_op jit(solution)/shard_map/ppermute | solution.py:701
  34.4 0.6 %collective-permute-start.13 = (s16[160,128]{1,0:T(8,128)(2,1)S(1)}, s16[160,128]{1,0:T(8,128)(2,1)S(1)}, u32[]{:S(2)}, u32[]{:S(2)}) collective-permute-start(s16[160,128]{1,0:T(8,128)(2,1)S(1)} %get-tuple-element.44), channel_id=1, source_target_pairs={{0,20},{4,24},{8,28},{12,16},{16,4},{20,8},{24,12},{28,0},{1,21},{... | collective-permute-start | bytes 122888 | tf_op jit(solution)/shard_map/ppermute | solution.py:701
  34.9 3.7 %collective-permute-start.14 = (s16[160,128]{1,0:T(8,128)(2,1)S(1)}, s16[160,128]{1,0:T(8,128)(2,1)S(1)}, u32[]{:S(2)}, u32[]{:S(2)}) collective-permute-start(s16[160,128]{1,0:T(8,128)(2,1)S(1)} %get-tuple-element.45), channel_id=1, source_target_pairs={{0,24},{4,28},{8,16},{12,20},{16,8},{20,12},{24,0},{28,4},{1,25},{... | collective-permute-start | bytes 122888 | tf_op jit(solution)/shard_map/ppermute | solution.py:701
  38.7 0.4 collective-permute-start.15
  39.1 0.0 collective-permute-done.12.in0
  39.1 2.1 %collective-permute-done.13.in1 = s16[160,128]{1,0:T(8,128)(2,1)S(1)} collective-permute-done((s16[160,128]{1,0:T(8,128)(2,1)S(1)}, s16[160,128]{1,0:T(8,128)(2,1)S(1)}, u32[]{:S(2)}, u32[]{:S(2)}) %collective-permute-start.13) | collective-permute-done | bytes 40992 | tf_op jit(solution)/shard_map/ppermute | solution.py:701
  41.2 0.2 collective-permute-done.14.in2
  41.4 2.2 %collective-permute-done.15.in3 = s16[160,128]{1,0:T(8,128)(2,1)S(1)} collective-permute-done((s16[160,128]{1,0:T(8,128)(2,1)S(1)}, s16[160,128]{1,0:T(8,128)(2,1)S(1)}, u32[]{:S(2)}, u32[]{:S(2)}) %collective-permute-start.15) | collective-permute-done | bytes 40992 | tf_op jit(solution)/shard_map/ppermute | solution.py:701
  43.6 0.0 copy-done
  43.6 0.0 copy-done.1
  43.6 0.0 copy-done.2
  43.6 0.9 %shard_map.71 = f32[1,2,19,4,512]{4,3,2,1,0:T(4,128)} custom-call(s16[160,128]{1,0:T(8,128)(2,1)S(1)} %collective-permute-done.12.in0, s16[160,128]{1,0:T(8,128)(2,1)S(1)} %collective-permute-done.13.in1, s16[160,128]{1,0:T(8,128)(2,1)S(1)} %collective-permute-done.14.in2, s16[160,128]{1,0:T(8,128)(2,1)S(1)} %collective-permute-done.15.in3, ...), custom_call_target="tpu_custom_call" | custom-call | tf_op jit(solution)/shard_map/pallas_call | solution.py:631
  (1 shorter events, 0.0 us)
Async XLA Ops:
  0.0 19.1 %copy-start.3 = (bf16[2,76,76]{2,0,1:T(2,128)(2,1)S(1)}, bf16[2,76,76]{2,0,1:T(2,128)(2,1)}, u32[]{:S(2)}) copy-start(bf16[2,76,76]{2,0,1:T(2,128)(2,1)} %param.11) | copy-start | bytes 69316
  1.7 8.5 %collective-permute-start = (s16[720,128]{1,0:T(8,128)(2,1)S(1)}, s16[720,128]{1,0:T(8,128)(2,1)S(1)}, u32[]{:S(2)}, u32[]{:S(2)}) collective-permute-start(s16[720,128]{1,0:T(8,128)(2,1)S(1)} %get-tuple-element.26), channel_id=1, source_target_pairs={{0,2},{1,3},{2,0},{3,1},{4,6},{5,7},{6,4},{7,5},{8,10},{9,11},{10,... | collective-permute-start | bytes 552968 | tf_op jit(solution)/shard_map/ppermute | solution.py:673
  4.7 9.4 %collective-permute-start.5 = (s16[240,128]{1,0:T(8,128)(2,1)S(1)}, s16[240,128]{1,0:T(8,128)(2,1)S(1)}, u32[]{:S(2)}, u32[]{:S(2)}) collective-permute-start(s16[240,128]{1,0:T(8,128)(2,1)S(1)} %get-tuple-element.32), channel_id=1, source_target_pairs={{0,4},{4,8},{8,12},{12,0},{1,5},{5,9},{9,13},{13,1},{2,6},{6,10},{... | collective-permute-start | bytes 184328 | tf_op jit(solution)/shard_map/ppermute | solution.py:650
  6.3 9.2 %collective-permute-start.6 = (s16[240,128]{1,0:T(8,128)(2,1)S(1)}, s16[240,128]{1,0:T(8,128)(2,1)S(1)}, u32[]{:S(2)}, u32[]{:S(2)}) collective-permute-start(s16[240,128]{1,0:T(8,128)(2,1)S(1)} %get-tuple-element.33), channel_id=1, source_target_pairs={{0,8},{4,12},{8,0},{12,4},{1,9},{5,13},{9,1},{13,5},{2,10},{6,14},... | collective-permute-start | bytes 184328 | tf_op jit(solution)/shard_map/ppermute | solution.py:650
  8.9 6.6 %collective-permute-start.7 = (s16[240,128]{1,0:T(8,128)(2,1)S(1)}, s16[240,128]{1,0:T(8,128)(2,1)S(1)}, u32[]{:S(2)}, u32[]{:S(2)}) collective-permute-start(s16[240,128]{1,0:T(8,128)(2,1)S(1)} %get-tuple-element.34), channel_id=1, source_target_pairs={{0,12},{4,0},{8,4},{12,8},{1,13},{5,1},{9,5},{13,9},{2,14},{6,2},{... | collective-permute-start | bytes 184328 | tf_op jit(solution)/shard_map/ppermute | solution.py:650
  10.5 6.3 %collective-permute-start.1 = (s16[240,128]{1,0:T(8,128)(2,1)S(1)}, s16[240,128]{1,0:T(8,128)(2,1)S(1)}, u32[]{:S(2)}, u32[]{:S(2)}) collective-permute-start(s16[240,128]{1,0:T(8,128)(2,1)S(1)} %get-tuple-element.28), channel_id=1, source_target_pairs={{0,4},{4,8},{8,12},{12,0},{1,5},{5,9},{9,13},{13,1},{2,6},{6,10},{... | collective-permute-start | bytes 184328 | tf_op jit(solution)/shard_map/ppermute | solution.py:650
  11.5 7.2 %collective-permute-start.2 = (s16[240,128]{1,0:T(8,128)(2,1)S(1)}, s16[240,128]{1,0:T(8,128)(2,1)S(1)}, u32[]{:S(2)}, u32[]{:S(2)}) collective-permute-start(s16[240,128]{1,0:T(8,128)(2,1)S(1)} %get-tuple-element.29), channel_id=1, source_target_pairs={{0,8},{4,12},{8,0},{12,4},{1,9},{5,13},{9,1},{13,5},{2,10},{6,14},... | collective-permute-start | bytes 184328 | tf_op jit(solution)/shard_map/ppermute | solution.py:650
  14.1 4.7 %collective-permute-start.3 = (s16[240,128]{1,0:T(8,128)(2,1)S(1)}, s16[240,128]{1,0:T(8,128)(2,1)S(1)}, u32[]{:S(2)}, u32[]{:S(2)}) collective-permute-start(s16[240,128]{1,0:T(8,128)(2,1)S(1)} %get-tuple-element.30), channel_id=1, source_target_pairs={{0,12},{4,0},{8,4},{12,8},{1,13},{5,1},{9,5},{13,9},{2,14},{6,2},{... | collective-permute-start | bytes 184328 | tf_op jit(solution)/shard_map/ppermute | solution.py:650
  15.7 3.5 %collective-permute-start.8 = (s16[640,128]{1,0:T(8,128)(2,1)S(1)}, s16[640,128]{1,0:T(8,128)(2,1)S(1)}, u32[]{:S(2)}, u32[]{:S(2)}) collective-permute-start(s16[640,128]{1,0:T(8,128)(2,1)S(1)} %shard_map.67), channel_id=1, source_target_pairs={{0,1},{1,0},{2,3},{3,2},{4,5},{5,4},{6,7},{7,6},{8,9},{9,8},{10,11... | collective-permute-start | bytes 491528 | tf_op jit(solution)/shard_map/ppermute | solution.py:678
  19.0 24.6 %copy-start = (f32[1,2,19,4,512]{4,3,2,1,0:T(4,128)S(1)}, f32[1,2,19,4,512]{4,3,2,1,0:T(4,128)}, u32[]{:S(2)}) copy-start(f32[1,2,19,4,512]{4,3,2,1,0:T(4,128)} %state.3) | copy-start | bytes 933892
  19.0 24.6 %copy-start.1 = (s32[4,512]{1,0:T(4,128)S(1)}, s32[4,512]{1,0:T(4,128)}, u32[]{:S(2)}) copy-start(s32[4,512]{1,0:T(4,128)} %land_sea.3) | copy-start | bytes 24580
  19.1 24.5 %copy-start.2 = (s32[4,512]{1,0:T(4,128)S(1)}, s32[4,512]{1,0:T(4,128)}, u32[]{:S(2)}) copy-start(s32[4,512]{1,0:T(4,128)} %depth_index.3) | copy-start | bytes 24580
  19.1 1.5 %collective-permute-start.4 = (s16[640,128]{1,0:T(8,128)(2,1)S(1)}, s16[640,128]{1,0:T(8,128)(2,1)S(1)}, u32[]{:S(2)}, u32[]{:S(2)}) collective-permute-start(s16[640,128]{1,0:T(8,128)(2,1)S(1)} %shard_map.66), channel_id=1, source_target_pairs={{0,1},{1,0},{2,3},{3,2},{4,5},{5,4},{6,7},{7,6},{8,9},{9,8},{10,11... | collective-permute-start | bytes 491528 | tf_op jit(solution)/shard_map/ppermute | solution.py:678
  27.2 4.1 %collective-permute-start.10 = (s16[160,128]{1,0:T(8,128)(2,1)S(1)}, s16[160,128]{1,0:T(8,128)(2,1)S(1)}, u32[]{:S(2)}, u32[]{:S(2)}) collective-permute-start(s16[160,128]{1,0:T(8,128)(2,1)S(1)} %get-tuple-element.41), channel_id=1, source_target_pairs={{0,2},{1,3},{2,0},{3,1},{4,6},{5,7},{6,4},{7,5},{8,10},{9,11},{10,... | collective-permute-start | bytes 122888 | tf_op jit(solution)/shard_map/ppermute | solution.py:643
  28.6 3.8 %collective-permute-start.11 = (s16[160,128]{1,0:T(8,128)(2,1)S(1)}, s16[160,128]{1,0:T(8,128)(2,1)S(1)}, u32[]{:S(2)}, u32[]{:S(2)}) collective-permute-start(s16[160,128]{1,0:T(8,128)(2,1)S(1)} %get-tuple-element.42), channel_id=1, source_target_pairs={{0,3},{1,2},{2,1},{3,0},{4,7},{5,6},{6,5},{7,4},{8,11},{9,10},{10,... | collective-permute-start | bytes 122888 | tf_op jit(solution)/shard_map/ppermute | solution.py:643
  28.8 3.6 %collective-permute-start.9 = (s16[160,128]{1,0:T(8,128)(2,1)S(1)}, s16[160,128]{1,0:T(8,128)(2,1)S(1)}, u32[]{:S(2)}, u32[]{:S(2)}) collective-permute-start(s16[160,128]{1,0:T(8,128)(2,1)S(1)} %get-tuple-element.40), channel_id=1, source_target_pairs={{0,1},{1,0},{2,3},{3,2},{4,5},{5,4},{6,7},{7,6},{8,9},{9,8},{10,11... | collective-permute-start | bytes 122888 | tf_op jit(solution)/shard_map/ppermute | solution.py:643
  32.8 6.3 %collective-permute-start.12 = (s16[160,128]{1,0:T(8,128)(2,1)S(1)}, s16[160,128]{1,0:T(8,128)(2,1)S(1)}, u32[]{:S(2)}, u32[]{:S(2)}) collective-permute-start(s16[160,128]{1,0:T(8,128)(2,1)S(1)} %get-tuple-element.43), channel_id=1, source_target_pairs={{0,16},{4,20},{8,24},{12,28},{16,0},{20,4},{24,8},{28,12},{1,17},{... | collective-permute-start | bytes 122888 | tf_op jit(solution)/shard_map/ppermute | solution.py:701
  34.4 6.8 %collective-permute-start.13 = (s16[160,128]{1,0:T(8,128)(2,1)S(1)}, s16[160,128]{1,0:T(8,128)(2,1)S(1)}, u32[]{:S(2)}, u32[]{:S(2)}) collective-permute-start(s16[160,128]{1,0:T(8,128)(2,1)S(1)} %get-tuple-element.44), channel_id=1, source_target_pairs={{0,20},{4,24},{8,28},{12,16},{16,4},{20,8},{24,12},{28,0},{1,21},{... | collective-permute-start | bytes 122888 | tf_op jit(solution)/shard_map/ppermute | solution.py:701
  34.9 6.4 %collective-permute-start.14 = (s16[160,128]{1,0:T(8,128)(2,1)S(1)}, s16[160,128]{1,0:T(8,128)(2,1)S(1)}, u32[]{:S(2)}, u32[]{:S(2)}) collective-permute-start(s16[160,128]{1,0:T(8,128)(2,1)S(1)} %get-tuple-element.45), channel_id=1, source_target_pairs={{0,24},{4,28},{8,16},{12,20},{16,8},{20,12},{24,0},{28,4},{1,25},{... | collective-permute-start | bytes 122888 | tf_op jit(solution)/shard_map/ppermute | solution.py:701
  38.7 4.9 %collective-permute-start.15 = (s16[160,128]{1,0:T(8,128)(2,1)S(1)}, s16[160,128]{1,0:T(8,128)(2,1)S(1)}, u32[]{:S(2)}, u32[]{:S(2)}) collective-permute-start(s16[160,128]{1,0:T(8,128)(2,1)S(1)} %get-tuple-element.46), channel_id=1, source_target_pairs={{0,28},{4,16},{8,20},{12,24},{16,12},{20,0},{24,4},{28,8},{1,29},{... | collective-permute-start | bytes 122888 | tf_op jit(solution)/shard_map/ppermute | solution.py:701

commit v9 on v8

--- a/solution.py
+++ b/solution.py
@@ -154,7 +154,7 @@
 
 
 def exponent(largest):
-    return jnp.clip(jnp.ceil(jnp.log2(jnp.maximum(largest, 1e-36))), -119.0, 125.0)
+    return jnp.clip(jnp.ceil(jnp.log2(jnp.maximum(largest, 1e-30))), -99.0, 125.0)
 
 
 def index(shape, dim):
@@ -458,48 +458,52 @@
             + (c[1] * two[0] + c[4] * two[1])
         )
 
-    def stage(source, g, emit):
-        def at(t, s):
+    def stage(source, gs, emit):
+        def at(t, s, g):
             return source[block(8 * t + s, g), :]
 
-        rows = jnp.concatenate([at(t, s) for t in range(2) for s in range(8)], axis=0)
+        rows = jnp.concatenate(
+            [at(t, s, g) for g in gs for t in range(2) for s in range(8)], axis=0
+        )
         high = rows.astype(jnp.bfloat16)
         low = (rows - high.astype(F32)).astype(jnp.bfloat16)
         moves = jnp.dot(jnp.concatenate([high, low], axis=1), shifts, preferred_element_type=F32)
-
-        columns = []
-        for t in range(2):
-            inner = [at(t, s) for s in range(8)]
-            turned = [pltpu.roll(inner[s], 64, 1) for s in (6, 7, 0, 1)]
-            columns.append(turned[:2] + inner + turned[2:])
-        for s in range(8):
-            stencil = own_coef.at[g, s] if g < HALF // 8 else coef.at[g - HALF // 8, s]
-            c = [stencil[i] for i in range(9)]
+        for i, g in enumerate(gs):
+            columns = []
             for t in range(2):
-                k = columns[t]
-                row = slice(8 * (8 * t + s), 8 * (8 * t + s) + 8)
-                two = moves[row, :128], moves[row, 128:]
-                emit(t, s, combine(c, k[s + 1 : s + 4], (k[s], k[s + 4]), two))
-
-    def first_stage(g):
-        def emit(t, s, value):
+                inner = [at(t, s, g) for s in range(8)]
+                turned = [pltpu.roll(inner[s], 64, 1) for s in (6, 7, 0, 1)]
+                columns.append(turned[:2] + inner + turned[2:])
+            for s in range(8):
+                stencil = own_coef.at[g, s] if g < HALF // 8 else coef.at[g - HALF // 8, s]
+                c = [stencil[i] for i in range(9)]
+                for t in range(2):
+                    k = columns[t]
+                    first = 128 * i + 8 * (8 * t + s)
+                    row = slice(first, first + 8)
+                    two = moves[row, :128], moves[row, 128:]
+                    emit(t, s, g, combine(c, k[s + 1 : s + 4], (k[s], k[s + 4]), two))
+
+    def first_stage(gs):
+        def emit(t, s, g, value):
             firsts[block(8 * t + s, g), :] = value
 
-        stage(cells, g, emit)
-
-    def second_stage(g):
-        def emit(t, s, value):
+        stage(cells, gs, emit)
+
+    def second_stage(gs):
+        def emit(t, s, g, value):
             at = block(8 * t + s, g)
             moved[at, :] = 0.5 * (cells[at, :] + value)
 
-        stage(firsts, g, emit)
+        stage(firsts, gs, emit)
 
     def step(n, carry):
-        for g in range(PITCH // 8 + 1):
-            if g < PITCH // 8:
-                first_stage(g)
-            if g > 0:
-                second_stage(g - 1)
+        sets = [tuple(range(g, g + 2)) for g in range(0, PITCH // 8, 2)]
+        for i in range(len(sets) + 1):
+            if i < len(sets):
+                first_stage(sets[i])
+            if i > 0:
+                second_stage(sets[i - 1])
         for pair in range(4):
             mixed = []
             for t in range(2):

time: 44.7 us -> 44.5 us (level)
  no operation moved by 1% of the time
where the time goes in v9:
time: 44.5 us; the launch traced here: 44.4 us
  starting transfers between devices  22.1 us (50%)
  Pallas kernels  11.2 us (25%)
  waiting for transfers between devices  11 us (25%)
    pallas_call x8, Pallas kernels, call(): pl.pallas_call(kernel, out_shape=outs, in_specs=[VMEM] * len(args), out_s...  11.2 us
    ppermute x6, starting transfers between devices, across_tiles(): lax.ppermute(messages[n], 'tile', [(i, (i + n) % TILES) for i in range(TI...  10.4 us
    ppermute x4, starting transfers between devices, window_shards(): lax.ppermute(turned[n], ('seg', 'tile'), [(s * TILES + t, (s + 1) % segs...  6.31 us
    ppermute x4, waiting for transfers between devices, window_shards(): lax.ppermute(turned[n], ('seg', 'tile'), [(s * TILES + t, (s + 1) % segs...  4.5 us
    ppermute x6, waiting for transfers between devices, across_tiles(): lax.ppermute(messages[n], 'tile', [(i, (i + n) % TILES) for i in range(TI...  3.09 us
    ppermute x1, starting transfers between devices, window_shards(): lax.ppermute(across, 'depth', [(i, i ^ CORES) for i in range(BLOCKS)])  3 us
    ppermute x3, waiting for transfers between devices, across_depth(): lax.ppermute(messages[n], 'depth', [(i, i ^ n) for i in range(BLOCKS)])  2.95 us
    ppermute x3, starting transfers between devices, across_depth(): lax.ppermute(messages[n], 'depth', [(i, i ^ n) for i in range(BLOCKS)])  2.21 us
  transfers between devices with their start and end apart: 16, of which 9 were waited for; matrix products, arithmetic and copies ran while one was open for 0% of the time, Pallas kernels for 4%

profile of v9, /device:TPU:0, one launch (start us, length us, event | category | flops | bytes accessed | tf_op | source)
XLA Modules:
  0.0 44.4 jit_solution(3460852131357377512)
XLA Ops:
  0.0 0.0 copy-start.3
  0.0 1.7 %shard_map.64 = (s16[720,128]{1,0:T(8,128)(2,1)S(1)}, s16[240,128]{1,0:T(8,128)(2,1)S(1)}, s16[240,128]{1,0:T(8,128)(2,1)S(1)}, s16[240,128]{1,0:T(8,128)(2,1)S(1)}, s16[240,128]{1,0:T(8,128)(2,1)S(1)}) custom-call(f32[1,2,19,4,512]{4,3,2,1,0:T(4,128)} %state.3, f32[1,2,19,4,512]{4,3,2,1,0:T(4,128)} %velocity.1, f32[1,4,512]{2,1,0:T(4,128)} %growth.1, ...), custom_call_target="tpu_custom_call" | custom-call | tf_op jit(solution)/shard_map/pallas_call | solution.py:635
  1.7 3.0 %collective-permute-start = (s16[720,128]{1,0:T(8,128)(2,1)S(1)}, s16[720,128]{1,0:T(8,128)(2,1)S(1)}, u32[]{:S(2)}, u32[]{:S(2)}) collective-permute-start(s16[720,128]{1,0:T(8,128)(2,1)S(1)} %get-tuple-element.26), channel_id=1, source_target_pairs={{0,2},{1,3},{2,0},{3,1},{4,6},{5,7},{6,4},{7,5},{8,10},{9,11},{10,... | collective-permute-start | bytes 552968 | tf_op jit(solution)/shard_map/ppermute | solution.py:677
  4.7 1.6 %collective-permute-start.5 = (s16[240,128]{1,0:T(8,128)(2,1)S(1)}, s16[240,128]{1,0:T(8,128)(2,1)S(1)}, u32[]{:S(2)}, u32[]{:S(2)}) collective-permute-start(s16[240,128]{1,0:T(8,128)(2,1)S(1)} %get-tuple-element.32), channel_id=1, source_target_pairs={{0,4},{4,8},{8,12},{12,0},{1,5},{5,9},{9,13},{13,1},{2,6},{6,10},{... | collective-permute-start | bytes 184328 | tf_op jit(solution)/shard_map/ppermute | solution.py:654
  6.3 2.6 %collective-permute-start.6 = (s16[240,128]{1,0:T(8,128)(2,1)S(1)}, s16[240,128]{1,0:T(8,128)(2,1)S(1)}, u32[]{:S(2)}, u32[]{:S(2)}) collective-permute-start(s16[240,128]{1,0:T(8,128)(2,1)S(1)} %get-tuple-element.33), channel_id=1, source_target_pairs={{0,8},{4,12},{8,0},{12,4},{1,9},{5,13},{9,1},{13,5},{2,10},{6,14},... | collective-permute-start | bytes 184328 | tf_op jit(solution)/shard_map/ppermute | solution.py:654
  8.9 1.3 %collective-permute-start.7 = (s16[240,128]{1,0:T(8,128)(2,1)S(1)}, s16[240,128]{1,0:T(8,128)(2,1)S(1)}, u32[]{:S(2)}, u32[]{:S(2)}) collective-permute-start(s16[240,128]{1,0:T(8,128)(2,1)S(1)} %get-tuple-element.34), channel_id=1, source_target_pairs={{0,12},{4,0},{8,4},{12,8},{1,13},{5,1},{9,5},{13,9},{2,14},{6,2},{... | collective-permute-start | bytes 184328 | tf_op jit(solution)/shard_map/ppermute | solution.py:654
  10.2 0.0 collective-permute-done.ref
  10.2 0.3 shard_map.65
  10.5 1.0 %collective-permute-start.1 = (s16[240,128]{1,0:T(8,128)(2,1)S(1)}, s16[240,128]{1,0:T(8,128)(2,1)S(1)}, u32[]{:S(2)}, u32[]{:S(2)}) collective-permute-start(s16[240,128]{1,0:T(8,128)(2,1)S(1)} %get-tuple-element.28), channel_id=1, source_target_pairs={{0,4},{4,8},{8,12},{12,0},{1,5},{5,9},{9,13},{13,1},{2,6},{6,10},{... | collective-permute-start | bytes 184328 | tf_op jit(solution)/shard_map/ppermute | solution.py:654
  11.5 2.6 %collective-permute-start.2 = (s16[240,128]{1,0:T(8,128)(2,1)S(1)}, s16[240,128]{1,0:T(8,128)(2,1)S(1)}, u32[]{:S(2)}, u32[]{:S(2)}) collective-permute-start(s16[240,128]{1,0:T(8,128)(2,1)S(1)} %get-tuple-element.29), channel_id=1, source_target_pairs={{0,8},{4,12},{8,0},{12,4},{1,9},{5,13},{9,1},{13,5},{2,10},{6,14},... | collective-permute-start | bytes 184328 | tf_op jit(solution)/shard_map/ppermute | solution.py:654
  14.1 0.0 collective-permute-done.5.refs_1_
  14.1 1.3 %collective-permute-start.3 = (s16[240,128]{1,0:T(8,128)(2,1)S(1)}, s16[240,128]{1,0:T(8,128)(2,1)S(1)}, u32[]{:S(2)}, u32[]{:S(2)}) collective-permute-start(s16[240,128]{1,0:T(8,128)(2,1)S(1)} %get-tuple-element.30), channel_id=1, source_target_pairs={{0,12},{4,0},{8,4},{12,8},{1,13},{5,1},{9,5},{13,9},{2,14},{6,2},{... | collective-permute-start | bytes 184328 | tf_op jit(solution)/shard_map/ppermute | solution.py:654
  15.5 0.0 collective-permute-done.6.refs_2_
  15.5 0.0 collective-permute-done.7.refs_3_
  15.5 0.2 shard_map.67
  15.7 0.1 collective-permute-start.8
  15.7 1.1 %collective-permute-done.1.refs_1_ = s16[240,128]{1,0:T(8,128)(2,1)S(1)} collective-permute-done((s16[240,128]{1,0:T(8,128)(2,1)S(1)}, s16[240,128]{1,0:T(8,128)(2,1)S(1)}, u32[]{:S(2)}, u32[]{:S(2)}) %collective-permute-start.1) | collective-permute-done | bytes 61472 | tf_op jit(solution)/shard_map/ppermute | solution.py:654
  16.8 1.9 %collective-permute-done.2.refs_2_ = s16[240,128]{1,0:T(8,128)(2,1)S(1)} collective-permute-done((s16[240,128]{1,0:T(8,128)(2,1)S(1)}, s16[240,128]{1,0:T(8,128)(2,1)S(1)}, u32[]{:S(2)}, u32[]{:S(2)}) %collective-permute-start.2) | collective-permute-done | bytes 61472 | tf_op jit(solution)/shard_map/ppermute | solution.py:654
  18.7 0.1 collective-permute-done.3.refs_3_
  18.8 0.2 shard_map.66
  19.0 0.0 copy-start
  19.0 0.0 copy-start.1
  19.1 0.0 copy-start.2
  19.1 0.1 collective-permute-start.4
  19.1 0.0 copy-done.3
  19.2 0.0 collective-permute-done.8.refs_4_
  19.2 0.9 %shard_map.68 = (f32[640,128]{1,0:T(8,128)S(1)}, f32[5,8,9,8,128]{4,3,2,1,0:T(8,128)S(1)}, f32[2,8,128]{2,1,0:T(8,128)S(1)}, bf16[2,80,80]{2,1,0:T(8,128)(2,1)S(1)}) custom-call(s16[240,128]{1,0:T(8,128)(2,1)S(1)} %get-tuple-element.31.refs_0_, s16[240,128]{1,0:T(8,128)(2,1)S(1)} %collective-permute-done.5.refs_1_, ...), custom_call_target="tpu_custom_call" | custom-call | tf_op jit(solution)/shard_map/pallas_call | solution.py:635
  20.1 0.4 collective-permute-done.4.refs_4_
  20.5 6.6 %shard_map.69 = (s16[160,128]{1,0:T(8,128)(2,1)S(1)}, s16[160,128]{1,0:T(8,128)(2,1)S(1)}, s16[160,128]{1,0:T(8,128)(2,1)S(1)}, s16[160,128]{1,0:T(8,128)(2,1)S(1)}) custom-call(s16[240,128]{1,0:T(8,128)(2,1)S(1)} %get-tuple-element.27.refs_0_, s16[240,128]{1,0:T(8,128)(2,1)S(1)} %collective-permute-done.1.refs_1_, ...), custom_call_target="tpu_custom_call" | custom-call | tf_op jit(solution)/shard_map/pallas_call | solution.py:635
  27.1 1.3 %collective-permute-start.10 = (s16[160,128]{1,0:T(8,128)(2,1)S(1)}, s16[160,128]{1,0:T(8,128)(2,1)S(1)}, u32[]{:S(2)}, u32[]{:S(2)}) collective-permute-start(s16[160,128]{1,0:T(8,128)(2,1)S(1)} %get-tuple-element.41), channel_id=1, source_target_pairs={{0,2},{1,3},{2,0},{3,1},{4,6},{5,7},{6,4},{7,5},{8,10},{9,11},{10,... | collective-permute-start | bytes 122888 | tf_op jit(solution)/shard_map/ppermute | solution.py:647
  28.4 0.2 collective-permute-start.11
  28.6 0.6 %collective-permute-start.9 = (s16[160,128]{1,0:T(8,128)(2,1)S(1)}, s16[160,128]{1,0:T(8,128)(2,1)S(1)}, u32[]{:S(2)}, u32[]{:S(2)}) collective-permute-start(s16[160,128]{1,0:T(8,128)(2,1)S(1)} %get-tuple-element.40), channel_id=1, source_target_pairs={{0,1},{1,0},{2,3},{3,2},{4,5},{5,4},{6,7},{7,6},{8,9},{9,8},{10,11... | collective-permute-start | bytes 122888 | tf_op jit(solution)/shard_map/ppermute | solution.py:647
  29.3 1.9 %collective-permute-done.10.in2 = s16[160,128]{1,0:T(8,128)(2,1)S(1)} collective-permute-done((s16[160,128]{1,0:T(8,128)(2,1)S(1)}, s16[160,128]{1,0:T(8,128)(2,1)S(1)}, u32[]{:S(2)}, u32[]{:S(2)}) %collective-permute-start.10) | collective-permute-done | bytes 40992 | tf_op jit(solution)/shard_map/ppermute | solution.py:647
  31.1 1.1 %collective-permute-done.11.in3 = s16[160,128]{1,0:T(8,128)(2,1)S(1)} collective-permute-done((s16[160,128]{1,0:T(8,128)(2,1)S(1)}, s16[160,128]{1,0:T(8,128)(2,1)S(1)}, u32[]{:S(2)}, u32[]{:S(2)}) %collective-permute-start.11) | collective-permute-done | bytes 40992 | tf_op jit(solution)/shard_map/ppermute | solution.py:647
  32.2 0.0 collective-permute-done.9.in1
  32.2 0.4 shard_map.70
  32.6 1.6 %collective-permute-start.12 = (s16[160,128]{1,0:T(8,128)(2,1)S(1)}, s16[160,128]{1,0:T(8,128)(2,1)S(1)}, u32[]{:S(2)}, u32[]{:S(2)}) collective-permute-start(s16[160,128]{1,0:T(8,128)(2,1)S(1)} %get-tuple-element.43), channel_id=1, source_target_pairs={{0,16},{4,20},{8,24},{12,28},{16,0},{20,4},{24,8},{28,12},{1,17},{... | collective-permute-start | bytes 122888 | tf_op jit(solution)/shard_map/ppermute | solution.py:705
  34.2 0.6 %collective-permute-start.13 = (s16[160,128]{1,0:T(8,128)(2,1)S(1)}, s16[160,128]{1,0:T(8,128)(2,1)S(1)}, u32[]{:S(2)}, u32[]{:S(2)}) collective-permute-start(s16[160,128]{1,0:T(8,128)(2,1)S(1)} %get-tuple-element.44), channel_id=1, source_target_pairs={{0,20},{4,24},{8,28},{12,16},{16,4},{20,8},{24,12},{28,0},{1,21},{... | collective-permute-start | bytes 122888 | tf_op jit(solution)/shard_map/ppermute | solution.py:705
  34.8 3.7 %collective-permute-start.14 = (s16[160,128]{1,0:T(8,128)(2,1)S(1)}, s16[160,128]{1,0:T(8,128)(2,1)S(1)}, u32[]{:S(2)}, u32[]{:S(2)}) collective-permute-start(s16[160,128]{1,0:T(8,128)(2,1)S(1)} %get-tuple-element.45), channel_id=1, source_target_pairs={{0,24},{4,28},{8,16},{12,20},{16,8},{20,12},{24,0},{28,4},{1,25},{... | collective-permute-start | bytes 122888 | tf_op jit(solution)/shard_map/ppermute | solution.py:705
  38.5 0.4 collective-permute-start.15
  38.9 0.0 collective-permute-done.12.in0
  38.9 2.1 %collective-permute-done.13.in1 = s16[160,128]{1,0:T(8,128)(2,1)S(1)} collective-permute-done((s16[160,128]{1,0:T(8,128)(2,1)S(1)}, s16[160,128]{1,0:T(8,128)(2,1)S(1)}, u32[]{:S(2)}, u32[]{:S(2)}) %collective-permute-start.13) | collective-permute-done | bytes 40992 | tf_op jit(solution)/shard_map/ppermute | solution.py:705
  41.0 0.2 collective-permute-done.14.in2
  41.2 2.2 %collective-permute-done.15.in3 = s16[160,128]{1,0:T(8,128)(2,1)S(1)} collective-permute-done((s16[160,128]{1,0:T(8,128)(2,1)S(1)}, s16[160,128]{1,0:T(8,128)(2,1)S(1)}, u32[]{:S(2)}, u32[]{:S(2)}) %collective-permute-start.15) | collective-permute-done | bytes 40992 | tf_op jit(solution)/shard_map/ppermute | solution.py:705
  43.4 0.0 copy-done
  43.4 0.0 copy-done.1
  43.4 0.0 copy-done.2
  43.4 0.9 %shard_map.71 = f32[1,2,19,4,512]{4,3,2,1,0:T(4,128)} custom-call(s16[160,128]{1,0:T(8,128)(2,1)S(1)} %collective-permute-done.12.in0, s16[160,128]{1,0:T(8,128)(2,1)S(1)} %collective-permute-done.13.in1, s16[160,128]{1,0:T(8,128)(2,1)S(1)} %collective-permute-done.14.in2, s16[160,128]{1,0:T(8,128)(2,1)S(1)} %collective-permute-done.15.in3, ...), custom_call_target="tpu_custom_call" | custom-call | tf_op jit(solution)/shard_map/pallas_call | solution.py:635
  (1 shorter events, 0.0 us)
Async XLA Ops:
  0.0 19.1 %copy-start.3 = (bf16[2,76,76]{2,0,1:T(2,128)(2,1)S(1)}, bf16[2,76,76]{2,0,1:T(2,128)(2,1)}, u32[]{:S(2)}) copy-start(bf16[2,76,76]{2,0,1:T(2,128)(2,1)} %param.11) | copy-start | bytes 69316
  1.7 8.5 %collective-permute-start = (s16[720,128]{1,0:T(8,128)(2,1)S(1)}, s16[720,128]{1,0:T(8,128)(2,1)S(1)}, u32[]{:S(2)}, u32[]{:S(2)}) collective-permute-start(s16[720,128]{1,0:T(8,128)(2,1)S(1)} %get-tuple-element.26), channel_id=1, source_target_pairs={{0,2},{1,3},{2,0},{3,1},{4,6},{5,7},{6,4},{7,5},{8,10},{9,11},{10,... | collective-permute-start | bytes 552968 | tf_op jit(solution)/shard_map/ppermute | solution.py:677
  4.7 9.4 %collective-permute-start.5 = (s16[240,128]{1,0:T(8,128)(2,1)S(1)}, s16[240,128]{1,0:T(8,128)(2,1)S(1)}, u32[]{:S(2)}, u32[]{:S(2)}) collective-permute-start(s16[240,128]{1,0:T(8,128)(2,1)S(1)} %get-tuple-element.32), channel_id=1, source_target_pairs={{0,4},{4,8},{8,12},{12,0},{1,5},{5,9},{9,13},{13,1},{2,6},{6,10},{... | collective-permute-start | bytes 184328 | tf_op jit(solution)/shard_map/ppermute | solution.py:654
  6.3 9.2 %collective-permute-start.6 = (s16[240,128]{1,0:T(8,128)(2,1)S(1)}, s16[240,128]{1,0:T(8,128)(2,1)S(1)}, u32[]{:S(2)}, u32[]{:S(2)}) collective-permute-start(s16[240,128]{1,0:T(8,128)(2,1)S(1)} %get-tuple-element.33), channel_id=1, source_target_pairs={{0,8},{4,12},{8,0},{12,4},{1,9},{5,13},{9,1},{13,5},{2,10},{6,14},... | collective-permute-start | bytes 184328 | tf_op jit(solution)/shard_map/ppermute | solution.py:654
  8.9 6.6 %collective-permute-start.7 = (s16[240,128]{1,0:T(8,128)(2,1)S(1)}, s16[240,128]{1,0:T(8,128)(2,1)S(1)}, u32[]{:S(2)}, u32[]{:S(2)}) collective-permute-start(s16[240,128]{1,0:T(8,128)(2,1)S(1)} %get-tuple-element.34), channel_id=1, source_target_pairs={{0,12},{4,0},{8,4},{12,8},{1,13},{5,1},{9,5},{13,9},{2,14},{6,2},{... | collective-permute-start | bytes 184328 | tf_op jit(solution)/shard_map/ppermute | solution.py:654
  10.5 6.3 %collective-permute-start.1 = (s16[240,128]{1,0:T(8,128)(2,1)S(1)}, s16[240,128]{1,0:T(8,128)(2,1)S(1)}, u32[]{:S(2)}, u32[]{:S(2)}) collective-permute-start(s16[240,128]{1,0:T(8,128)(2,1)S(1)} %get-tuple-element.28), channel_id=1, source_target_pairs={{0,4},{4,8},{8,12},{12,0},{1,5},{5,9},{9,13},{13,1},{2,6},{6,10},{... | collective-permute-start | bytes 184328 | tf_op jit(solution)/shard_map/ppermute | solution.py:654
  11.5 7.2 %collective-permute-start.2 = (s16[240,128]{1,0:T(8,128)(2,1)S(1)}, s16[240,128]{1,0:T(8,128)(2,1)S(1)}, u32[]{:S(2)}, u32[]{:S(2)}) collective-permute-start(s16[240,128]{1,0:T(8,128)(2,1)S(1)} %get-tuple-element.29), channel_id=1, source_target_pairs={{0,8},{4,12},{8,0},{12,4},{1,9},{5,13},{9,1},{13,5},{2,10},{6,14},... | collective-permute-start | bytes 184328 | tf_op jit(solution)/shard_map/ppermute | solution.py:654
  14.1 4.7 %collective-permute-start.3 = (s16[240,128]{1,0:T(8,128)(2,1)S(1)}, s16[240,128]{1,0:T(8,128)(2,1)S(1)}, u32[]{:S(2)}, u32[]{:S(2)}) collective-permute-start(s16[240,128]{1,0:T(8,128)(2,1)S(1)} %get-tuple-element.30), channel_id=1, source_target_pairs={{0,12},{4,0},{8,4},{12,8},{1,13},{5,1},{9,5},{13,9},{2,14},{6,2},{... | collective-permute-start | bytes 184328 | tf_op jit(solution)/shard_map/ppermute | solution.py:654
  15.7 3.5 %collective-permute-start.8 = (s16[640,128]{1,0:T(8,128)(2,1)S(1)}, s16[640,128]{1,0:T(8,128)(2,1)S(1)}, u32[]{:S(2)}, u32[]{:S(2)}) collective-permute-start(s16[640,128]{1,0:T(8,128)(2,1)S(1)} %shard_map.67), channel_id=1, source_target_pairs={{0,1},{1,0},{2,3},{3,2},{4,5},{5,4},{6,7},{7,6},{8,9},{9,8},{10,11... | collective-permute-start | bytes 491528 | tf_op jit(solution)/shard_map/ppermute | solution.py:682
  19.0 24.4 %copy-start = (f32[1,2,19,4,512]{4,3,2,1,0:T(4,128)S(1)}, f32[1,2,19,4,512]{4,3,2,1,0:T(4,128)}, u32[]{:S(2)}) copy-start(f32[1,2,19,4,512]{4,3,2,1,0:T(4,128)} %state.3) | copy-start | bytes 933892
  19.0 24.4 %copy-start.1 = (s32[4,512]{1,0:T(4,128)S(1)}, s32[4,512]{1,0:T(4,128)}, u32[]{:S(2)}) copy-start(s32[4,512]{1,0:T(4,128)} %land_sea.3) | copy-start | bytes 24580
  19.1 24.4 %copy-start.2 = (s32[4,512]{1,0:T(4,128)S(1)}, s32[4,512]{1,0:T(4,128)}, u32[]{:S(2)}) copy-start(s32[4,512]{1,0:T(4,128)} %depth_index.3) | copy-start | bytes 24580
  19.1 1.5 %collective-permute-start.4 = (s16[640,128]{1,0:T(8,128)(2,1)S(1)}, s16[640,128]{1,0:T(8,128)(2,1)S(1)}, u32[]{:S(2)}, u32[]{:S(2)}) collective-permute-start(s16[640,128]{1,0:T(8,128)(2,1)S(1)} %shard_map.66), channel_id=1, source_target_pairs={{0,1},{1,0},{2,3},{3,2},{4,5},{5,4},{6,7},{7,6},{8,9},{9,8},{10,11... | collective-permute-start | bytes 491528 | tf_op jit(solution)/shard_map/ppermute | solution.py:682
  27.1 4.1 %collective-permute-start.10 = (s16[160,128]{1,0:T(8,128)(2,1)S(1)}, s16[160,128]{1,0:T(8,128)(2,1)S(1)}, u32[]{:S(2)}, u32[]{:S(2)}) collective-permute-start(s16[160,128]{1,0:T(8,128)(2,1)S(1)} %get-tuple-element.41), channel_id=1, source_target_pairs={{0,2},{1,3},{2,0},{3,1},{4,6},{5,7},{6,4},{7,5},{8,10},{9,11},{10,... | collective-permute-start | bytes 122888 | tf_op jit(solution)/shard_map/ppermute | solution.py:647
  28.4 3.8 %collective-permute-start.11 = (s16[160,128]{1,0:T(8,128)(2,1)S(1)}, s16[160,128]{1,0:T(8,128)(2,1)S(1)}, u32[]{:S(2)}, u32[]{:S(2)}) collective-permute-start(s16[160,128]{1,0:T(8,128)(2,1)S(1)} %get-tuple-element.42), channel_id=1, source_target_pairs={{0,3},{1,2},{2,1},{3,0},{4,7},{5,6},{6,5},{7,4},{8,11},{9,10},{10,... | collective-permute-start | bytes 122888 | tf_op jit(solution)/shard_map/ppermute | solution.py:647
  28.6 3.6 %collective-permute-start.9 = (s16[160,128]{1,0:T(8,128)(2,1)S(1)}, s16[160,128]{1,0:T(8,128)(2,1)S(1)}, u32[]{:S(2)}, u32[]{:S(2)}) collective-permute-start(s16[160,128]{1,0:T(8,128)(2,1)S(1)} %get-tuple-element.40), channel_id=1, source_target_pairs={{0,1},{1,0},{2,3},{3,2},{4,5},{5,4},{6,7},{7,6},{8,9},{9,8},{10,11... | collective-permute-start | bytes 122888 | tf_op jit(solution)/shard_map/ppermute | solution.py:647
  32.6 6.3 %collective-permute-start.12 = (s16[160,128]{1,0:T(8,128)(2,1)S(1)}, s16[160,128]{1,0:T(8,128)(2,1)S(1)}, u32[]{:S(2)}, u32[]{:S(2)}) collective-permute-start(s16[160,128]{1,0:T(8,128)(2,1)S(1)} %get-tuple-element.43), channel_id=1, source_target_pairs={{0,16},{4,20},{8,24},{12,28},{16,0},{20,4},{24,8},{28,12},{1,17},{... | collective-permute-start | bytes 122888 | tf_op jit(solution)/shard_map/ppermute | solution.py:705
  34.2 6.8 %collective-permute-start.13 = (s16[160,128]{1,0:T(8,128)(2,1)S(1)}, s16[160,128]{1,0:T(8,128)(2,1)S(1)}, u32[]{:S(2)}, u32[]{:S(2)}) collective-permute-start(s16[160,128]{1,0:T(8,128)(2,1)S(1)} %get-tuple-element.44), channel_id=1, source_target_pairs={{0,20},{4,24},{8,28},{12,16},{16,4},{20,8},{24,12},{28,0},{1,21},{... | collective-permute-start | bytes 122888 | tf_op jit(solution)/shard_map/ppermute | solution.py:705
  34.8 6.5 %collective-permute-start.14 = (s16[160,128]{1,0:T(8,128)(2,1)S(1)}, s16[160,128]{1,0:T(8,128)(2,1)S(1)}, u32[]{:S(2)}, u32[]{:S(2)}) collective-permute-start(s16[160,128]{1,0:T(8,128)(2,1)S(1)} %get-tuple-element.45), channel_id=1, source_target_pairs={{0,24},{4,28},{8,16},{12,20},{16,8},{20,12},{24,0},{28,4},{1,25},{... | collective-permute-start | bytes 122888 | tf_op jit(solution)/shard_map/ppermute | solution.py:705
  38.5 4.9 %collective-permute-start.15 = (s16[160,128]{1,0:T(8,128)(2,1)S(1)}, s16[160,128]{1,0:T(8,128)(2,1)S(1)}, u32[]{:S(2)}, u32[]{:S(2)}) collective-permute-start(s16[160,128]{1,0:T(8,128)(2,1)S(1)} %get-tuple-element.46), channel_id=1, source_target_pairs={{0,28},{4,16},{8,20},{12,24},{16,12},{20,0},{24,4},{28,8},{1,29},{... | collective-permute-start | bytes 122888 | tf_op jit(solution)/shard_map/ppermute | solution.py:705

commit v10 on v9

--- a/solution.py
+++ b/solution.py
@@ -601,7 +601,7 @@
         out[...] = sent[(tile + n) % TILES]
 
 
-def finish_kernel(in0, in1, in2, in3, state, land_sea, depth_index, out, got):
+def finish_kernel(in0, in1, in2, in3, state, land_sea, depth_index, far, got, out, sent):
     block = lax.axis_index("depth")
     tile = lax.axis_index("tile")
     for n, ref in enumerate((in0, in1, in2, in3)):
@@ -609,6 +609,7 @@
     wet_levels = jnp.where(land_sea[...] == 1, depth_index[...], 0)
     first = block * OWN_LEVELS
     left = index((16, 128), 1) < 64
+    windows_of = []
     for q in range(4):
         half, west = divmod(q, 2)
         lanes = slice(128 * q, 128 * q + 128)
@@ -617,14 +618,23 @@
             x, y = (wide(got[2 * west + i, 16 * pair : 16 * pair + 16, :]) for i in range(2))
             x = jnp.where(left, turn(x, 2 * half), turn(y, 2 - 2 * half))
             values += [x[0:4], x[4:8], x[8:12], x[12:16]]
-        for t in range(2):
-            base = t * (OWN_LEVELS + 1)
+        windows_of.append(values)
+    copies = [
+        pltpu.make_async_copy(out.at[0, t], far.at[0, t], sent.at[t]) for t in range(2)
+    ]
+    for t in range(2):
+        base = t * (OWN_LEVELS + 1)
+        for q, values in enumerate(windows_of):
+            lanes = slice(128 * q, 128 * q + 128)
             unit = jnp.exp2(values[base + OWN_LEVELS]) * (1.0 / CODE)
             for k in range(OWN_LEVELS):
                 wet = wet_levels[:, lanes] > first + k
                 out[0, t, k, :, lanes] = jnp.where(
                     wet, values[base + k] * unit - state[0, t, k, :, lanes], 0.0
                 )
+        copies[t].start()
+    for copy in copies:
+        copy.wait()
 
 
 def near(*arrays):
@@ -713,15 +723,19 @@
         )
         for n in range(4)
     ]
-    return call(
+    arguments = near(*last, initial_states, land_sea, depth_index)
+    return pl.pallas_call(
         finish_kernel,
-        jax.ShapeDtypeStruct(initial_states.shape, F32),
-        [slots],
-        *last,
-        initial_states,
-        land_sea,
-        depth_index,
-    )
+        out_shape=jax.ShapeDtypeStruct(initial_states.shape, F32),
+        in_specs=[VMEM] * len(arguments),
+        out_specs=pl.BlockSpec(memory_space=pl.ANY),
+        scratch_shapes=[
+            slots,
+            pltpu.VMEM(initial_states.shape, F32),
+            pltpu.SemaphoreType.DMA((2,)),
+        ],
+        compiler_params=pltpu.CompilerParams(vmem_limit_bytes=8 << 20),
+    )(*arguments)
 
 
 def shards(initial_states, velocity, growth, land_sea, depth_index, column_ops):

time: 44.5 us -> 44.5 us (level)
    pallas_call x8 -> x7, Pallas kernels: 11.2 us -> 10.2 us  [call(): pl.pallas_call(kernel, out_shape=outs, in_specs=[VMEM] * len(args), out_s...]
    pallas_call x0 -> x1, Pallas kernels: none -> 0.93 us  [window_shards(): pl.pallas_call(finish_kernel, out_shape=jax.ShapeDtypeStruct(initial_stat...]
where the time goes in v10:
time: 44.5 us; the launch traced here: 44.4 us
  starting transfers between devices  22.1 us (50%)
  Pallas kernels  11.1 us (25%)
  waiting for transfers between devices  11 us (25%)
    ppermute x6, starting transfers between devices, across_tiles(): lax.ppermute(messages[n], 'tile', [(i, (i + n) % TILES) for i in range(TI...  10.4 us
    pallas_call x7, Pallas kernels, call(): pl.pallas_call(kernel, out_shape=outs, in_specs=[VMEM] * len(args), out_s...  10.2 us
    ppermute x4, starting transfers between devices, window_shards(): lax.ppermute(turned[n], ('seg', 'tile'), [(s * TILES + t, (s + 1) % segs...  6.31 us
    ppermute x4, waiting for transfers between devices, window_shards(): lax.ppermute(turned[n], ('seg', 'tile'), [(s * TILES + t, (s + 1) % segs...  4.5 us
    ppermute x6, waiting for transfers between devices, across_tiles(): lax.ppermute(messages[n], 'tile', [(i, (i + n) % TILES) for i in range(TI...  3.09 us
    ppermute x1, starting transfers between devices, window_shards(): lax.ppermute(across, 'depth', [(i, i ^ CORES) for i in range(BLOCKS)])  3 us
    ppermute x3, waiting for transfers between devices, across_depth(): lax.ppermute(messages[n], 'depth', [(i, i ^ n) for i in range(BLOCKS)])  2.95 us
    ppermute x3, starting transfers between devices, across_depth(): lax.ppermute(messages[n], 'depth', [(i, i ^ n) for i in range(BLOCKS)])  2.21 us
  transfers between devices with their start and end apart: 16, of which 9 were waited for; matrix products, arithmetic and copies ran while one was open for 0% of the time, Pallas kernels for 4%

profile of v10, /device:TPU:0, one launch (start us, length us, event | category | flops | bytes accessed | tf_op | source)
XLA Modules:
  0.0 44.4 jit_solution(16630194590616950410)
XLA Ops:
  0.0 0.0 copy-start.3
  0.0 1.7 %shard_map.64 = (s16[720,128]{1,0:T(8,128)(2,1)S(1)}, s16[240,128]{1,0:T(8,128)(2,1)S(1)}, s16[240,128]{1,0:T(8,128)(2,1)S(1)}, s16[240,128]{1,0:T(8,128)(2,1)S(1)}, s16[240,128]{1,0:T(8,128)(2,1)S(1)}) custom-call(f32[1,2,19,4,512]{4,3,2,1,0:T(4,128)} %state.3, f32[1,2,19,4,512]{4,3,2,1,0:T(4,128)} %velocity.1, f32[1,4,512]{2,1,0:T(4,128)} %growth.1, ...), custom_call_target="tpu_custom_call" | custom-call | tf_op jit(solution)/shard_map/pallas_call | solution.py:645
  1.7 3.0 %collective-permute-start = (s16[720,128]{1,0:T(8,128)(2,1)S(1)}, s16[720,128]{1,0:T(8,128)(2,1)S(1)}, u32[]{:S(2)}, u32[]{:S(2)}) collective-permute-start(s16[720,128]{1,0:T(8,128)(2,1)S(1)} %get-tuple-element.26), channel_id=1, source_target_pairs={{0,2},{1,3},{2,0},{3,1},{4,6},{5,7},{6,4},{7,5},{8,10},{9,11},{10,... | collective-permute-start | bytes 552968 | tf_op jit(solution)/shard_map/ppermute | solution.py:687
  4.7 1.6 %collective-permute-start.5 = (s16[240,128]{1,0:T(8,128)(2,1)S(1)}, s16[240,128]{1,0:T(8,128)(2,1)S(1)}, u32[]{:S(2)}, u32[]{:S(2)}) collective-permute-start(s16[240,128]{1,0:T(8,128)(2,1)S(1)} %get-tuple-element.32), channel_id=1, source_target_pairs={{0,4},{4,8},{8,12},{12,0},{1,5},{5,9},{9,13},{13,1},{2,6},{6,10},{... | collective-permute-start | bytes 184328 | tf_op jit(solution)/shard_map/ppermute | solution.py:664
  6.3 2.6 %collective-permute-start.6 = (s16[240,128]{1,0:T(8,128)(2,1)S(1)}, s16[240,128]{1,0:T(8,128)(2,1)S(1)}, u32[]{:S(2)}, u32[]{:S(2)}) collective-permute-start(s16[240,128]{1,0:T(8,128)(2,1)S(1)} %get-tuple-element.33), channel_id=1, source_target_pairs={{0,8},{4,12},{8,0},{12,4},{1,9},{5,13},{9,1},{13,5},{2,10},{6,14},... | collective-permute-start | bytes 184328 | tf_op jit(solution)/shard_map/ppermute | solution.py:664
  8.9 1.3 %collective-permute-start.7 = (s16[240,128]{1,0:T(8,128)(2,1)S(1)}, s16[240,128]{1,0:T(8,128)(2,1)S(1)}, u32[]{:S(2)}, u32[]{:S(2)}) collective-permute-start(s16[240,128]{1,0:T(8,128)(2,1)S(1)} %get-tuple-element.34), channel_id=1, source_target_pairs={{0,12},{4,0},{8,4},{12,8},{1,13},{5,1},{9,5},{13,9},{2,14},{6,2},{... | collective-permute-start | bytes 184328 | tf_op jit(solution)/shard_map/ppermute | solution.py:664
  10.2 0.0 collective-permute-done.ref
  10.2 0.3 shard_map.65
  10.5 1.0 %collective-permute-start.1 = (s16[240,128]{1,0:T(8,128)(2,1)S(1)}, s16[240,128]{1,0:T(8,128)(2,1)S(1)}, u32[]{:S(2)}, u32[]{:S(2)}) collective-permute-start(s16[240,128]{1,0:T(8,128)(2,1)S(1)} %get-tuple-element.28), channel_id=1, source_target_pairs={{0,4},{4,8},{8,12},{12,0},{1,5},{5,9},{9,13},{13,1},{2,6},{6,10},{... | collective-permute-start | bytes 184328 | tf_op jit(solution)/shard_map/ppermute | solution.py:664
  11.5 2.6 %collective-permute-start.2 = (s16[240,128]{1,0:T(8,128)(2,1)S(1)}, s16[240,128]{1,0:T(8,128)(2,1)S(1)}, u32[]{:S(2)}, u32[]{:S(2)}) collective-permute-start(s16[240,128]{1,0:T(8,128)(2,1)S(1)} %get-tuple-element.29), channel_id=1, source_target_pairs={{0,8},{4,12},{8,0},{12,4},{1,9},{5,13},{9,1},{13,5},{2,10},{6,14},... | collective-permute-start | bytes 184328 | tf_op jit(solution)/shard_map/ppermute | solution.py:664
  14.1 0.0 collective-permute-done.5.refs_1_
  14.1 1.3 %collective-permute-start.3 = (s16[240,128]{1,0:T(8,128)(2,1)S(1)}, s16[240,128]{1,0:T(8,128)(2,1)S(1)}, u32[]{:S(2)}, u32[]{:S(2)}) collective-permute-start(s16[240,128]{1,0:T(8,128)(2,1)S(1)} %get-tuple-element.30), channel_id=1, source_target_pairs={{0,12},{4,0},{8,4},{12,8},{1,13},{5,1},{9,5},{13,9},{2,14},{6,2},{... | collective-permute-start | bytes 184328 | tf_op jit(solution)/shard_map/ppermute | solution.py:664
  15.5 0.0 collective-permute-done.6.refs_2_
  15.5 0.0 collective-permute-done.7.refs_3_
  15.5 0.2 shard_map.67
  15.7 0.1 collective-permute-start.8
  15.7 1.1 %collective-permute-done.1.refs_1_ = s16[240,128]{1,0:T(8,128)(2,1)S(1)} collective-permute-done((s16[240,128]{1,0:T(8,128)(2,1)S(1)}, s16[240,128]{1,0:T(8,128)(2,1)S(1)}, u32[]{:S(2)}, u32[]{:S(2)}) %collective-permute-start.1) | collective-permute-done | bytes 61472 | tf_op jit(solution)/shard_map/ppermute | solution.py:664
  16.8 1.9 %collective-permute-done.2.refs_2_ = s16[240,128]{1,0:T(8,128)(2,1)S(1)} collective-permute-done((s16[240,128]{1,0:T(8,128)(2,1)S(1)}, s16[240,128]{1,0:T(8,128)(2,1)S(1)}, u32[]{:S(2)}, u32[]{:S(2)}) %collective-permute-start.2) | collective-permute-done | bytes 61472 | tf_op jit(solution)/shard_map/ppermute | solution.py:664
  18.7 0.1 collective-permute-done.3.refs_3_
  18.8 0.2 shard_map.66
  19.0 0.0 copy-start
  19.0 0.0 copy-start.1
  19.1 0.0 copy-start.2
  19.1 0.1 collective-permute-start.4
  19.1 0.0 copy-done.3
  19.2 0.0 collective-permute-done.8.refs_4_
  19.2 0.9 %shard_map.68 = (f32[640,128]{1,0:T(8,128)S(1)}, f32[5,8,9,8,128]{4,3,2,1,0:T(8,128)S(1)}, f32[2,8,128]{2,1,0:T(8,128)S(1)}, bf16[2,80,80]{2,1,0:T(8,128)(2,1)S(1)}) custom-call(s16[240,128]{1,0:T(8,128)(2,1)S(1)} %get-tuple-element.31.refs_0_, s16[240,128]{1,0:T(8,128)(2,1)S(1)} %collective-permute-done.5.refs_1_, ...), custom_call_target="tpu_custom_call" | custom-call | tf_op jit(solution)/shard_map/pallas_call | solution.py:645
  20.1 0.4 collective-permute-done.4.refs_4_
  20.5 6.6 %shard_map.69 = (s16[160,128]{1,0:T(8,128)(2,1)S(1)}, s16[160,128]{1,0:T(8,128)(2,1)S(1)}, s16[160,128]{1,0:T(8,128)(2,1)S(1)}, s16[160,128]{1,0:T(8,128)(2,1)S(1)}) custom-call(s16[240,128]{1,0:T(8,128)(2,1)S(1)} %get-tuple-element.27.refs_0_, s16[240,128]{1,0:T(8,128)(2,1)S(1)} %collective-permute-done.1.refs_1_, ...), custom_call_target="tpu_custom_call" | custom-call | tf_op jit(solution)/shard_map/pallas_call | solution.py:645
  27.1 1.3 %collective-permute-start.10 = (s16[160,128]{1,0:T(8,128)(2,1)S(1)}, s16[160,128]{1,0:T(8,128)(2,1)S(1)}, u32[]{:S(2)}, u32[]{:S(2)}) collective-permute-start(s16[160,128]{1,0:T(8,128)(2,1)S(1)} %get-tuple-element.41), channel_id=1, source_target_pairs={{0,2},{1,3},{2,0},{3,1},{4,6},{5,7},{6,4},{7,5},{8,10},{9,11},{10,... | collective-permute-start | bytes 122888 | tf_op jit(solution)/shard_map/ppermute | solution.py:657
  28.4 0.2 collective-permute-start.11
  28.6 0.6 %collective-permute-start.9 = (s16[160,128]{1,0:T(8,128)(2,1)S(1)}, s16[160,128]{1,0:T(8,128)(2,1)S(1)}, u32[]{:S(2)}, u32[]{:S(2)}) collective-permute-start(s16[160,128]{1,0:T(8,128)(2,1)S(1)} %get-tuple-element.40), channel_id=1, source_target_pairs={{0,1},{1,0},{2,3},{3,2},{4,5},{5,4},{6,7},{7,6},{8,9},{9,8},{10,11... | collective-permute-start | bytes 122888 | tf_op jit(solution)/shard_map/ppermute | solution.py:657
  29.3 1.9 %collective-permute-done.10.in2 = s16[160,128]{1,0:T(8,128)(2,1)S(1)} collective-permute-done((s16[160,128]{1,0:T(8,128)(2,1)S(1)}, s16[160,128]{1,0:T(8,128)(2,1)S(1)}, u32[]{:S(2)}, u32[]{:S(2)}) %collective-permute-start.10) | collective-permute-done | bytes 40992 | tf_op jit(solution)/shard_map/ppermute | solution.py:657
  31.1 1.1 %collective-permute-done.11.in3 = s16[160,128]{1,0:T(8,128)(2,1)S(1)} collective-permute-done((s16[160,128]{1,0:T(8,128)(2,1)S(1)}, s16[160,128]{1,0:T(8,128)(2,1)S(1)}, u32[]{:S(2)}, u32[]{:S(2)}) %collective-permute-start.11) | collective-permute-done | bytes 40992 | tf_op jit(solution)/shard_map/ppermute | solution.py:657
  32.2 0.0 collective-permute-done.9.in1
  32.2 0.4 shard_map.70
  32.6 1.6 %collective-permute-start.12 = (s16[160,128]{1,0:T(8,128)(2,1)S(1)}, s16[160,128]{1,0:T(8,128)(2,1)S(1)}, u32[]{:S(2)}, u32[]{:S(2)}) collective-permute-start(s16[160,128]{1,0:T(8,128)(2,1)S(1)} %get-tuple-element.43), channel_id=1, source_target_pairs={{0,16},{4,20},{8,24},{12,28},{16,0},{20,4},{24,8},{28,12},{1,17},{... | collective-permute-start | bytes 122888 | tf_op jit(solution)/shard_map/ppermute | solution.py:715
  34.2 0.6 %collective-permute-start.13 = (s16[160,128]{1,0:T(8,128)(2,1)S(1)}, s16[160,128]{1,0:T(8,128)(2,1)S(1)}, u32[]{:S(2)}, u32[]{:S(2)}) collective-permute-start(s16[160,128]{1,0:T(8,128)(2,1)S(1)} %get-tuple-element.44), channel_id=1, source_target_pairs={{0,20},{4,24},{8,28},{12,16},{16,4},{20,8},{24,12},{28,0},{1,21},{... | collective-permute-start | bytes 122888 | tf_op jit(solution)/shard_map/ppermute | solution.py:715
  34.8 3.7 %collective-permute-start.14 = (s16[160,128]{1,0:T(8,128)(2,1)S(1)}, s16[160,128]{1,0:T(8,128)(2,1)S(1)}, u32[]{:S(2)}, u32[]{:S(2)}) collective-permute-start(s16[160,128]{1,0:T(8,128)(2,1)S(1)} %get-tuple-element.45), channel_id=1, source_target_pairs={{0,24},{4,28},{8,16},{12,20},{16,8},{20,12},{24,0},{28,4},{1,25},{... | collective-permute-start | bytes 122888 | tf_op jit(solution)/shard_map/ppermute | solution.py:715
  38.5 0.4 collective-permute-start.15
  38.9 0.0 collective-permute-done.12.in0
  38.9 2.1 %collective-permute-done.13.in1 = s16[160,128]{1,0:T(8,128)(2,1)S(1)} collective-permute-done((s16[160,128]{1,0:T(8,128)(2,1)S(1)}, s16[160,128]{1,0:T(8,128)(2,1)S(1)}, u32[]{:S(2)}, u32[]{:S(2)}) %collective-permute-start.13) | collective-permute-done | bytes 40992 | tf_op jit(solution)/shard_map/ppermute | solution.py:715
  41.0 0.2 collective-permute-done.14.in2
  41.2 2.2 %collective-permute-done.15.in3 = s16[160,128]{1,0:T(8,128)(2,1)S(1)} collective-permute-done((s16[160,128]{1,0:T(8,128)(2,1)S(1)}, s16[160,128]{1,0:T(8,128)(2,1)S(1)}, u32[]{:S(2)}, u32[]{:S(2)}) %collective-permute-start.15) | collective-permute-done | bytes 40992 | tf_op jit(solution)/shard_map/ppermute | solution.py:715
  43.4 0.0 copy-done
  43.4 0.0 copy-done.1
  43.4 0.0 copy-done.2
  43.4 0.9 %shard_map.71 = f32[1,2,19,4,512]{4,3,2,1,0:T(4,128)} custom-call(s16[160,128]{1,0:T(8,128)(2,1)S(1)} %collective-permute-done.12.in0, s16[160,128]{1,0:T(8,128)(2,1)S(1)} %collective-permute-done.13.in1, s16[160,128]{1,0:T(8,128)(2,1)S(1)} %collective-permute-done.14.in2, s16[160,128]{1,0:T(8,128)(2,1)S(1)} %collective-permute-done.15.in3, ...), custom_call_target="tpu_custom_call" | custom-call | tf_op jit(solution)/shard_map/pallas_call | solution.py:727
  (1 shorter events, 0.0 us)
Async XLA Ops:
  0.0 19.1 %copy-start.3 = (bf16[2,76,76]{2,0,1:T(2,128)(2,1)S(1)}, bf16[2,76,76]{2,0,1:T(2,128)(2,1)}, u32[]{:S(2)}) copy-start(bf16[2,76,76]{2,0,1:T(2,128)(2,1)} %param.11) | copy-start | bytes 69316
  1.7 8.5 %collective-permute-start = (s16[720,128]{1,0:T(8,128)(2,1)S(1)}, s16[720,128]{1,0:T(8,128)(2,1)S(1)}, u32[]{:S(2)}, u32[]{:S(2)}) collective-permute-start(s16[720,128]{1,0:T(8,128)(2,1)S(1)} %get-tuple-element.26), channel_id=1, source_target_pairs={{0,2},{1,3},{2,0},{3,1},{4,6},{5,7},{6,4},{7,5},{8,10},{9,11},{10,... | collective-permute-start | bytes 552968 | tf_op jit(solution)/shard_map/ppermute | solution.py:687
  4.7 9.4 %collective-permute-start.5 = (s16[240,128]{1,0:T(8,128)(2,1)S(1)}, s16[240,128]{1,0:T(8,128)(2,1)S(1)}, u32[]{:S(2)}, u32[]{:S(2)}) collective-permute-start(s16[240,128]{1,0:T(8,128)(2,1)S(1)} %get-tuple-element.32), channel_id=1, source_target_pairs={{0,4},{4,8},{8,12},{12,0},{1,5},{5,9},{9,13},{13,1},{2,6},{6,10},{... | collective-permute-start | bytes 184328 | tf_op jit(solution)/shard_map/ppermute | solution.py:664
  6.3 9.2 %collective-permute-start.6 = (s16[240,128]{1,0:T(8,128)(2,1)S(1)}, s16[240,128]{1,0:T(8,128)(2,1)S(1)}, u32[]{:S(2)}, u32[]{:S(2)}) collective-permute-start(s16[240,128]{1,0:T(8,128)(2,1)S(1)} %get-tuple-element.33), channel_id=1, source_target_pairs={{0,8},{4,12},{8,0},{12,4},{1,9},{5,13},{9,1},{13,5},{2,10},{6,14},... | collective-permute-start | bytes 184328 | tf_op jit(solution)/shard_map/ppermute | solution.py:664
  8.9 6.6 %collective-permute-start.7 = (s16[240,128]{1,0:T(8,128)(2,1)S(1)}, s16[240,128]{1,0:T(8,128)(2,1)S(1)}, u32[]{:S(2)}, u32[]{:S(2)}) collective-permute-start(s16[240,128]{1,0:T(8,128)(2,1)S(1)} %get-tuple-element.34), channel_id=1, source_target_pairs={{0,12},{4,0},{8,4},{12,8},{1,13},{5,1},{9,5},{13,9},{2,14},{6,2},{... | collective-permute-start | bytes 184328 | tf_op jit(solution)/shard_map/ppermute | solution.py:664
  10.5 6.3 %collective-permute-start.1 = (s16[240,128]{1,0:T(8,128)(2,1)S(1)}, s16[240,128]{1,0:T(8,128)(2,1)S(1)}, u32[]{:S(2)}, u32[]{:S(2)}) collective-permute-start(s16[240,128]{1,0:T(8,128)(2,1)S(1)} %get-tuple-element.28), channel_id=1, source_target_pairs={{0,4},{4,8},{8,12},{12,0},{1,5},{5,9},{9,13},{13,1},{2,6},{6,10},{... | collective-permute-start | bytes 184328 | tf_op jit(solution)/shard_map/ppermute | solution.py:664
  11.5 7.2 %collective-permute-start.2 = (s16[240,128]{1,0:T(8,128)(2,1)S(1)}, s16[240,128]{1,0:T(8,128)(2,1)S(1)}, u32[]{:S(2)}, u32[]{:S(2)}) collective-permute-start(s16[240,128]{1,0:T(8,128)(2,1)S(1)} %get-tuple-element.29), channel_id=1, source_target_pairs={{0,8},{4,12},{8,0},{12,4},{1,9},{5,13},{9,1},{13,5},{2,10},{6,14},... | collective-permute-start | bytes 184328 | tf_op jit(solution)/shard_map/ppermute | solution.py:664
  14.1 4.7 %collective-permute-start.3 = (s16[240,128]{1,0:T(8,128)(2,1)S(1)}, s16[240,128]{1,0:T(8,128)(2,1)S(1)}, u32[]{:S(2)}, u32[]{:S(2)}) collective-permute-start(s16[240,128]{1,0:T(8,128)(2,1)S(1)} %get-tuple-element.30), channel_id=1, source_target_pairs={{0,12},{4,0},{8,4},{12,8},{1,13},{5,1},{9,5},{13,9},{2,14},{6,2},{... | collective-permute-start | bytes 184328 | tf_op jit(solution)/shard_map/ppermute | solution.py:664
  15.7 3.5 %collective-permute-start.8 = (s16[640,128]{1,0:T(8,128)(2,1)S(1)}, s16[640,128]{1,0:T(8,128)(2,1)S(1)}, u32[]{:S(2)}, u32[]{:S(2)}) collective-permute-start(s16[640,128]{1,0:T(8,128)(2,1)S(1)} %shard_map.67), channel_id=1, source_target_pairs={{0,1},{1,0},{2,3},{3,2},{4,5},{5,4},{6,7},{7,6},{8,9},{9,8},{10,11... | collective-permute-start | bytes 491528 | tf_op jit(solution)/shard_map/ppermute | solution.py:692
  19.0 24.4 %copy-start = (f32[1,2,19,4,512]{4,3,2,1,0:T(4,128)S(1)}, f32[1,2,19,4,512]{4,3,2,1,0:T(4,128)}, u32[]{:S(2)}) copy-start(f32[1,2,19,4,512]{4,3,2,1,0:T(4,128)} %state.3) | copy-start | bytes 933892
  19.0 24.4 %copy-start.1 = (s32[4,512]{1,0:T(4,128)S(1)}, s32[4,512]{1,0:T(4,128)}, u32[]{:S(2)}) copy-start(s32[4,512]{1,0:T(4,128)} %land_sea.3) | copy-start | bytes 24580
  19.1 24.4 %copy-start.2 = (s32[4,512]{1,0:T(4,128)S(1)}, s32[4,512]{1,0:T(4,128)}, u32[]{:S(2)}) copy-start(s32[4,512]{1,0:T(4,128)} %depth_index.3) | copy-start | bytes 24580
  19.1 1.5 %collective-permute-start.4 = (s16[640,128]{1,0:T(8,128)(2,1)S(1)}, s16[640,128]{1,0:T(8,128)(2,1)S(1)}, u32[]{:S(2)}, u32[]{:S(2)}) collective-permute-start(s16[640,128]{1,0:T(8,128)(2,1)S(1)} %shard_map.66), channel_id=1, source_target_pairs={{0,1},{1,0},{2,3},{3,2},{4,5},{5,4},{6,7},{7,6},{8,9},{9,8},{10,11... | collective-permute-start | bytes 491528 | tf_op jit(solution)/shard_map/ppermute | solution.py:692
  27.1 4.1 %collective-permute-start.10 = (s16[160,128]{1,0:T(8,128)(2,1)S(1)}, s16[160,128]{1,0:T(8,128)(2,1)S(1)}, u32[]{:S(2)}, u32[]{:S(2)}) collective-permute-start(s16[160,128]{1,0:T(8,128)(2,1)S(1)} %get-tuple-element.41), channel_id=1, source_target_pairs={{0,2},{1,3},{2,0},{3,1},{4,6},{5,7},{6,4},{7,5},{8,10},{9,11},{10,... | collective-permute-start | bytes 122888 | tf_op jit(solution)/shard_map/ppermute | solution.py:657
  28.4 3.8 %collective-permute-start.11 = (s16[160,128]{1,0:T(8,128)(2,1)S(1)}, s16[160,128]{1,0:T(8,128)(2,1)S(1)}, u32[]{:S(2)}, u32[]{:S(2)}) collective-permute-start(s16[160,128]{1,0:T(8,128)(2,1)S(1)} %get-tuple-element.42), channel_id=1, source_target_pairs={{0,3},{1,2},{2,1},{3,0},{4,7},{5,6},{6,5},{7,4},{8,11},{9,10},{10,... | collective-permute-start | bytes 122888 | tf_op jit(solution)/shard_map/ppermute | solution.py:657
  28.6 3.6 %collective-permute-start.9 = (s16[160,128]{1,0:T(8,128)(2,1)S(1)}, s16[160,128]{1,0:T(8,128)(2,1)S(1)}, u32[]{:S(2)}, u32[]{:S(2)}) collective-permute-start(s16[160,128]{1,0:T(8,128)(2,1)S(1)} %get-tuple-element.40), channel_id=1, source_target_pairs={{0,1},{1,0},{2,3},{3,2},{4,5},{5,4},{6,7},{7,6},{8,9},{9,8},{10,11... | collective-permute-start | bytes 122888 | tf_op jit(solution)/shard_map/ppermute | solution.py:657
  32.6 6.3 %collective-permute-start.12 = (s16[160,128]{1,0:T(8,128)(2,1)S(1)}, s16[160,128]{1,0:T(8,128)(2,1)S(1)}, u32[]{:S(2)}, u32[]{:S(2)}) collective-permute-start(s16[160,128]{1,0:T(8,128)(2,1)S(1)} %get-tuple-element.43), channel_id=1, source_target_pairs={{0,16},{4,20},{8,24},{12,28},{16,0},{20,4},{24,8},{28,12},{1,17},{... | collective-permute-start | bytes 122888 | tf_op jit(solution)/shard_map/ppermute | solution.py:715
  34.2 6.8 %collective-permute-start.13 = (s16[160,128]{1,0:T(8,128)(2,1)S(1)}, s16[160,128]{1,0:T(8,128)(2,1)S(1)}, u32[]{:S(2)}, u32[]{:S(2)}) collective-permute-start(s16[160,128]{1,0:T(8,128)(2,1)S(1)} %get-tuple-element.44), channel_id=1, source_target_pairs={{0,20},{4,24},{8,28},{12,16},{16,4},{20,8},{24,12},{28,0},{1,21},{... | collective-permute-start | bytes 122888 | tf_op jit(solution)/shard_map/ppermute | solution.py:715
  34.8 6.5 %collective-permute-start.14 = (s16[160,128]{1,0:T(8,128)(2,1)S(1)}, s16[160,128]{1,0:T(8,128)(2,1)S(1)}, u32[]{:S(2)}, u32[]{:S(2)}) collective-permute-start(s16[160,128]{1,0:T(8,128)(2,1)S(1)} %get-tuple-element.45), channel_id=1, source_target_pairs={{0,24},{4,28},{8,16},{12,20},{16,8},{20,12},{24,0},{28,4},{1,25},{... | collective-permute-start | bytes 122888 | tf_op jit(solution)/shard_map/ppermute | solution.py:715
  38.5 4.9 %collective-permute-start.15 = (s16[160,128]{1,0:T(8,128)(2,1)S(1)}, s16[160,128]{1,0:T(8,128)(2,1)S(1)}, u32[]{:S(2)}, u32[]{:S(2)}) collective-permute-start(s16[160,128]{1,0:T(8,128)(2,1)S(1)} %get-tuple-element.46), channel_id=1, source_target_pairs={{0,28},{4,16},{8,20},{12,24},{16,12},{20,0},{24,4},{28,8},{1,29},{... | collective-permute-start | bytes 122888 | tf_op jit(solution)/shard_map/ppermute | solution.py:715
